TPU v7x, 128 devices: a whole 4x4x4 slice. The times are simulated.
128 devices in a mesh: rows: 8 (over y, core), cols: 16 (over x, z).
Axes of the slice: x: 4, y: 4, z: 4, core: 2. Of those that a mesh axis runs over, the one named last changes fastest.
Arguments:
- query_cells: bfloat16 [128, 1024, 1024], P('rows', 'cols'), may hold values from -6 to 6
- key_cells: bfloat16 [128, 1024, 1024], P('rows', 'cols'), may hold values from -6 to 6
- value_cells: bfloat16 [128, 1024, 1024], P('rows', 'cols'), may hold values from -6 to 6
- out_weight: bfloat16 [1024, 4096], P(None, ('rows', 'cols')), may hold values from -0.1875 to 0.1875
- row_pattern: int32 [128, 32, 6], P('rows'), may hold values from 0 to 31, as said below
- row_count: int32 [128], P('rows'), may hold values from 256 to 1024, as said below
- col_pattern: int32 [1024, 4, 2], P('cols'), may hold values from 0 to 3, as said below
- col_count: int32 [1024], P('cols'), may hold values from 32 to 128, as said below
Outputs:
- mixed: bfloat16 [128, 1024, 4096], P('rows', 'cols')
Inputs may be any that keep to these rules, and one draw needn't show every extreme that they name: `row_pattern`: for each table row and query block, entry 0 is the query block itself and the 6 entries are distinct block numbers. `col_pattern`: for each table column and query block, entry 0 is the query block itself and the 2 entries are distinct block numbers. Cells of table row i at column positions row_count[i] or more are padding. Cells of table column j at row positions col_count[j] or more are padding.
All inputs are finite; a program needn't handle non-finite values.
Results may differ from a plain program's by a relative error of at most 0.006.
Values may be sent and summed in bfloat16 or wider, within the bound.
No kernel may reach another device: no remote copies, remote signals or barrier semaphores. Data moves between devices by JAX's collectives and lax.ppermute only.
A program may use at most 192 MiB of HBM per device.

v0:
```python
import functools

import jax
import jax.numpy as jnp
from jax import lax
from jax.experimental import pallas as pl
from jax.experimental.pallas import tpu as pltpu
from jax.sharding import PartitionSpec as P


HR = 4
HC = 4
HD = 128
BLK = 32
NEG_FILL = -1e30


def row_pack_kernel(q_ref, k_ref, v_ref, out_ref):
    width = HR * HD
    out_ref[:, :, 0:width] = q_ref[...]
    out_ref[:, :, width : 2 * width] = k_ref[...]
    out_ref[:, :, 2 * width : 3 * width] = v_ref[...]


def row_pack(q, k, v):
    span, cells, _ = q.shape
    width = HR * HD
    step = 4
    part = pl.BlockSpec((step, cells, width), lambda i: (i, 0, 0))
    return pl.pallas_call(
        row_pack_kernel,
        grid=(span // step,),
        in_specs=[part, part, part],
        out_specs=pl.BlockSpec((step, cells, 3 * width), lambda i: (i, 0, 0)),
        out_shape=jax.ShapeDtypeStruct((span, cells, 3 * width), q.dtype),
        name="row_pack",
    )(q, k, v)


def swap_lead(x):
    return jnp.swapaxes(x.astype(jnp.float32), 0, 1).astype(jnp.bfloat16)


def col_pack_kernel(me_ref, q_ref, k_ref, v_ref, *rest):
    outs, (buf, sem) = rest[:-2], rest[-2:]
    peers = len(outs)
    width = HC * HD
    step = pl.program_id(0)
    slot = lax.rem(step, 2)

    @pl.when(step >= 2)
    def _():
        pltpu.make_async_copy(buf.at[slot], outs[0], sem.at[slot]).wait()

    for t, ref in enumerate((q_ref, k_ref, v_ref)):
        buf[slot, :, :, t * width : (t + 1) * width] = swap_lead(ref[...])
    for s in range(peers):

        @pl.when(step == s)
        def _(s=s):
            pltpu.make_async_copy(buf.at[slot], outs[s], sem.at[slot]).start()

    @pl.when(step == peers - 1)
    def _():
        pltpu.make_async_copy(buf.at[1 - slot], outs[0], sem.at[1 - slot]).wait()
        pltpu.make_async_copy(buf.at[slot], outs[0], sem.at[slot]).wait()


def col_pack(me, q, k, v, peers):
    span, cells, _ = q.shape
    width = HC * HD
    own = cells // peers
    part = pl.BlockSpec((span, own, width), lambda s, me: (0, me[0] ^ s, 1))
    piece = (own, span, 3 * width)
    return pl.pallas_call(
        col_pack_kernel,
        grid_spec=pltpu.PrefetchScalarGridSpec(
            num_scalar_prefetch=1,
            grid=(peers,),
            in_specs=[part, part, part],
            out_specs=[pl.BlockSpec(memory_space=pl.ANY)] * peers,
            scratch_shapes=[
                pltpu.VMEM((2,) + piece, q.dtype),
                pltpu.SemaphoreType.DMA((2,)),
            ],
        ),
        out_shape=[jax.ShapeDtypeStruct(piece, q.dtype)] * peers,
        name="col_pack",
    )(me, q, k, v)


def row_attend_kernel(pattern_ref, count_ref, x_ref, out_ref, *, chosen):
    width = HR * HD
    count = count_ref[0]
    blocks = x_ref.shape[0] // BLK
    key_lane = lax.broadcasted_iota(jnp.int32, (1, chosen * BLK), 1)
    slot_of = key_lane // BLK
    in_block = key_lane - slot_of * BLK
    query_row = lax.broadcasted_iota(jnp.int32, (BLK, 1), 0)
    zero = jnp.zeros((BLK, HD), jnp.bfloat16)

    def one(n):
        at = pl.multiple_of(n * BLK, BLK)
        q = x_ref[pl.ds(at, BLK), 0:width]
        keys, values = [], []
        limit = jnp.zeros((1, chosen * BLK), jnp.int32)
        for s in range(chosen):
            b = pattern_ref[n * chosen + s]
            k_at = pl.multiple_of(b * BLK, BLK)
            keys.append(x_ref[pl.ds(k_at, BLK), width : 2 * width])
            values.append(x_ref[pl.ds(k_at, BLK), 2 * width : 3 * width])
            limit = jnp.where(slot_of == s, count - b * BLK, limit)
        keys = jnp.concatenate(keys, axis=0)
        values = jnp.concatenate(values, axis=0)
        live = in_block < limit
        spread = jnp.concatenate(
            [
                jnp.concatenate(
                    [q[:, h * HD : (h + 1) * HD] if g == h else zero for g in range(HR)], axis=1
                )
                for h in range(HR)
            ],
            axis=0,
        )
        scores = lax.dot_general(
            spread, keys, (((1,), (1,)), ((), ())), preferred_element_type=jnp.float32
        ) * HD ** (-0.5)
        top = jnp.max(jnp.where(live, scores, NEG_FILL), axis=1, keepdims=True)
        weights = jnp.where(live, jnp.exp(scores - top), 0.0)
        total = jnp.sum(weights, axis=1, keepdims=True)
        weights = weights.astype(jnp.bfloat16)
        query_live = (query_row + n * BLK) < count
        for pair in range(HR // 2):
            rows = slice(pair * 2 * BLK, (pair + 1) * 2 * BLK)
            lanes = slice(pair * 2 * HD, (pair + 1) * 2 * HD)
            added = lax.dot_general(
                weights[rows],
                values[:, lanes],
                (((1,), (0,)), ((), ())),
                preferred_element_type=jnp.float32,
            )
            for g in range(2):
                h = pair * 2 + g
                part = added[g * BLK : (g + 1) * BLK, g * HD : (g + 1) * HD]
                safe = jnp.where(query_live, total[h * BLK : (h + 1) * BLK], 1.0)
                done = jnp.where(query_live, part / safe, 0.0)
                out_ref[pl.ds(at, BLK), h * HD : (h + 1) * HD] = done.astype(jnp.bfloat16)

    def group(g, _):
        for u in range(4):
            one(g * 4 + u)
        return 0

    lax.fori_loop(0, blocks // 4, group, 0)


def row_attend(pattern, count, x):
    cells = x.shape[0]
    chosen = pattern.shape[-1]
    return pl.pallas_call(
        functools.partial(row_attend_kernel, chosen=chosen),
        grid_spec=pltpu.PrefetchScalarGridSpec(
            num_scalar_prefetch=2,
            grid=(1,),
            in_specs=[pl.BlockSpec(x.shape, lambda i, *_: (0, 0), pipeline_mode=pl.Buffered(1))],
            out_specs=pl.BlockSpec((cells, HR * HD), lambda i, *_: (0, 0)),
        ),
        out_shape=jax.ShapeDtypeStruct((cells, HR * HD), x.dtype),
        name="row_attend",
    )(pattern.reshape(-1), count, x)


def col_attend_kernel(me_ref, pattern_ref, count_ref, *rest, chosen):
    peers = (len(rest) - 2) // 2
    pieces, outs, (line, held) = rest[:peers], rest[peers : 2 * peers], rest[2 * peers :]
    width = HC * HD
    me = me_ref[0]
    j = pl.program_id(0)
    span = pieces[0].shape[1]
    cells = peers * span
    own = held.shape[0]
    first = me * own + j
    count = count_ref[first]
    for s in range(peers):
        line[pl.ds(pl.multiple_of((me ^ s) * span, span), span), :] = pieces[s][0]
    key_at = lax.broadcasted_iota(jnp.int32, (1, cells), 1)
    key_block = key_at // BLK
    query_row = lax.broadcasted_iota(jnp.int32, (cells, 1), 0)
    query_live = query_row < count
    blocks = cells // BLK
    rows = []
    for n in range(blocks):
        listed = key_block == pattern_ref[(first * blocks + n) * chosen]
        for s in range(1, chosen):
            listed = listed | (key_block == pattern_ref[(first * blocks + n) * chosen + s])
        row = jnp.where(listed & (key_at < count), 1.0, 0.0)
        rows.append(jnp.broadcast_to(row, (BLK, cells)))
    live = jnp.concatenate(rows, axis=0) > 0.5
    for h in range(HC):
        q = line[:, h * HD : (h + 1) * HD]
        k = line[:, width + h * HD : width + (h + 1) * HD]
        v = line[:, 2 * width + h * HD : 2 * width + (h + 1) * HD]
        scores = lax.dot_general(
            q, k, (((1,), (1,)), ((), ())), preferred_element_type=jnp.float32
        ) * HD ** (-0.5)
        top = jnp.max(jnp.where(live, scores, NEG_FILL), axis=1, keepdims=True)
        weights = jnp.where(live, jnp.exp(scores - top), 0.0)
        total = jnp.sum(weights, axis=1, keepdims=True)
        added = lax.dot_general(
            weights.astype(jnp.bfloat16),
            v,
            (((1,), (0,)), ((), ())),
            preferred_element_type=jnp.float32,
        )
        safe = jnp.where(query_live, total, 1.0)
        held[j, :, h * HD : (h + 1) * HD] = jnp.where(query_live, added / safe, 0.0)

    @pl.when(j == own - 1)
    def _():
        for s in range(peers):
            at = pl.multiple_of((me ^ s) * span, span)
            part = held[:, pl.ds(at, span), :]
            outs[s][...] = jnp.swapaxes(part, 0, 1).astype(jnp.bfloat16)


def col_attend(me, pattern, count, pieces):
    peers = len(pieces)
    own, span, wide = pieces[0].shape
    width = HC * HD
    chosen = pattern.shape[-1]
    result = (span, own, width)
    return pl.pallas_call(
        functools.partial(col_attend_kernel, chosen=chosen),
        grid_spec=pltpu.PrefetchScalarGridSpec(
            num_scalar_prefetch=3,
            grid=(own,),
            in_specs=[pl.BlockSpec((1, span, wide), lambda j, *_: (j, 0, 0))] * peers,
            out_specs=[pl.BlockSpec(result, lambda j, *_: (0, 0, 0))] * peers,
            scratch_shapes=[
                pltpu.VMEM((peers * span, wide), jnp.bfloat16),
                pltpu.VMEM((own, peers * span, width), jnp.float32),
            ],
        ),
        out_shape=[jax.ShapeDtypeStruct(result, jnp.bfloat16)] * peers,
        name="col_attend",
    )(me, pattern.reshape(-1), count, *pieces)


def project_kernel(me_ref, row_ref, *rest):
    pieces, (w_ref, out_ref, heads) = rest[:-3], rest[-3:]
    width = HR * HD
    _, own, _ = pieces[0].shape

    @pl.when(pl.program_id(0) == 0)
    def _():
        me = me_ref[0]
        odd = lax.rem(me, 2) == 1
        heads[:, :, 0:width] = row_ref[...]
        for s in range(0, len(pieces), 2):
            a = pieces[s][...].astype(jnp.float32)
            b = pieces[s + 1][...].astype(jnp.float32)
            both = jnp.concatenate([jnp.where(odd, b, a), jnp.where(odd, a, b)], axis=1)
            at = pl.multiple_of(((me ^ s) // 2) * 2 * own, 2 * own)
            heads[:, pl.ds(at, 2 * own), width:] = both.astype(jnp.bfloat16)

    lhs = heads[...].reshape(heads.shape[0] * heads.shape[1], heads.shape[2])
    out_ref[...] = lax.dot_general(
        lhs, w_ref[...], (((1,), (1,)), ((), ())), preferred_element_type=jnp.float32
    ).astype(jnp.bfloat16)


def project(me, row_out, pieces, weight):
    span, cells, _ = row_out.shape
    outs, channels = weight.shape
    tile = 512
    whole = lambda a: pl.BlockSpec(a.shape, lambda j, *_: (0,) * a.ndim)
    return pl.pallas_call(
        project_kernel,
        grid_spec=pltpu.PrefetchScalarGridSpec(
            num_scalar_prefetch=1,
            grid=(outs // tile,),
            in_specs=[whole(row_out)]
            + [whole(p) for p in pieces]
            + [pl.BlockSpec((tile, channels), lambda j, *_: (j, 0))],
            out_specs=pl.BlockSpec((span * cells, tile), lambda j, *_: (0, j)),
            scratch_shapes=[pltpu.VMEM((span, cells, channels), jnp.bfloat16)],
        ),
        out_shape=jax.ShapeDtypeStruct((span * cells, outs), jnp.bfloat16),
        name="project",
    )(me, row_out, *pieces, weight)


def swap_pieces(pieces):
    peers = len(pieces)
    return [pieces[0]] + [
        lax.ppermute(pieces[s], "rows", [(d, d ^ s) for d in range(peers)])
        for s in range(1, peers)
    ]


def body(
    query_cells, key_cells, value_cells, out_weight, row_pattern, row_count, col_pattern, col_count
):
    row_span, col_span, _ = query_cells.shape
    peers = lax.axis_size("rows")
    row_share = row_span // lax.axis_size("cols")
    weight = lax.all_gather(out_weight.T, ("rows", "cols"), axis=0, tiled=True)
    me = lax.axis_index("rows").astype(jnp.int32).reshape(1)
    row_first = lax.axis_index("cols") * row_share
    pattern = lax.dynamic_slice_in_dim(row_pattern, row_first, row_share, 0)
    count = lax.dynamic_slice_in_dim(row_count, row_first, row_share, 0)

    packed = row_pack(query_cells, key_cells, value_cells)
    lines = lax.all_to_all(packed, "cols", 0, 0, tiled=True)
    sent = col_pack(me, query_cells, key_cells, value_cells, peers)
    pieces = swap_pieces(sent)
    row_out = row_attend(pattern, count, lines.reshape(-1, lines.shape[-1]))
    row_out = lax.all_to_all(row_out.reshape(row_span, col_span, -1), "cols", 0, 0, tiled=True)
    col_out = col_attend(me, col_pattern, col_count, pieces)
    col_out = swap_pieces(col_out)
    projected = project(me, row_out, col_out, weight)
    return projected.reshape(row_span, col_span, projected.shape[-1])


def solution(mesh):
    placed = (
        P("rows", "cols", None),
        P("rows", "cols", None),
        P("rows", "cols", None),
        P(None, ("rows", "cols")),
        P("rows", None, None),
        P("rows"),
        P("cols", None, None),
        P("cols"),
    )
    return jax.shard_map(
        body, mesh=mesh, in_specs=placed, out_specs=P("rows", "cols", None), check_vma=False
    )
```

profile of v0, /device:TPU:1, one launch (start us, length us, event | category | flops | bytes accessed | tf_op | source)
XLA Modules:
  0.0 193.4 jit_solution(2119400842141420951)
XLA Ops:
  7.3 4.2 %row_pack.1 = bf16[16,64,1536]{2,1,0:T(8,128)(2,1)} custom-call(bf16[16,64,1024]{2,1,0:T(8,128)(2,1)} %q_ref.3, bf16[16,64,1024]{2,1,0:T(8,128)(2,1)} %k_ref.3, bf16[16,64,1024]{2,1,0:T(8,128)(2,1)} %v_ref.3), custom_call_target="tpu_custom_call" | custom-call | tf_op jit(solution)/shard_map/row_pack/pallas_call | solution.py:30
  11.4 8.4 %all-to-all-start = ((bf16[16,64,1536]{2,1,0:T(8,128)(2,1)}), bf16[16,64,1536]{2,1,0:T(8,128)(2,1)S(1)}, u32[]{:S(2)}, u32[]{:S(2)}) async-start(bf16[16,64,1536]{2,1,0:T(8,128)(2,1)} %row_pack.1), calls=%async_computation | async-start | bytes 6291456 | tf_op jit(solution)/shard_map/all_to_all | solution.py:314
  19.9 6.8 %col_pack.1 = (bf16[8,16,1536]{2,1,0:T(8,128)(2,1)}, bf16[8,16,1536]{2,1,0:T(8,128)(2,1)}, bf16[8,16,1536]{2,1,0:T(8,128)(2,1)}, bf16[8,16,1536]{2,1,0:T(8,128)(...) custom-call(s32[1]{0:T(128)} %bitcast.me_ref, ...), custom_call_target="tpu_custom_call" | custom-call | tf_op jit(solution)/shard_map/col_pack/pallas_call | solution.py:75
  30.4 30.6 %all-to-all-done = bf16[16,64,1536]{2,1,0:T(8,128)(2,1)S(1)} async-done(((bf16[16,64,1536]{2,1,0:T(8,128)(2,1)}), bf16[16,64,1536]{2,1,0:T(8,128)(2,1)S(1)}, u32[]{:S(2)}, u32[]{:S(2)}) %all-to-all-start) | async-done | bytes 3145760 | tf_op jit(solution)/shard_map/all_to_all | solution.py:314
  61.0 1.7 copy-done.1
  62.6 14.3 %row_attend.1 = bf16[1024,512]{1,0:T(8,128)(2,1)} custom-call(s32[192]{0:T(256)} %reshape.19.pattern_ref, s32[1]{0:T(128)} %dynamic_slice.7.count_ref, bf16[1024,1536]{1,0:T(8,128)(2,1)} %bitcast.5), custom_call_target="tpu_custom_call" | custom-call | tf_op jit(solution)/shard_map/row_attend/pallas_call | solution.py:160
  76.9 8.3 %all-to-all-start.1 = ((bf16[16,64,512]{2,1,0:T(8,128)(2,1)}), bf16[16,64,512]{2,1,0:T(8,128)(2,1)S(1)}, u32[]{:S(2)}, u32[]{:S(2)}) async-start(bf16[16,64,512]{2,1,0:T(8,128)(2,1)} %bitcast.6), calls=%async_computation.1 | async-start | bytes 2097152 | tf_op jit(solution)/shard_map/all_to_all | solution.py:318
  85.2 3.6 %collective-permute-start.2 = (bf16[8,16,1536]{2,1,0:T(8,128)(2,1)}, bf16[8,16,1536]{2,1,0:T(8,128)(2,1)S(1)}, u32[]{:S(2)}, u32[]{:S(2)}) collective-permute-start(bf16[8,16,1536]{2,1,0:T(8,128)(2,1)} %get-tuple-element.24), channel_id=1, source_target_pairs={{0,48},{16,32},{32,16},{48,0},{64,112},{80,96},{96,80},{112,64},{1... | collective-permute-start | bytes 1179656 | tf_op jit(solution)/shard_map/ppermute | solution.py:296
  88.8 2.6 %collective-permute-start.3 = (bf16[8,16,1536]{2,1,0:T(8,128)(2,1)}, bf16[8,16,1536]{2,1,0:T(8,128)(2,1)S(1)}, u32[]{:S(2)}, u32[]{:S(2)}) collective-permute-start(bf16[8,16,1536]{2,1,0:T(8,128)(2,1)} %get-tuple-element.25), channel_id=1, source_target_pairs={{0,64},{16,80},{32,96},{48,112},{64,0},{80,16},{96,32},{112,48},{1... | collective-permute-start | bytes 1179656 | tf_op jit(solution)/shard_map/ppermute | solution.py:296
  91.5 2.2 %collective-permute-start.5 = (bf16[8,16,1536]{2,1,0:T(8,128)(2,1)}, bf16[8,16,1536]{2,1,0:T(8,128)(2,1)S(1)}, u32[]{:S(2)}, u32[]{:S(2)}) collective-permute-start(bf16[8,16,1536]{2,1,0:T(8,128)(2,1)} %get-tuple-element.27), channel_id=1, source_target_pairs={{0,96},{16,112},{32,64},{48,80},{64,32},{80,48},{96,0},{112,16},{1... | collective-permute-start | bytes 1179656 | tf_op jit(solution)/shard_map/ppermute | solution.py:296
  93.6 1.4 collective-permute-start.6
  95.9 6.9 %collective-permute-done.2.rest_3_ = bf16[8,16,1536]{2,1,0:T(8,128)(2,1)S(1)} collective-permute-done((bf16[8,16,1536]{2,1,0:T(8,128)(2,1)}, bf16[8,16,1536]{2,1,0:T(8,128)(2,1)S(1)}, u32[]{:S(2)}, u32[]{:S(2)}) %collective-permute-start.2) | collective-permute-done | bytes 393248 | tf_op jit(solution)/shard_map/ppermute | solution.py:296
  102.8 16.0 %collective-permute-done.3.rest_4_ = bf16[8,16,1536]{2,1,0:T(8,128)(2,1)S(1)} collective-permute-done((bf16[8,16,1536]{2,1,0:T(8,128)(2,1)}, bf16[8,16,1536]{2,1,0:T(8,128)(2,1)S(1)}, u32[]{:S(2)}, u32[]{:S(2)}) %collective-permute-start.3) | collective-permute-done | bytes 393248 | tf_op jit(solution)/shard_map/ppermute | solution.py:296
  118.8 8.1 %collective-permute-done.4.rest_5_ = bf16[8,16,1536]{2,1,0:T(8,128)(2,1)S(1)} collective-permute-done((bf16[8,16,1536]{2,1,0:T(8,128)(2,1)}, bf16[8,16,1536]{2,1,0:T(8,128)(2,1)S(1)}, u32[]{:S(2)}, u32[]{:S(2)}) %collective-permute-start.4) | collective-permute-done | bytes 393248 | tf_op jit(solution)/shard_map/ppermute | solution.py:296
  126.9 11.1 %collective-permute-done.6.rest_7_ = bf16[8,16,1536]{2,1,0:T(8,128)(2,1)S(1)} collective-permute-done((bf16[8,16,1536]{2,1,0:T(8,128)(2,1)}, bf16[8,16,1536]{2,1,0:T(8,128)(2,1)S(1)}, u32[]{:S(2)}, u32[]{:S(2)}) %collective-permute-start.6) | collective-permute-done | bytes 393248 | tf_op jit(solution)/shard_map/ppermute | solution.py:296
  138.8 12.3 %col_attend.1 = (bf16[16,8,512]{2,1,0:T(8,128)(2,1)}, bf16[16,8,512]{2,1,0:T(8,128)(2,1)}, bf16[16,8,512]{2,1,0:T(8,128)(2,1)}, bf16[16,8,512]{2,1,0:T(8,128)(2,...) custom-call(s32[1]{0:T(128)} %bitcast.me_ref, ...), custom_call_target="tpu_custom_call" | custom-call | tf_op jit(solution)/shard_map/col_attend/pallas_call | solution.py:232
  151.5 1.8 collective-permute-start.9
  153.9 2.7 %collective-permute-start.11 = (bf16[16,8,512]{2,1,0:T(8,128)(2,1)}, bf16[16,8,512]{2,1,0:T(8,128)(2,1)S(1)}, u32[]{:S(2)}, u32[]{:S(2)}) collective-permute-start(bf16[16,8,512]{2,1,0:T(8,128)(2,1)} %get-tuple-element.34), channel_id=1, source_target_pairs={{0,80},{16,64},{32,112},{48,96},{64,16},{80,0},{96,48},{112,32},{1... | collective-permute-start | bytes 393224 | tf_op jit(solution)/shard_map/ppermute | solution.py:296
  156.8 2.8 %collective-permute-start.13 = (bf16[16,8,512]{2,1,0:T(8,128)(2,1)}, bf16[16,8,512]{2,1,0:T(8,128)(2,1)S(1)}, u32[]{:S(2)}, u32[]{:S(2)}) collective-permute-start(bf16[16,8,512]{2,1,0:T(8,128)(2,1)} %get-tuple-element.36), channel_id=1, source_target_pairs={{0,112},{16,96},{32,80},{48,64},{64,48},{80,32},{96,16},{112,0},{1... | collective-permute-start | bytes 393224 | tf_op jit(solution)/shard_map/ppermute | solution.py:296
  160.4 1.6 collective-permute-done.10.rest_4_
  162.0 3.5 %collective-permute-done.11.rest_5_ = bf16[16,8,512]{2,1,0:T(8,128)(2,1)S(1)} collective-permute-done((bf16[16,8,512]{2,1,0:T(8,128)(2,1)}, bf16[16,8,512]{2,1,0:T(8,128)(2,1)S(1)}, u32[]{:S(2)}, u32[]{:S(2)}) %collective-permute-start.11) | collective-permute-done | bytes 131104 | tf_op jit(solution)/shard_map/ppermute | solution.py:296
  165.5 2.7 %collective-permute-done.12.rest_6_ = bf16[16,8,512]{2,1,0:T(8,128)(2,1)S(1)} collective-permute-done((bf16[16,8,512]{2,1,0:T(8,128)(2,1)}, bf16[16,8,512]{2,1,0:T(8,128)(2,1)S(1)}, u32[]{:S(2)}, u32[]{:S(2)}) %collective-permute-start.12) | collective-permute-done | bytes 131104 | tf_op jit(solution)/shard_map/ppermute | solution.py:296
  168.1 2.8 %collective-permute-done.13.rest_7_ = bf16[16,8,512]{2,1,0:T(8,128)(2,1)S(1)} collective-permute-done((bf16[16,8,512]{2,1,0:T(8,128)(2,1)}, bf16[16,8,512]{2,1,0:T(8,128)(2,1)S(1)}, u32[]{:S(2)}, u32[]{:S(2)}) %collective-permute-start.13) | collective-permute-done | bytes 131104 | tf_op jit(solution)/shard_map/ppermute | solution.py:296
  172.0 14.6 %project.1 = bf16[1024,4096]{1,0:T(8,128)(2,1)} custom-call(s32[1]{0:T(128)} %bitcast.me_ref, bf16[16,64,512]{2,1,0:T(8,128)(2,1)} %copy-done.2, bf16[16,8,512]{2,1,0:T(8,128)(2,1)} %get-tuple-element.29.rest_0_, bf16[16,8,512]{2,1,0:T(8,128)(2,1)} %copy-done.8, bf16[16,8,512]{2,1,0:T(8,128)(2,1)} %copy-done.9, bf16[16,8,512]{2,1,0:T(8,128)(2,1)} %copy-done.10, ...), custom_call_target="tpu_custom_call" | custom-call | tf_op jit(solution)/shard_map/project/pallas_call | solution.py:277
  (56 shorter events, 9.1 us)
Async XLA Ops:
  6.5 23.1 %copy-start = (s32[16,32,6]{1,0,2:T(8,128)S(1)}, s32[16,32,6]{1,0,2:T(8,128)}, u32[]{:S(2)}) copy-start(s32[16,32,6]{1,0,2:T(8,128)} %param.12) | copy-start | bytes 36868
  6.5 164.4 %all-gather.2.cloned.1.call-start = ((), (), s32[]{:S(2)}) async-start(), calls=%async_computation.2 | async-start | bytes 8454144 | tf_op jit(solution)/shard_map/all_gather | solution.py:307
  11.4 49.6 %all-to-all-start = ((bf16[16,64,1536]{2,1,0:T(8,128)(2,1)}), bf16[16,64,1536]{2,1,0:T(8,128)(2,1)S(1)}, u32[]{:S(2)}, u32[]{:S(2)}) async-start(bf16[16,64,1536]{2,1,0:T(8,128)(2,1)} %row_pack.1), calls=%async_computation | async-start | bytes 6291456 | tf_op jit(solution)/shard_map/all_to_all | solution.py:314
  26.7 64.8 %collective-permute-start = (bf16[8,16,1536]{2,1,0:T(8,128)(2,1)}, bf16[8,16,1536]{2,1,0:T(8,128)(2,1)}, u32[]{:S(2)}, u32[]{:S(2)}) collective-permute-start(bf16[8,16,1536]{2,1,0:T(8,128)(2,1)} %get-tuple-element.22), channel_id=1, source_target_pairs={{0,16},{16,0},{32,48},{48,32},{64,80},{80,64},{96,112},{112,96},{1... | collective-permute-start | bytes 1179656 | tf_op jit(solution)/shard_map/ppermute | solution.py:296
  27.7 65.9 %collective-permute-start.1 = (bf16[8,16,1536]{2,1,0:T(8,128)(2,1)}, bf16[8,16,1536]{2,1,0:T(8,128)(2,1)}, u32[]{:S(2)}, u32[]{:S(2)}) collective-permute-start(bf16[8,16,1536]{2,1,0:T(8,128)(2,1)} %get-tuple-element.23), channel_id=1, source_target_pairs={{0,32},{16,48},{32,0},{48,16},{64,96},{80,112},{96,64},{112,80},{1... | collective-permute-start | bytes 1179656 | tf_op jit(solution)/shard_map/ppermute | solution.py:296
  62.6 32.4 %copy-start.15 = (s32[64,4,2]{0,2,1:T(2,128)S(1)}, s32[64,4,2]{0,2,1:T(2,128)}, u32[]{:S(2)}) copy-start(s32[64,4,2]{0,2,1:T(2,128)} %param.14) | copy-start | bytes 6148
  76.9 94.0 %all-to-all-start.1 = ((bf16[16,64,512]{2,1,0:T(8,128)(2,1)}), bf16[16,64,512]{2,1,0:T(8,128)(2,1)S(1)}, u32[]{:S(2)}, u32[]{:S(2)}) async-start(bf16[16,64,512]{2,1,0:T(8,128)(2,1)} %bitcast.6), calls=%async_computation.1 | async-start | bytes 2097152 | tf_op jit(solution)/shard_map/all_to_all | solution.py:318
  85.2 17.6 %collective-permute-start.2 = (bf16[8,16,1536]{2,1,0:T(8,128)(2,1)}, bf16[8,16,1536]{2,1,0:T(8,128)(2,1)S(1)}, u32[]{:S(2)}, u32[]{:S(2)}) collective-permute-start(bf16[8,16,1536]{2,1,0:T(8,128)(2,1)} %get-tuple-element.24), channel_id=1, source_target_pairs={{0,48},{16,32},{32,16},{48,0},{64,112},{80,96},{96,80},{112,64},{1... | collective-permute-start | bytes 1179656 | tf_op jit(solution)/shard_map/ppermute | solution.py:296
  88.8 30.0 %collective-permute-start.3 = (bf16[8,16,1536]{2,1,0:T(8,128)(2,1)}, bf16[8,16,1536]{2,1,0:T(8,128)(2,1)S(1)}, u32[]{:S(2)}, u32[]{:S(2)}) collective-permute-start(bf16[8,16,1536]{2,1,0:T(8,128)(2,1)} %get-tuple-element.25), channel_id=1, source_target_pairs={{0,64},{16,80},{32,96},{48,112},{64,0},{80,16},{96,32},{112,48},{1... | collective-permute-start | bytes 1179656 | tf_op jit(solution)/shard_map/ppermute | solution.py:296
  91.5 35.5 %collective-permute-start.4 = (bf16[8,16,1536]{2,1,0:T(8,128)(2,1)}, bf16[8,16,1536]{2,1,0:T(8,128)(2,1)S(1)}, u32[]{:S(2)}, u32[]{:S(2)}) collective-permute-start(bf16[8,16,1536]{2,1,0:T(8,128)(2,1)} %get-tuple-element.26), channel_id=1, source_target_pairs={{0,80},{16,64},{32,112},{48,96},{64,16},{80,0},{96,48},{112,32},{1... | collective-permute-start | bytes 1179656 | tf_op jit(solution)/shard_map/ppermute | solution.py:296
  91.5 35.5 %collective-permute-start.5 = (bf16[8,16,1536]{2,1,0:T(8,128)(2,1)}, bf16[8,16,1536]{2,1,0:T(8,128)(2,1)S(1)}, u32[]{:S(2)}, u32[]{:S(2)}) collective-permute-start(bf16[8,16,1536]{2,1,0:T(8,128)(2,1)} %get-tuple-element.27), channel_id=1, source_target_pairs={{0,96},{16,112},{32,64},{48,80},{64,32},{80,48},{96,0},{112,16},{1... | collective-permute-start | bytes 1179656 | tf_op jit(solution)/shard_map/ppermute | solution.py:296
  93.6 44.4 %collective-permute-start.6 = (bf16[8,16,1536]{2,1,0:T(8,128)(2,1)}, bf16[8,16,1536]{2,1,0:T(8,128)(2,1)S(1)}, u32[]{:S(2)}, u32[]{:S(2)}) collective-permute-start(bf16[8,16,1536]{2,1,0:T(8,128)(2,1)} %get-tuple-element.28), channel_id=1, source_target_pairs={{0,112},{16,96},{32,80},{48,64},{64,48},{80,32},{96,16},{112,0},{1... | collective-permute-start | bytes 1179656 | tf_op jit(solution)/shard_map/ppermute | solution.py:296
  102.8 35.3 %copy-start.3 = (bf16[8,16,1536]{2,1,0:T(8,128)(2,1)}, bf16[8,16,1536]{2,1,0:T(8,128)(2,1)S(1)}, u32[]{:S(2)}) copy-start(bf16[8,16,1536]{2,1,0:T(8,128)(2,1)S(1)} %collective-permute-done.2.rest_3_) | copy-start | bytes 1179652
  118.8 19.2 %copy-start.4 = (bf16[8,16,1536]{2,1,0:T(8,128)(2,1)}, bf16[8,16,1536]{2,1,0:T(8,128)(2,1)S(1)}, u32[]{:S(2)}) copy-start(bf16[8,16,1536]{2,1,0:T(8,128)(2,1)S(1)} %collective-permute-done.3.rest_4_) | copy-start | bytes 1179652
  126.9 11.2 %copy-start.6 = (bf16[8,16,1536]{2,1,0:T(8,128)(2,1)}, bf16[8,16,1536]{2,1,0:T(8,128)(2,1)S(1)}, u32[]{:S(2)}) copy-start(bf16[8,16,1536]{2,1,0:T(8,128)(2,1)S(1)} %collective-permute-done.5.rest_6_) | copy-start | bytes 1179652
  151.1 5.4 %collective-permute-start.7 = (bf16[16,8,512]{2,1,0:T(8,128)(2,1)}, bf16[16,8,512]{2,1,0:T(8,128)(2,1)S(1)}, u32[]{:S(2)}, u32[]{:S(2)}) collective-permute-start(bf16[16,8,512]{2,1,0:T(8,128)(2,1)} %get-tuple-element.30), channel_id=1, source_target_pairs={{0,16},{16,0},{32,48},{48,32},{64,80},{80,64},{96,112},{112,96},{1... | collective-permute-start | bytes 393224 | tf_op jit(solution)/shard_map/ppermute | solution.py:296
  151.5 5.2 %collective-permute-start.8 = (bf16[16,8,512]{2,1,0:T(8,128)(2,1)}, bf16[16,8,512]{2,1,0:T(8,128)(2,1)S(1)}, u32[]{:S(2)}, u32[]{:S(2)}) collective-permute-start(bf16[16,8,512]{2,1,0:T(8,128)(2,1)} %get-tuple-element.31), channel_id=1, source_target_pairs={{0,32},{16,48},{32,0},{48,16},{64,96},{80,112},{96,64},{112,80},{1... | collective-permute-start | bytes 393224 | tf_op jit(solution)/shard_map/ppermute | solution.py:296
  151.5 8.9 %collective-permute-start.9 = (bf16[16,8,512]{2,1,0:T(8,128)(2,1)}, bf16[16,8,512]{2,1,0:T(8,128)(2,1)S(1)}, u32[]{:S(2)}, u32[]{:S(2)}) collective-permute-start(bf16[16,8,512]{2,1,0:T(8,128)(2,1)} %get-tuple-element.32), channel_id=1, source_target_pairs={{0,48},{16,32},{32,16},{48,0},{64,112},{80,96},{96,80},{112,64},{1... | collective-permute-start | bytes 393224 | tf_op jit(solution)/shard_map/ppermute | solution.py:296
  153.3 8.7 %collective-permute-start.10 = (bf16[16,8,512]{2,1,0:T(8,128)(2,1)}, bf16[16,8,512]{2,1,0:T(8,128)(2,1)S(1)}, u32[]{:S(2)}, u32[]{:S(2)}) collective-permute-start(bf16[16,8,512]{2,1,0:T(8,128)(2,1)} %get-tuple-element.33), channel_id=1, source_target_pairs={{0,64},{16,80},{32,96},{48,112},{64,0},{80,16},{96,32},{112,48},{1... | collective-permute-start | bytes 393224 | tf_op jit(solution)/shard_map/ppermute | solution.py:296
  153.9 11.6 %collective-permute-start.11 = (bf16[16,8,512]{2,1,0:T(8,128)(2,1)}, bf16[16,8,512]{2,1,0:T(8,128)(2,1)S(1)}, u32[]{:S(2)}, u32[]{:S(2)}) collective-permute-start(bf16[16,8,512]{2,1,0:T(8,128)(2,1)} %get-tuple-element.34), channel_id=1, source_target_pairs={{0,80},{16,64},{32,112},{48,96},{64,16},{80,0},{96,48},{112,32},{1... | collective-permute-start | bytes 393224 | tf_op jit(solution)/shard_map/ppermute | solution.py:296
  156.5 14.4 %copy-start.8 = (bf16[16,8,512]{2,1,0:T(8,128)(2,1)}, bf16[16,8,512]{2,1,0:T(8,128)(2,1)S(1)}, u32[]{:S(2)}) copy-start(bf16[16,8,512]{2,1,0:T(8,128)(2,1)S(1)} %collective-permute-done.7.rest_1_) | copy-start | bytes 393220
  156.5 11.6 %collective-permute-start.12 = (bf16[16,8,512]{2,1,0:T(8,128)(2,1)}, bf16[16,8,512]{2,1,0:T(8,128)(2,1)S(1)}, u32[]{:S(2)}, u32[]{:S(2)}) collective-permute-start(bf16[16,8,512]{2,1,0:T(8,128)(2,1)} %get-tuple-element.35), channel_id=1, source_target_pairs={{0,96},{16,112},{32,64},{48,80},{64,32},{80,48},{96,0},{112,16},{1... | collective-permute-start | bytes 393224 | tf_op jit(solution)/shard_map/ppermute | solution.py:296
  156.8 14.2 %copy-start.9 = (bf16[16,8,512]{2,1,0:T(8,128)(2,1)}, bf16[16,8,512]{2,1,0:T(8,128)(2,1)S(1)}, u32[]{:S(2)}) copy-start(bf16[16,8,512]{2,1,0:T(8,128)(2,1)S(1)} %collective-permute-done.8.rest_2_) | copy-start | bytes 393220
  156.8 14.1 %collective-permute-start.13 = (bf16[16,8,512]{2,1,0:T(8,128)(2,1)}, bf16[16,8,512]{2,1,0:T(8,128)(2,1)S(1)}, u32[]{:S(2)}, u32[]{:S(2)}) collective-permute-start(bf16[16,8,512]{2,1,0:T(8,128)(2,1)} %get-tuple-element.36), channel_id=1, source_target_pairs={{0,112},{16,96},{32,80},{48,64},{64,48},{80,32},{96,16},{112,0},{1... | collective-permute-start | bytes 393224 | tf_op jit(solution)/shard_map/ppermute | solution.py:296
  (10 other events, 52.5 us)
Sparse Core Ops, SparseCore 0:
  10.5 127.0 all-gather.1
where the time goes:
time: 194 us; the launch traced here: 193 us
  waiting for transfers between devices  84.8 us (44%)
  Pallas kernels  52.2 us (27%)
  starting transfers between devices  37.2 us (19%)
  between operations  13.5 us (7%)
  local copies, waits for them, and re-layouts  5.65 us (3%)
    ppermute x14, waiting for transfers between devices, swap_pieces(): lax.ppermute(pieces[s], 'rows', [(d, d ^ s) for d in range(peers)])  53.5 us
    all_to_all x1, waiting for transfers between devices, body(): lines = lax.all_to_all(packed, 'cols', 0, 0, tiled=True)  30.6 us
    ppermute x14, starting transfers between devices, swap_pieces(): lax.ppermute(pieces[s], 'rows', [(d, d ^ s) for d in range(peers)])  20.6 us
    pallas_call x1, Pallas kernels, project(): pl.pallas_call(project_kernel, grid_spec=pltpu.PrefetchScalarGridSpec(num...  14.6 us
    pallas_call x1, Pallas kernels, row_attend(): pl.pallas_call(functools.partial(row_attend_kernel, chosen=chosen), grid_...  14.3 us
    pallas_call x1, Pallas kernels, col_attend(): pl.pallas_call(functools.partial(col_attend_kernel, chosen=chosen), grid_...  12.3 us
    all_to_all x1, starting transfers between devices, body(): lines = lax.all_to_all(packed, 'cols', 0, 0, tiled=True)  8.42 us
    all_to_all x1, starting transfers between devices, body(): lax.all_to_all(row_out.reshape(row_span, col_span, -1), 'cols', 0, 0, til...  8.26 us
  transfers between devices with their start and end apart: 17, of which 10 were waited for; matrix products, arithmetic and copies ran while one was open for 1% of the time, Pallas kernels for 19%

commit v1 on v0

v1 whole, which is shorter than its diff:
```python
import functools
import math

import jax
import jax.numpy as jnp
from jax import lax
from jax.experimental import pallas as pl
from jax.experimental.pallas import tpu as pltpu
from jax.sharding import PartitionSpec as P


HR = 4
HC = 4
HD = 128
BLK = 32
NEG_FILL = -1e30
UNROLL = 4
EXP_SCALE = HD ** (-0.5) * math.log2(math.e)


def row_pack_kernel(q_ref, k_ref, v_ref, out_ref):
    width = HR * HD
    out_ref[:, :, 0:width] = q_ref[...]
    out_ref[:, :, width : 2 * width] = k_ref[...]
    out_ref[:, :, 2 * width : 3 * width] = v_ref[...]


def row_pack(q, k, v):
    span, cells, _ = q.shape
    width = HR * HD
    step = 4
    part = pl.BlockSpec((step, cells, width), lambda i: (i, 0, 0))
    return pl.pallas_call(
        row_pack_kernel,
        grid=(span // step,),
        in_specs=[part, part, part],
        out_specs=pl.BlockSpec((step, cells, 3 * width), lambda i: (i, 0, 0)),
        out_shape=jax.ShapeDtypeStruct((span, cells, 3 * width), q.dtype),
        name="row_pack",
    )(q, k, v)


def col_pack_kernel(me_ref, q_ref, k_ref, v_ref, *rest):
    outs, (wide, buf, sem) = rest[:-3], rest[-3:]
    peers = len(outs)
    width = HC * HD
    span, own, _ = q_ref.shape
    step = pl.program_id(0)
    slot = lax.rem(step, 2)

    @pl.when(step >= 2)
    def _():
        pltpu.make_async_copy(buf.at[slot], outs[0], sem.at[slot]).wait()

    for t, ref in enumerate((q_ref, k_ref, v_ref)):
        for h in range(HC):
            lanes = slice(h * HD, (h + 1) * HD)
            wide[t * HC + h] = ref[:, :, lanes].reshape(span * own, HD).astype(jnp.float32)
    for t in range(3):
        for h in range(HC):
            for j in range(own):
                line = wide[t * HC + h, pl.ds(j, span, stride=own), :]
                at = t * width + h * HD
                buf[slot, j, :, at : at + HD] = line.astype(jnp.bfloat16)
    for s in range(peers):

        @pl.when(step == s)
        def _(s=s):
            pltpu.make_async_copy(buf.at[slot], outs[s], sem.at[slot]).start()

    @pl.when(step == peers - 1)
    def _():
        pltpu.make_async_copy(buf.at[1 - slot], outs[0], sem.at[1 - slot]).wait()
        pltpu.make_async_copy(buf.at[slot], outs[0], sem.at[slot]).wait()


def col_pack(me, q, k, v, peers):
    span, cells, _ = q.shape
    width = HC * HD
    own = cells // peers
    part = pl.BlockSpec((span, own, width), lambda s, me: (0, me[0] ^ s, 1))
    piece = (own, span, 3 * width)
    return pl.pallas_call(
        col_pack_kernel,
        grid_spec=pltpu.PrefetchScalarGridSpec(
            num_scalar_prefetch=1,
            grid=(peers,),
            in_specs=[part, part, part],
            out_specs=[pl.BlockSpec(memory_space=pl.ANY)] * peers,
            scratch_shapes=[
                pltpu.VMEM((3 * HC, span * own, HD), jnp.float32),
                pltpu.VMEM((2,) + piece, q.dtype),
                pltpu.SemaphoreType.DMA((2,)),
            ],
        ),
        out_shape=[jax.ShapeDtypeStruct(piece, q.dtype)] * peers,
        name="col_pack",
    )(me, q, k, v)


def row_attend_kernel(pattern_ref, count_ref, x_ref, out_ref, *, chosen):
    width = HR * HD
    count = count_ref[0]
    blocks = x_ref.shape[0] // BLK
    key_lane = lax.broadcasted_iota(jnp.int32, (1, chosen * BLK), 1)
    slot_of = key_lane // BLK
    in_block = key_lane - slot_of * BLK
    query_row = lax.broadcasted_iota(jnp.int32, (BLK, 1), 0)
    zero = jnp.zeros((BLK, HD), jnp.bfloat16)

    def stage_scores(n):
        at = pl.multiple_of(n * BLK, BLK)
        q = x_ref[pl.ds(at, BLK), 0:width]
        keys = []
        limit = jnp.zeros((1, chosen * BLK), jnp.int32)
        for s in range(chosen):
            b = pattern_ref[n * chosen + s]
            k_at = pl.multiple_of(b * BLK, BLK)
            keys.append(x_ref[pl.ds(k_at, BLK), width : 2 * width])
            limit = jnp.where(slot_of == s, count - b * BLK, limit)
        keys = jnp.concatenate(keys, axis=0)
        live = in_block < limit
        spread = jnp.concatenate(
            [
                jnp.concatenate(
                    [q[:, h * HD : (h + 1) * HD] if g == h else zero for g in range(HR)], axis=1
                )
                for h in range(HR)
            ],
            axis=0,
        )
        scores = lax.dot_general(
            spread, keys, (((1,), (1,)), ((), ())), preferred_element_type=jnp.float32
        )
        return jnp.where(live, scores, NEG_FILL)

    def stage_values(n, weights, total):
        at = pl.multiple_of(n * BLK, BLK)
        values = []
        for s in range(chosen):
            k_at = pl.multiple_of(pattern_ref[n * chosen + s] * BLK, BLK)
            values.append(x_ref[pl.ds(k_at, BLK), 2 * width : 3 * width])
        values = jnp.concatenate(values, axis=0)
        query_live = (query_row + n * BLK) < count
        for pair in range(HR // 2):
            rows = slice(pair * 2 * BLK, (pair + 1) * 2 * BLK)
            lanes = slice(pair * 2 * HD, (pair + 1) * 2 * HD)
            added = lax.dot_general(
                weights[rows],
                values[:, lanes],
                (((1,), (0,)), ((), ())),
                preferred_element_type=jnp.float32,
            )
            for g in range(2):
                h = pair * 2 + g
                part = added[g * BLK : (g + 1) * BLK, g * HD : (g + 1) * HD]
                safe = jnp.where(query_live, total[h * BLK : (h + 1) * BLK], 1.0)
                done = jnp.where(query_live, part / safe, 0.0)
                out_ref[pl.ds(at, BLK), h * HD : (h + 1) * HD] = done.astype(jnp.bfloat16)

    def group(g, _):
        blocks_here = [g * UNROLL + u for u in range(UNROLL)]
        scores = [stage_scores(n) for n in blocks_here]
        tops = [jnp.max(s, axis=1, keepdims=True) for s in scores]
        weights = [jnp.exp2((s - m) * EXP_SCALE) for s, m in zip(scores, tops)]
        totals = [jnp.sum(w, axis=1, keepdims=True) for w in weights]
        for n, w, t in zip(blocks_here, weights, totals):
            stage_values(n, w.astype(jnp.bfloat16), t)
        return 0

    lax.fori_loop(0, blocks // UNROLL, group, 0)


def row_attend(pattern, count, x):
    cells = x.shape[0]
    chosen = pattern.shape[-1]
    return pl.pallas_call(
        functools.partial(row_attend_kernel, chosen=chosen),
        grid_spec=pltpu.PrefetchScalarGridSpec(
            num_scalar_prefetch=2,
            grid=(1,),
            in_specs=[pl.BlockSpec(x.shape, lambda i, *_: (0, 0), pipeline_mode=pl.Buffered(1))],
            out_specs=pl.BlockSpec((cells, HR * HD), lambda i, *_: (0, 0)),
        ),
        out_shape=jax.ShapeDtypeStruct((cells, HR * HD), x.dtype),
        name="row_attend",
    )(pattern.reshape(-1), count, x)


def col_attend_kernel(me_ref, pattern_ref, count_ref, *rest, chosen, lines):
    peers = (len(rest) - 2) // 2
    pieces, outs, (line, held) = rest[:peers], rest[peers : 2 * peers], rest[2 * peers :]
    width = HC * HD
    me = me_ref[0]
    step = pl.program_id(0)
    span = pieces[0].shape[1]
    cells = peers * span
    own = held.shape[1] // cells
    blocks = cells // BLK
    key_at = lax.broadcasted_iota(jnp.int32, (1, cells), 1)
    key_block = key_at // BLK
    query_row = lax.broadcasted_iota(jnp.int32, (cells, 1), 0)
    for u in range(lines):
        for s in range(peers):
            line[u, pl.ds(pl.multiple_of((me ^ s) * span, span), span), :] = pieces[s][u]
    jobs, scores = [], []
    for u in range(lines):
        j = step * lines + u
        first = me * own + j
        count = count_ref[first]
        rows = []
        for n in range(blocks):
            listed = key_block == pattern_ref[(first * blocks + n) * chosen]
            for s in range(1, chosen):
                listed = listed | (key_block == pattern_ref[(first * blocks + n) * chosen + s])
            row = jnp.where(listed & (key_at < count), 0.0, NEG_FILL)
            rows.append(jnp.broadcast_to(row, (BLK, cells)))
        bias = jnp.concatenate(rows, axis=0)
        query_live = query_row < count
        for h in range(HC):
            q = line[u, :, h * HD : (h + 1) * HD]
            k = line[u, :, width + h * HD : width + (h + 1) * HD]
            product = lax.dot_general(
                q, k, (((1,), (1,)), ((), ())), preferred_element_type=jnp.float32
            )
            scores.append(jnp.where(bias < 0.0, NEG_FILL, product))
            jobs.append((u, j, h, query_live))
    tops = [jnp.max(s, axis=1, keepdims=True) for s in scores]
    weights = [jnp.exp2((s - m) * EXP_SCALE) for s, m in zip(scores, tops)]
    totals = [jnp.sum(w, axis=1, keepdims=True) for w in weights]
    for (u, j, h, query_live), w, total in zip(jobs, weights, totals):
        v = line[u, :, 2 * width + h * HD : 2 * width + (h + 1) * HD]
        added = lax.dot_general(
            w.astype(jnp.bfloat16), v, (((1,), (0,)), ((), ())), preferred_element_type=jnp.float32
        )
        safe = jnp.where(query_live, total, 1.0)
        done = jnp.where(query_live, added / safe, 0.0)
        held[h, pl.ds(j, cells, stride=own), :] = done

    @pl.when(step == pl.num_programs(0) - 1)
    def _():
        for s in range(peers):
            at = pl.multiple_of((me ^ s) * span * own, span * own)
            for h in range(HC):
                part = held[h, pl.ds(at, span * own), :].reshape(span, own, HD)
                outs[s][:, :, h * HD : (h + 1) * HD] = part.astype(jnp.bfloat16)


def col_attend(me, pattern, count, pieces):
    peers = len(pieces)
    own, span, wide = pieces[0].shape
    width = HC * HD
    chosen = pattern.shape[-1]
    lines = 2
    result = (span, own, width)
    return pl.pallas_call(
        functools.partial(col_attend_kernel, chosen=chosen, lines=lines),
        grid_spec=pltpu.PrefetchScalarGridSpec(
            num_scalar_prefetch=3,
            grid=(own // lines,),
            in_specs=[pl.BlockSpec((lines, span, wide), lambda j, *_: (j, 0, 0))] * peers,
            out_specs=[pl.BlockSpec(result, lambda j, *_: (0, 0, 0))] * peers,
            scratch_shapes=[
                pltpu.VMEM((lines, peers * span, wide), jnp.bfloat16),
                pltpu.VMEM((HC, own * peers * span, HD), jnp.float32),
            ],
        ),
        out_shape=[jax.ShapeDtypeStruct(result, jnp.bfloat16)] * peers,
        name="col_attend",
    )(me, pattern.reshape(-1), count, *pieces)


def project_first_kernel(me_ref, row_ref, *rest):
    pieces, (w_ref, out_ref, heads) = rest[:-3], rest[-3:]
    width = HR * HD
    own = pieces[0].shape[1]

    @pl.when(pl.program_id(0) == 0)
    def _():
        me = me_ref[0]
        odd = lax.rem(me, 2) == 1
        heads[:, :, 0:width] = row_ref[...]
        for s in range(0, len(pieces), 2):
            a = pieces[s][...].astype(jnp.float32)
            b = pieces[s + 1][...].astype(jnp.float32)
            both = jnp.concatenate([jnp.where(odd, b, a), jnp.where(odd, a, b)], axis=1)
            at = pl.multiple_of(((me ^ s) // 2) * 2 * own, 2 * own)
            heads[:, pl.ds(at, 2 * own), width:] = both.astype(jnp.bfloat16)

    project_block(heads, w_ref, out_ref)


def project_block(heads, w_ref, out_ref):
    channels = heads.shape[2]
    out_ref[...] = lax.dot_general(
        heads[...].reshape(-1, channels),
        w_ref[...].reshape(-1, channels),
        (((1,), (1,)), ((), ())),
        preferred_element_type=jnp.float32,
    ).astype(jnp.bfloat16)


def project_second_kernel(me_ref, heads, w_ref, kept_ref, out_ref):
    project_block(heads, w_ref, out_ref)


def weight_spec(weight):
    planes, _, span, channels = weight.shape
    return pl.BlockSpec((planes, None, span, channels), lambda j, *_: (0, j, 0, 0))


def whole(a):
    return pl.BlockSpec(a.shape, lambda j, *_: (0,) * a.ndim)


def project_first(me, row_out, pieces, weight, outs):
    span, cells, _ = row_out.shape
    planes, turns, part, channels = weight.shape
    tile = planes * part
    return pl.pallas_call(
        project_first_kernel,
        grid_spec=pltpu.PrefetchScalarGridSpec(
            num_scalar_prefetch=1,
            grid=(turns,),
            in_specs=[whole(row_out)] + [whole(p) for p in pieces] + [weight_spec(weight)],
            out_specs=[
                pl.BlockSpec((span * cells, tile), lambda j, me: (0, me[0] ^ (2 * j))),
                pl.BlockSpec((span, cells, channels), lambda j, *_: (0, 0, 0)),
            ],
        ),
        out_shape=[
            jax.ShapeDtypeStruct((span * cells, outs), jnp.bfloat16),
            jax.ShapeDtypeStruct((span, cells, channels), jnp.bfloat16),
        ],
        name="project_first",
    )(me, row_out, *pieces, weight)


def project_second(me, heads, weight, kept):
    span, cells, _ = heads.shape
    planes, turns, part, _ = weight.shape
    tile = planes * part
    return pl.pallas_call(
        project_second_kernel,
        grid_spec=pltpu.PrefetchScalarGridSpec(
            num_scalar_prefetch=1,
            grid=(turns,),
            in_specs=[whole(heads), weight_spec(weight), pl.BlockSpec(memory_space=pl.ANY)],
            out_specs=pl.BlockSpec((span * cells, tile), lambda j, me: (0, me[0] ^ (2 * j + 1))),
        ),
        out_shape=jax.ShapeDtypeStruct(kept.shape, jnp.bfloat16),
        input_output_aliases={3: 0},
        name="project_second",
    )(me, heads, weight, kept)


def swap_pieces(pieces):
    peers = len(pieces)
    return [pieces[0]] + [
        lax.ppermute(pieces[s], "rows", [(d, d ^ s) for d in range(peers)])
        for s in range(1, peers)
    ]


def body(
    query_cells, key_cells, value_cells, out_weight, row_pattern, row_count, col_pattern, col_count
):
    row_span, col_span, _ = query_cells.shape
    peers = lax.axis_size("rows")
    row_share = row_span // lax.axis_size("cols")
    me = lax.axis_index("rows").astype(jnp.int32).reshape(1)
    row_first = lax.axis_index("cols") * row_share
    pattern = lax.dynamic_slice_in_dim(row_pattern, row_first, row_share, 0)
    count = lax.dynamic_slice_in_dim(row_count, row_first, row_share, 0)

    shard = out_weight.T
    near = [shard] + [
        lax.ppermute(shard, "rows", [(d, d ^ s) for d in range(peers)])
        for s in range(2, peers, 2)
    ]
    weight = lax.all_gather(jnp.stack(near)[None], "cols", axis=0, tiled=True)
    weight_other = lax.ppermute(weight, "rows", [(d, d ^ 1) for d in range(peers)])
    sent = col_pack(me, query_cells, key_cells, value_cells, peers)
    pieces = swap_pieces(sent)
    packed = row_pack(query_cells, key_cells, value_cells)
    lines = lax.all_to_all(packed, "cols", 0, 0, tiled=True)
    col_out = col_attend(me, col_pattern, col_count, pieces)
    col_out = swap_pieces(col_out)
    row_out = row_attend(pattern, count, lines.reshape(-1, lines.shape[-1]))
    row_out = lax.all_to_all(row_out.reshape(row_span, col_span, -1), "cols", 0, 0, tiled=True)
    half, heads = project_first(
        me, row_out, col_out, weight, out_weight.shape[1] * peers * lax.axis_size("cols")
    )
    projected = project_second(me, heads, weight_other, half)
    return projected.reshape(row_span, col_span, projected.shape[-1])


def solution(mesh):
    placed = (
        P("rows", "cols", None),
        P("rows", "cols", None),
        P("rows", "cols", None),
        P(None, ("rows", "cols")),
        P("rows", None, None),
        P("rows"),
        P("cols", None, None),
        P("cols"),
    )
    return jax.shard_map(
        body, mesh=mesh, in_specs=placed, out_specs=P("rows", "cols", None), check_vma=False
    )
```

time: 194 us -> 236 us (1.22)
  waiting for transfers between devices: 84.8 us -> 129 us
  Pallas kernels: 52.2 us -> 44.2 us
  starting transfers between devices: 37.2 us -> 41.5 us
    all_gather x1, waiting for transfers between devices: 0.02 us -> 53 us  [body(): weight = lax.all_gather(jnp.stack(near)[None], 'cols', axis=0, tiled=True)]
    ppermute x14, waiting for transfers between devices: 53.5 us -> 40.6 us  [swap_pieces(): lax.ppermute(pieces[s], 'rows', [(d, d ^ s) for d in range(peers)])]
    ppermute x0 -> x4, starting transfers between devices: none -> 5.35 us  [the longest x3 4.51 us: body(): lax.ppermute(shard, 'rows', [(d, d ^ s) for d in range(peers)])]
    pallas_call x1, Pallas kernels: 14.3 us -> 9.66 us  [row_attend(): pl.pallas_call(functools.partial(row_attend_kernel, chosen=chosen), grid_...]
    ppermute x0 -> x4, waiting for transfers between devices: none -> 4.16 us  [the longest x3 4.16 us: body(): lax.ppermute(shard, 'rows', [(d, d ^ s) for d in range(peers)])]
    all_to_all x1, starting transfers between devices: 8.42 us -> 4.98 us  [body(): lines = lax.all_to_all(packed, 'cols', 0, 0, tiled=True)]
    all_to_all x1, starting transfers between devices: 8.26 us -> 11.6 us  [body(): lax.all_to_all(row_out.reshape(row_span, col_span, -1), 'cols', 0, 0, til...]
    pallas_call x2 -> x3, Pallas kernels: 26.9 us -> 23.5 us  [the longest x1 8.79 us: project_first(): pl.pallas_call(project_first_kernel, grid_spec=pltpu.PrefetchScalarGridSp...]
  transfers between devices with their start and end apart: 17 -> 21, of which waited for: 10 -> 14; matrix products, arithmetic and copies ran while one was open for 1% -> 1% of each run, Pallas kernels for 19% -> 15%
where the time goes in v1:
time: 236 us; the launch traced here: 235 us
  waiting for transfers between devices  129 us (55%)
  Pallas kernels  44.2 us (19%)
  starting transfers between devices  41.5 us (18%)
  between operations  13.5 us (6%)
  local copies, waits for them, and re-layouts  5.71 us (2%)
    all_gather x1, waiting for transfers between devices, body(): weight = lax.all_gather(jnp.stack(near)[None], 'cols', axis=0, tiled=True)  53 us
    ppermute x14, waiting for transfers between devices, swap_pieces(): lax.ppermute(pieces[s], 'rows', [(d, d ^ s) for d in range(peers)])  40.6 us
    all_to_all x1, waiting for transfers between devices, body(): lines = lax.all_to_all(packed, 'cols', 0, 0, tiled=True)  30.9 us
    ppermute x14, starting transfers between devices, swap_pieces(): lax.ppermute(pieces[s], 'rows', [(d, d ^ s) for d in range(peers)])  19.6 us
    all_to_all x1, starting transfers between devices, body(): lax.all_to_all(row_out.reshape(row_span, col_span, -1), 'cols', 0, 0, til...  11.6 us
    pallas_call x1, Pallas kernels, row_attend(): pl.pallas_call(functools.partial(row_attend_kernel, chosen=chosen), grid_...  9.66 us
    pallas_call x1, Pallas kernels, project_first(): pl.pallas_call(project_first_kernel, grid_spec=pltpu.PrefetchScalarGridSp...  8.79 us
    pallas_call x1, Pallas kernels, project_second(): pl.pallas_call(project_second_kernel, grid_spec=pltpu.PrefetchScalarGridS...  8.5 us
  transfers between devices with their start and end apart: 21, of which 14 were waited for; matrix products, arithmetic and copies ran while one was open for 1% of the time, Pallas kernels for 15%

profile of v1, /device:TPU:1, one launch (start us, length us, event | category | flops | bytes accessed | tf_op | source)
XLA Modules:
  0.0 235.2 jit_solution(13578386433633088450)
XLA Ops:
  6.5 3.7 %collective-permute-start.15 = (bf16[32,1024]{1,0:T(8,128)(2,1)}, bf16[32,1024]{1,0:T(8,128)(2,1)S(1)}, u32[]{:S(2)}, u32[]{:S(2)}) collective-permute-start(bf16[32,1024]{1,0:T(8,128)(2,1)} %bitcast.15), channel_id=1, source_target_pairs={{0,64},{16,80},{32,96},{48,112},{64,0},{80,16},{96,32},{112,48},{1... | collective-permute-start | bytes 196616 | tf_op jit(solution)/shard_map/ppermute | solution.py:378
  12.1 2.1 collective-permute-done.14
  16.8 53.0 %all-gather.3.cloned.1.call-done = bf16[64,32,1024]{2,1,0:T(8,128)(2,1)} async-done(((bf16[4,32,1024]{2,1,0:T(8,128)(2,1)}), bf16[64,32,1024]{2,1,0:T(8,128)(2,1)}) %all-gather.3.cloned.1.call-update) | async-done | bytes 4194320 | tf_op jit(solution)/shard_map/all_gather | solution.py:381
  70.6 4.1 %row_pack.1 = bf16[16,64,1536]{2,1,0:T(8,128)(2,1)} custom-call(bf16[16,64,1024]{2,1,0:T(8,128)(2,1)} %q_ref.3, bf16[16,64,1024]{2,1,0:T(8,128)(2,1)} %k_ref.3, bf16[16,64,1024]{2,1,0:T(8,128)(2,1)} %v_ref.3), custom_call_target="tpu_custom_call" | custom-call | tf_op jit(solution)/shard_map/row_pack/pallas_call | solution.py:33
  74.8 5.0 %all-to-all-start = ((bf16[16,64,1536]{2,1,0:T(8,128)(2,1)}), bf16[16,64,1536]{2,1,0:T(8,128)(2,1)S(1)}, u32[]{:S(2)}, u32[]{:S(2)}) async-start(bf16[16,64,1536]{2,1,0:T(8,128)(2,1)} %row_pack.1), calls=%async_computation | async-start | bytes 6291456 | tf_op jit(solution)/shard_map/all_to_all | solution.py:386
  79.8 6.8 %col_pack.1 = (bf16[8,16,1536]{2,1,0:T(8,128)(2,1)}, bf16[8,16,1536]{2,1,0:T(8,128)(2,1)}, bf16[8,16,1536]{2,1,0:T(8,128)(2,1)}, bf16[8,16,1536]{2,1,0:T(8,128)(...) custom-call(s32[1]{0:T(128)} %bitcast.me_ref, ...), custom_call_target="tpu_custom_call" | custom-call | tf_op jit(solution)/shard_map/col_pack/pallas_call | solution.py:83
  90.3 30.9 %all-to-all-done = bf16[16,64,1536]{2,1,0:T(8,128)(2,1)S(1)} async-done(((bf16[16,64,1536]{2,1,0:T(8,128)(2,1)}), bf16[16,64,1536]{2,1,0:T(8,128)(2,1)S(1)}, u32[]{:S(2)}, u32[]{:S(2)}) %all-to-all-start) | async-done | bytes 3145760 | tf_op jit(solution)/shard_map/all_to_all | solution.py:386
  122.9 9.7 %row_attend.1 = bf16[1024,512]{1,0:T(8,128)(2,1)} custom-call(s32[192]{0:T(256)} %reshape.19.pattern_ref, s32[1]{0:T(128)} %dynamic_slice.7.count_ref, bf16[1024,1536]{1,0:T(8,128)(2,1)} %bitcast.11), custom_call_target="tpu_custom_call" | custom-call | tf_op jit(solution)/shard_map/row_attend/pallas_call | solution.py:177
  132.5 11.6 %all-to-all-start.1 = ((bf16[16,64,512]{2,1,0:T(8,128)(2,1)}), bf16[16,64,512]{2,1,0:T(8,128)(2,1)S(1)}, u32[]{:S(2)}, u32[]{:S(2)}) async-start(bf16[16,64,512]{2,1,0:T(8,128)(2,1)} %bitcast.12), calls=%async_computation.1 | async-start | bytes 2097152 | tf_op jit(solution)/shard_map/all_to_all | solution.py:390
  144.2 2.8 %collective-permute-start.3 = (bf16[8,16,1536]{2,1,0:T(8,128)(2,1)}, bf16[8,16,1536]{2,1,0:T(8,128)(2,1)S(1)}, u32[]{:S(2)}, u32[]{:S(2)}) collective-permute-start(bf16[8,16,1536]{2,1,0:T(8,128)(2,1)} %get-tuple-element.27), channel_id=1, source_target_pairs={{0,64},{16,80},{32,96},{48,112},{64,0},{80,16},{96,32},{112,48},{1... | collective-permute-start | bytes 1179656 | tf_op jit(solution)/shard_map/ppermute | solution.py:360
  148.8 2.5 %collective-permute-start.5 = (bf16[8,16,1536]{2,1,0:T(8,128)(2,1)}, bf16[8,16,1536]{2,1,0:T(8,128)(2,1)S(1)}, u32[]{:S(2)}, u32[]{:S(2)}) collective-permute-start(bf16[8,16,1536]{2,1,0:T(8,128)(2,1)} %get-tuple-element.29), channel_id=1, source_target_pairs={{0,96},{16,112},{32,64},{48,80},{64,32},{80,48},{96,0},{112,16},{1... | collective-permute-start | bytes 1179656 | tf_op jit(solution)/shard_map/ppermute | solution.py:360
  152.5 2.8 %collective-permute-done.3.rest_4_ = bf16[8,16,1536]{2,1,0:T(8,128)(2,1)S(1)} collective-permute-done((bf16[8,16,1536]{2,1,0:T(8,128)(2,1)}, bf16[8,16,1536]{2,1,0:T(8,128)(2,1)S(1)}, u32[]{:S(2)}, u32[]{:S(2)}) %collective-permute-start.3) | collective-permute-done | bytes 393248 | tf_op jit(solution)/shard_map/ppermute | solution.py:360
  155.3 10.1 %collective-permute-done.4.rest_5_ = bf16[8,16,1536]{2,1,0:T(8,128)(2,1)S(1)} collective-permute-done((bf16[8,16,1536]{2,1,0:T(8,128)(2,1)}, bf16[8,16,1536]{2,1,0:T(8,128)(2,1)S(1)}, u32[]{:S(2)}, u32[]{:S(2)}) %collective-permute-start.4) | collective-permute-done | bytes 393248 | tf_op jit(solution)/shard_map/ppermute | solution.py:360
  165.3 8.6 %collective-permute-done.5.rest_6_ = bf16[8,16,1536]{2,1,0:T(8,128)(2,1)S(1)} collective-permute-done((bf16[8,16,1536]{2,1,0:T(8,128)(2,1)}, bf16[8,16,1536]{2,1,0:T(8,128)(2,1)S(1)}, u32[]{:S(2)}, u32[]{:S(2)}) %collective-permute-start.5) | collective-permute-done | bytes 393248 | tf_op jit(solution)/shard_map/ppermute | solution.py:360
  173.9 8.4 %collective-permute-done.6.rest_7_ = bf16[8,16,1536]{2,1,0:T(8,128)(2,1)S(1)} collective-permute-done((bf16[8,16,1536]{2,1,0:T(8,128)(2,1)}, bf16[8,16,1536]{2,1,0:T(8,128)(2,1)S(1)}, u32[]{:S(2)}, u32[]{:S(2)}) %collective-permute-start.6) | collective-permute-done | bytes 393248 | tf_op jit(solution)/shard_map/ppermute | solution.py:360
  183.1 6.3 %col_attend.1 = (bf16[16,8,512]{2,1,0:T(8,128)(2,1)}, bf16[16,8,512]{2,1,0:T(8,128)(2,1)}, bf16[16,8,512]{2,1,0:T(8,128)(2,1)}, bf16[16,8,512]{2,1,0:T(8,128)(2,...) custom-call(s32[1]{0:T(128)} %bitcast.me_ref, ...), custom_call_target="tpu_custom_call" | custom-call | tf_op jit(solution)/shard_map/col_attend/pallas_call | solution.py:256
  191.5 2.8 %collective-permute-start.10 = (bf16[16,8,512]{2,1,0:T(8,128)(2,1)}, bf16[16,8,512]{2,1,0:T(8,128)(2,1)S(1)}, u32[]{:S(2)}, u32[]{:S(2)}) collective-permute-start(bf16[16,8,512]{2,1,0:T(8,128)(2,1)} %get-tuple-element.35), channel_id=1, source_target_pairs={{0,64},{16,80},{32,96},{48,112},{64,0},{80,16},{96,32},{112,48},{1... | collective-permute-start | bytes 393224 | tf_op jit(solution)/shard_map/ppermute | solution.py:360
  194.9 2.5 %collective-permute-start.12 = (bf16[16,8,512]{2,1,0:T(8,128)(2,1)}, bf16[16,8,512]{2,1,0:T(8,128)(2,1)S(1)}, u32[]{:S(2)}, u32[]{:S(2)}) collective-permute-start(bf16[16,8,512]{2,1,0:T(8,128)(2,1)} %get-tuple-element.37), channel_id=1, source_target_pairs={{0,96},{16,112},{32,64},{48,80},{64,32},{80,48},{96,0},{112,16},{1... | collective-permute-start | bytes 393224 | tf_op jit(solution)/shard_map/ppermute | solution.py:360
  198.6 1.9 collective-permute-start.13
  200.6 2.3 collective-permute-done.10.rest_4_
  202.8 3.1 %collective-permute-done.11.rest_5_ = bf16[16,8,512]{2,1,0:T(8,128)(2,1)S(1)} collective-permute-done((bf16[16,8,512]{2,1,0:T(8,128)(2,1)}, bf16[16,8,512]{2,1,0:T(8,128)(2,1)S(1)}, u32[]{:S(2)}, u32[]{:S(2)}) %collective-permute-start.11) | collective-permute-done | bytes 131104 | tf_op jit(solution)/shard_map/ppermute | solution.py:360
  206.0 4.1 %collective-permute-done.13.rest_7_ = bf16[16,8,512]{2,1,0:T(8,128)(2,1)S(1)} collective-permute-done((bf16[16,8,512]{2,1,0:T(8,128)(2,1)}, bf16[16,8,512]{2,1,0:T(8,128)(2,1)S(1)}, u32[]{:S(2)}, u32[]{:S(2)}) %collective-permute-start.13) | collective-permute-done | bytes 131104 | tf_op jit(solution)/shard_map/ppermute | solution.py:360
  211.1 8.8 %project_first.1 = (bf16[1024,4096]{1,0:T(8,128)(2,1)}, bf16[16,64,1024]{2,1,0:T(8,128)(2,1)}) custom-call(s32[1]{0:T(128)} %bitcast.me_ref, bf16[16,64,512]{2,1,0:T(8,128)(2,1)} %copy-done.2, bf16[16,8,512]{2,1,0:T(8,128)(2,1)} %get-tuple-element.31.rest_0_, bf16[16,8,512]{2,1,0:T(8,128)(2,1)} %copy-done.7, bf16[16,8,512]{2,1,0:T(8,128)(2,1)} %copy-done.8, ...), custom_call_target="tpu_custom_call" | custom-call | tf_op jit(solution)/shard_map/project_first/pallas_call | solution.py:320
  219.9 8.5 %project_second.1 = bf16[1024,4096]{1,0:T(8,128)(2,1)} custom-call(s32[1]{0:T(128)} %bitcast.me_ref, bf16[16,64,1024]{2,1,0:T(8,128)(2,1)} %get-tuple-element.39.heads, bf16[16,4,32,1024]{3,2,1,0:T(8,128)(2,1)} %collective-permute-done.17.w_ref, bf16[1024,4096]{1,0:T(8,128)(2,1)} %get-tuple-element.40.kept_ref), custom_call_target="tpu_custom_call", output_to_operand_aliasing={{}: (3, {})} | custom-call | tf_op jit(solution)/shard_map/project_second/pallas_call | solution.py:343
  (64 shorter events, 19.3 us)
Async XLA Ops:
  6.5 83.0 %copy-start = (s32[16,32,6]{1,0,2:T(8,128)S(1)}, s32[16,32,6]{1,0,2:T(8,128)}, u32[]{:S(2)}) copy-start(s32[16,32,6]{1,0,2:T(8,128)} %param.12) | copy-start | bytes 36868
  6.5 63.3 %all-gather.3.cloned.1.call-start = ((), (), s32[]{:S(2)}) async-start(), calls=%async_computation.2 | async-start | bytes 4456448 | tf_op jit(solution)/shard_map/all_gather | solution.py:381
  6.5 5.6 %collective-permute-start.15 = (bf16[32,1024]{1,0:T(8,128)(2,1)}, bf16[32,1024]{1,0:T(8,128)(2,1)S(1)}, u32[]{:S(2)}, u32[]{:S(2)}) collective-permute-start(bf16[32,1024]{1,0:T(8,128)(2,1)} %bitcast.15), channel_id=1, source_target_pairs={{0,64},{16,80},{32,96},{48,112},{64,0},{80,16},{96,32},{112,48},{1... | collective-permute-start | bytes 196616 | tf_op jit(solution)/shard_map/ppermute | solution.py:378
  10.3 4.0 %collective-permute-start.14 = (bf16[32,1024]{1,0:T(8,128)(2,1)}, bf16[32,1024]{1,0:T(8,128)(2,1)S(1)}, u32[]{:S(2)}, u32[]{:S(2)}) collective-permute-start(bf16[32,1024]{1,0:T(8,128)(2,1)} %bitcast.16), channel_id=1, source_target_pairs={{0,32},{16,48},{32,0},{48,16},{64,96},{80,112},{96,64},{112,80},{1... | collective-permute-start | bytes 196616 | tf_op jit(solution)/shard_map/ppermute | solution.py:378
  10.7 4.5 %collective-permute-start.16 = (bf16[32,1024]{1,0:T(8,128)(2,1)}, bf16[32,1024]{1,0:T(8,128)(2,1)S(1)}, u32[]{:S(2)}, u32[]{:S(2)}) collective-permute-start(bf16[32,1024]{1,0:T(8,128)(2,1)} %bitcast.17), channel_id=1, source_target_pairs={{0,96},{16,112},{32,64},{48,80},{64,32},{80,48},{96,0},{112,16},{1... | collective-permute-start | bytes 196616 | tf_op jit(solution)/shard_map/ppermute | solution.py:378
  69.8 150.1 %collective-permute-start.17 = (bf16[16,4,32,1024]{3,2,1,0:T(8,128)(2,1)}, bf16[16,4,32,1024]{3,2,1,0:T(8,128)(2,1)}, u32[]{:S(2)}, u32[]{:S(2)}) collective-permute-start(bf16[16,4,32,1024]{3,2,1,0:T(8,128)(2,1)} %bitcast.13), channel_id=1, source_target_pairs={{0,16},{16,0},{32,48},{48,32},{64,80},{80,64},{96,112},{112,96},{1... | collective-permute-start | bytes 12582920 | tf_op jit(solution)/shard_map/ppermute | solution.py:382
  74.8 46.4 %all-to-all-start = ((bf16[16,64,1536]{2,1,0:T(8,128)(2,1)}), bf16[16,64,1536]{2,1,0:T(8,128)(2,1)S(1)}, u32[]{:S(2)}, u32[]{:S(2)}) async-start(bf16[16,64,1536]{2,1,0:T(8,128)(2,1)} %row_pack.1), calls=%async_computation | async-start | bytes 6291456 | tf_op jit(solution)/shard_map/all_to_all | solution.py:386
  86.6 60.4 %collective-permute-start = (bf16[8,16,1536]{2,1,0:T(8,128)(2,1)}, bf16[8,16,1536]{2,1,0:T(8,128)(2,1)}, u32[]{:S(2)}, u32[]{:S(2)}) collective-permute-start(bf16[8,16,1536]{2,1,0:T(8,128)(2,1)} %get-tuple-element.24), channel_id=1, source_target_pairs={{0,16},{16,0},{32,48},{48,32},{64,80},{80,64},{96,112},{112,96},{1... | collective-permute-start | bytes 1179656 | tf_op jit(solution)/shard_map/ppermute | solution.py:360
  87.0 61.8 %collective-permute-start.1 = (bf16[8,16,1536]{2,1,0:T(8,128)(2,1)}, bf16[8,16,1536]{2,1,0:T(8,128)(2,1)}, u32[]{:S(2)}, u32[]{:S(2)}) collective-permute-start(bf16[8,16,1536]{2,1,0:T(8,128)(2,1)} %get-tuple-element.25), channel_id=1, source_target_pairs={{0,32},{16,48},{32,0},{48,16},{64,96},{80,112},{96,64},{112,80},{1... | collective-permute-start | bytes 1179656 | tf_op jit(solution)/shard_map/ppermute | solution.py:360
  88.2 63.1 %collective-permute-start.2 = (bf16[8,16,1536]{2,1,0:T(8,128)(2,1)}, bf16[8,16,1536]{2,1,0:T(8,128)(2,1)}, u32[]{:S(2)}, u32[]{:S(2)}) collective-permute-start(bf16[8,16,1536]{2,1,0:T(8,128)(2,1)} %get-tuple-element.26), channel_id=1, source_target_pairs={{0,48},{16,32},{32,16},{48,0},{64,112},{80,96},{96,80},{112,64},{1... | collective-permute-start | bytes 1179656 | tf_op jit(solution)/shard_map/ppermute | solution.py:360
  122.9 28.7 %copy-start.14 = (s32[64,4,2]{0,2,1:T(2,128)S(1)}, s32[64,4,2]{0,2,1:T(2,128)}, u32[]{:S(2)}) copy-start(s32[64,4,2]{0,2,1:T(2,128)} %param.14) | copy-start | bytes 6148
  132.5 77.5 %all-to-all-start.1 = ((bf16[16,64,512]{2,1,0:T(8,128)(2,1)}), bf16[16,64,512]{2,1,0:T(8,128)(2,1)S(1)}, u32[]{:S(2)}, u32[]{:S(2)}) async-start(bf16[16,64,512]{2,1,0:T(8,128)(2,1)} %bitcast.12), calls=%async_computation.1 | async-start | bytes 2097152 | tf_op jit(solution)/shard_map/all_to_all | solution.py:390
  144.2 11.1 %collective-permute-start.3 = (bf16[8,16,1536]{2,1,0:T(8,128)(2,1)}, bf16[8,16,1536]{2,1,0:T(8,128)(2,1)S(1)}, u32[]{:S(2)}, u32[]{:S(2)}) collective-permute-start(bf16[8,16,1536]{2,1,0:T(8,128)(2,1)} %get-tuple-element.27), channel_id=1, source_target_pairs={{0,64},{16,80},{32,96},{48,112},{64,0},{80,16},{96,32},{112,48},{1... | collective-permute-start | bytes 1179656 | tf_op jit(solution)/shard_map/ppermute | solution.py:360
  147.0 18.3 %collective-permute-start.4 = (bf16[8,16,1536]{2,1,0:T(8,128)(2,1)}, bf16[8,16,1536]{2,1,0:T(8,128)(2,1)S(1)}, u32[]{:S(2)}, u32[]{:S(2)}) collective-permute-start(bf16[8,16,1536]{2,1,0:T(8,128)(2,1)} %get-tuple-element.28), channel_id=1, source_target_pairs={{0,80},{16,64},{32,112},{48,96},{64,16},{80,0},{96,48},{112,32},{1... | collective-permute-start | bytes 1179656 | tf_op jit(solution)/shard_map/ppermute | solution.py:360
  148.8 25.1 %collective-permute-start.5 = (bf16[8,16,1536]{2,1,0:T(8,128)(2,1)}, bf16[8,16,1536]{2,1,0:T(8,128)(2,1)S(1)}, u32[]{:S(2)}, u32[]{:S(2)}) collective-permute-start(bf16[8,16,1536]{2,1,0:T(8,128)(2,1)} %get-tuple-element.29), channel_id=1, source_target_pairs={{0,96},{16,112},{32,64},{48,80},{64,32},{80,48},{96,0},{112,16},{1... | collective-permute-start | bytes 1179656 | tf_op jit(solution)/shard_map/ppermute | solution.py:360
  151.3 31.1 %collective-permute-start.6 = (bf16[8,16,1536]{2,1,0:T(8,128)(2,1)}, bf16[8,16,1536]{2,1,0:T(8,128)(2,1)S(1)}, u32[]{:S(2)}, u32[]{:S(2)}) collective-permute-start(bf16[8,16,1536]{2,1,0:T(8,128)(2,1)} %get-tuple-element.30), channel_id=1, source_target_pairs={{0,112},{16,96},{32,80},{48,64},{64,48},{80,32},{96,16},{112,0},{1... | collective-permute-start | bytes 1179656 | tf_op jit(solution)/shard_map/ppermute | solution.py:360
  155.3 27.1 %copy-start.3 = (bf16[8,16,1536]{2,1,0:T(8,128)(2,1)}, bf16[8,16,1536]{2,1,0:T(8,128)(2,1)S(1)}, u32[]{:S(2)}) copy-start(bf16[8,16,1536]{2,1,0:T(8,128)(2,1)S(1)} %collective-permute-done.3.rest_4_) | copy-start | bytes 1179652
  189.3 5.0 %collective-permute-start.7 = (bf16[16,8,512]{2,1,0:T(8,128)(2,1)}, bf16[16,8,512]{2,1,0:T(8,128)(2,1)S(1)}, u32[]{:S(2)}, u32[]{:S(2)}) collective-permute-start(bf16[16,8,512]{2,1,0:T(8,128)(2,1)} %get-tuple-element.32), channel_id=1, source_target_pairs={{0,16},{16,0},{32,48},{48,32},{64,80},{80,64},{96,112},{112,96},{1... | collective-permute-start | bytes 393224 | tf_op jit(solution)/shard_map/ppermute | solution.py:360
  189.8 5.1 %collective-permute-start.8 = (bf16[16,8,512]{2,1,0:T(8,128)(2,1)}, bf16[16,8,512]{2,1,0:T(8,128)(2,1)S(1)}, u32[]{:S(2)}, u32[]{:S(2)}) collective-permute-start(bf16[16,8,512]{2,1,0:T(8,128)(2,1)} %get-tuple-element.33), channel_id=1, source_target_pairs={{0,32},{16,48},{32,0},{48,16},{64,96},{80,112},{96,64},{112,80},{1... | collective-permute-start | bytes 393224 | tf_op jit(solution)/shard_map/ppermute | solution.py:360
  191.0 7.6 %collective-permute-start.9 = (bf16[16,8,512]{2,1,0:T(8,128)(2,1)}, bf16[16,8,512]{2,1,0:T(8,128)(2,1)S(1)}, u32[]{:S(2)}, u32[]{:S(2)}) collective-permute-start(bf16[16,8,512]{2,1,0:T(8,128)(2,1)} %get-tuple-element.34), channel_id=1, source_target_pairs={{0,48},{16,32},{32,16},{48,0},{64,112},{80,96},{96,80},{112,64},{1... | collective-permute-start | bytes 393224 | tf_op jit(solution)/shard_map/ppermute | solution.py:360
  191.5 11.3 %collective-permute-start.10 = (bf16[16,8,512]{2,1,0:T(8,128)(2,1)}, bf16[16,8,512]{2,1,0:T(8,128)(2,1)S(1)}, u32[]{:S(2)}, u32[]{:S(2)}) collective-permute-start(bf16[16,8,512]{2,1,0:T(8,128)(2,1)} %get-tuple-element.35), channel_id=1, source_target_pairs={{0,64},{16,80},{32,96},{48,112},{64,0},{80,16},{96,32},{112,48},{1... | collective-permute-start | bytes 393224 | tf_op jit(solution)/shard_map/ppermute | solution.py:360
  194.3 11.7 %collective-permute-start.11 = (bf16[16,8,512]{2,1,0:T(8,128)(2,1)}, bf16[16,8,512]{2,1,0:T(8,128)(2,1)S(1)}, u32[]{:S(2)}, u32[]{:S(2)}) collective-permute-start(bf16[16,8,512]{2,1,0:T(8,128)(2,1)} %get-tuple-element.36), channel_id=1, source_target_pairs={{0,80},{16,64},{32,112},{48,96},{64,16},{80,0},{96,48},{112,32},{1... | collective-permute-start | bytes 393224 | tf_op jit(solution)/shard_map/ppermute | solution.py:360
  194.9 11.0 %collective-permute-start.12 = (bf16[16,8,512]{2,1,0:T(8,128)(2,1)}, bf16[16,8,512]{2,1,0:T(8,128)(2,1)S(1)}, u32[]{:S(2)}, u32[]{:S(2)}) collective-permute-start(bf16[16,8,512]{2,1,0:T(8,128)(2,1)} %get-tuple-element.37), channel_id=1, source_target_pairs={{0,96},{16,112},{32,64},{48,80},{64,32},{80,48},{96,0},{112,16},{1... | collective-permute-start | bytes 393224 | tf_op jit(solution)/shard_map/ppermute | solution.py:360
  198.6 11.5 %collective-permute-start.13 = (bf16[16,8,512]{2,1,0:T(8,128)(2,1)}, bf16[16,8,512]{2,1,0:T(8,128)(2,1)S(1)}, u32[]{:S(2)}, u32[]{:S(2)}) collective-permute-start(bf16[16,8,512]{2,1,0:T(8,128)(2,1)} %get-tuple-element.38), channel_id=1, source_target_pairs={{0,112},{16,96},{32,80},{48,64},{64,48},{80,32},{96,16},{112,0},{1... | collective-permute-start | bytes 393224 | tf_op jit(solution)/shard_map/ppermute | solution.py:360
  (13 other events, 96.6 us)
Sparse Core Ops, SparseCore 0:
  16.9 52.8 all-gather.2

commit v2 on v1

--- a/solution.py
+++ b/solution.py
@@ -179,7 +179,7 @@
         grid_spec=pltpu.PrefetchScalarGridSpec(
             num_scalar_prefetch=2,
             grid=(1,),
-            in_specs=[pl.BlockSpec(x.shape, lambda i, *_: (0, 0), pipeline_mode=pl.Buffered(1))],
+            in_specs=[pl.BlockSpec(memory_space=pltpu.VMEM)],
             out_specs=pl.BlockSpec((cells, HR * HD), lambda i, *_: (0, 0)),
         ),
         out_shape=jax.ShapeDtypeStruct((cells, HR * HD), x.dtype),
@@ -270,8 +270,24 @@
     )(me, pattern.reshape(-1), count, *pieces)
 
 
-def project_first_kernel(me_ref, row_ref, *rest):
-    pieces, (w_ref, out_ref, heads) = rest[:-3], rest[-3:]
+def project_block(plane, heads, weights, line, out_ref):
+    quarter = len(weights)
+    near, span, channels = weights[0].shape
+    for sx in range(quarter):
+        for sz in range(near):
+            at = ((plane // near ^ sx) * near + (lax.rem(plane, near) ^ sz)) * span
+            line[pl.ds(pl.multiple_of(at, span), span), :] = weights[sx][sz]
+    out_ref[...] = lax.dot_general(
+        heads[...].reshape(-1, channels),
+        line[...],
+        (((1,), (1,)), ((), ())),
+        preferred_element_type=jnp.float32,
+    ).astype(jnp.bfloat16)
+
+
+def project_first_kernel(me_ref, row_ref, *rest, quarter):
+    pieces, weights = rest[: -3 - quarter], rest[-3 - quarter : -3]
+    out_ref, heads, line = rest[-3:]
     width = HR * HD
     own = pieces[0].shape[1]
 
@@ -287,71 +303,72 @@
             at = pl.multiple_of(((me ^ s) // 2) * 2 * own, 2 * own)
             heads[:, pl.ds(at, 2 * own), width:] = both.astype(jnp.bfloat16)
 
-    project_block(heads, w_ref, out_ref)
-
-
-def project_block(heads, w_ref, out_ref):
-    channels = heads.shape[2]
-    out_ref[...] = lax.dot_general(
-        heads[...].reshape(-1, channels),
-        w_ref[...].reshape(-1, channels),
-        (((1,), (1,)), ((), ())),
-        preferred_element_type=jnp.float32,
-    ).astype(jnp.bfloat16)
-
-
-def project_second_kernel(me_ref, heads, w_ref, kept_ref, out_ref):
-    project_block(heads, w_ref, out_ref)
+    project_block(me_ref[1], heads, weights, line, out_ref)
+
+
+def project_second_kernel(me_ref, heads, *rest, quarter):
+    weights, (_, out_ref, line) = rest[:quarter], rest[quarter:]
+    project_block(me_ref[1], heads, weights, line, out_ref)
 
 
 def weight_spec(weight):
-    planes, _, span, channels = weight.shape
-    return pl.BlockSpec((planes, None, span, channels), lambda j, *_: (0, j, 0, 0))
+    near, _, span, channels = weight.shape
+    return pl.BlockSpec((near, None, span, channels), lambda j, *_: (0, j, 0, 0))
 
 
 def whole(a):
     return pl.BlockSpec(a.shape, lambda j, *_: (0,) * a.ndim)
 
 
-def project_first(me, row_out, pieces, weight, outs):
+def project_first(me, row_out, pieces, weights, outs):
     span, cells, _ = row_out.shape
-    planes, turns, part, channels = weight.shape
-    tile = planes * part
-    return pl.pallas_call(
-        project_first_kernel,
+    near, turns, part, channels = weights[0].shape
+    tile = len(weights) * near * part
+    held = pl.BlockSpec(memory_space=pltpu.VMEM)
+    return pl.pallas_call(
+        functools.partial(project_first_kernel, quarter=len(weights)),
         grid_spec=pltpu.PrefetchScalarGridSpec(
             num_scalar_prefetch=1,
             grid=(turns,),
-            in_specs=[whole(row_out)] + [whole(p) for p in pieces] + [weight_spec(weight)],
+            in_specs=[held] * (1 + len(pieces)) + [weight_spec(w) for w in weights],
             out_specs=[
                 pl.BlockSpec((span * cells, tile), lambda j, me: (0, me[0] ^ (2 * j))),
                 pl.BlockSpec((span, cells, channels), lambda j, *_: (0, 0, 0)),
             ],
+            scratch_shapes=[pltpu.VMEM((tile, channels), jnp.bfloat16)],
         ),
         out_shape=[
             jax.ShapeDtypeStruct((span * cells, outs), jnp.bfloat16),
             jax.ShapeDtypeStruct((span, cells, channels), jnp.bfloat16),
         ],
         name="project_first",
-    )(me, row_out, *pieces, weight)
-
-
-def project_second(me, heads, weight, kept):
-    span, cells, _ = heads.shape
-    planes, turns, part, _ = weight.shape
-    tile = planes * part
-    return pl.pallas_call(
-        project_second_kernel,
+    )(me, row_out, *pieces, *weights)
+
+
+def project_second(me, heads, weights, kept):
+    span, cells, channels = heads.shape
+    near, turns, part, _ = weights[0].shape
+    tile = len(weights) * near * part
+    return pl.pallas_call(
+        functools.partial(project_second_kernel, quarter=len(weights)),
         grid_spec=pltpu.PrefetchScalarGridSpec(
             num_scalar_prefetch=1,
             grid=(turns,),
-            in_specs=[whole(heads), weight_spec(weight), pl.BlockSpec(memory_space=pl.ANY)],
+            in_specs=[whole(heads)]
+            + [weight_spec(w) for w in weights]
+            + [pl.BlockSpec(memory_space=pl.ANY)],
             out_specs=pl.BlockSpec((span * cells, tile), lambda j, me: (0, me[0] ^ (2 * j + 1))),
+            scratch_shapes=[pltpu.VMEM((tile, channels), jnp.bfloat16)],
         ),
         out_shape=jax.ShapeDtypeStruct(kept.shape, jnp.bfloat16),
-        input_output_aliases={3: 0},
+        input_output_aliases={2 + len(weights): 0},
         name="project_second",
-    )(me, heads, weight, kept)
+    )(me, heads, *weights, kept)
+
+
+def by_xor(x, axis, masks):
+    size = lax.axis_size(axis)
+    return [lax.ppermute(x, axis, [(d, d ^ s) for d in range(size)]) for s in masks]
 
 
 def swap_pieces(pieces):
@@ -373,25 +390,31 @@
     pattern = lax.dynamic_slice_in_dim(row_pattern, row_first, row_share, 0)
     count = lax.dynamic_slice_in_dim(row_count, row_first, row_share, 0)
 
+    place = jnp.stack([lax.axis_index("rows"), lax.axis_index("cols")]).astype(jnp.int32)
+
     shard = out_weight.T
-    near = [shard] + [
-        lax.ppermute(shard, "rows", [(d, d ^ s) for d in range(peers)])
-        for s in range(2, peers, 2)
-    ]
-    weight = lax.all_gather(jnp.stack(near)[None], "cols", axis=0, tiled=True)
-    weight_other = lax.ppermute(weight, "rows", [(d, d ^ 1) for d in range(peers)])
+    along_y = [shard] + by_xor(shard, "rows", (2, 4, 6))
+    packed = row_pack(query_cells, key_cells, value_cells)
+    lines = lax.all_to_all(packed, "cols", 0, 0, tiled=True)
+    held = jnp.stack(along_y)
+    along_z = [held] + by_xor(held, "cols", (1, 2, 3))
     sent = col_pack(me, query_cells, key_cells, value_cells, peers)
     pieces = swap_pieces(sent)
-    packed = row_pack(query_cells, key_cells, value_cells)
-    lines = lax.all_to_all(packed, "cols", 0, 0, tiled=True)
+    held = jnp.stack(along_z)
+    weights = [held] + by_xor(held, "cols", (4, 8, 12))
+    row_out = row_attend(pattern, count, lines.reshape(-1, lines.shape[-1]))
+    row_out = lax.all_to_all(row_out.reshape(row_span, col_span, -1), "cols", 0, 0, tiled=True)
     col_out = col_attend(me, col_pattern, col_count, pieces)
     col_out = swap_pieces(col_out)
-    row_out = row_attend(pattern, count, lines.reshape(-1, lines.shape[-1]))
-    row_out = lax.all_to_all(row_out.reshape(row_span, col_span, -1), "cols", 0, 0, tiled=True)
+    others = [by_xor(w, "rows", (1,))[0] for w in weights]
     half, heads = project_first(
-        me, row_out, col_out, weight, out_weight.shape[1] * peers * lax.axis_size("cols")
+        place,
+        row_out,
+        col_out,
+        weights,
+        out_weight.shape[1] * peers * lax.axis_size("cols"),
     )
-    projected = project_second(me, heads, weight_other, half)
+    projected = project_second(place, heads, others, half)
     return projected.reshape(row_span, col_span, projected.shape[-1])
 
 

time: 236 us -> 202 us (0.86)
  waiting for transfers between devices: 129 us -> 89.5 us
  starting transfers between devices: 41.5 us -> 57 us
  between operations: 13.5 us -> 0.16 us
    all_gather x1 -> x0, waiting for transfers between devices: 53 us -> none  [body(): weight = lax.all_gather(jnp.stack(near)[None], 'cols', axis=0, tiled=True)]
    all_to_all x1, waiting for transfers between devices: 30.9 us -> 0.01 us  [body(): lines = lax.all_to_all(packed, 'cols', 0, 0, tiled=True)]
    ppermute x4 -> x13, waiting for transfers between devices: 4.16 us -> 31.6 us  [by_xor(): lax.ppermute(x, axis, [(d, d ^ s) for d in range(size)])]
    ppermute x14, waiting for transfers between devices: 40.6 us -> 57.9 us  [swap_pieces(): lax.ppermute(pieces[s], 'rows', [(d, d ^ s) for d in range(peers)])]
    ppermute x4 -> x13, starting transfers between devices: 5.35 us -> 18.1 us  [by_xor(): lax.ppermute(x, axis, [(d, d ^ s) for d in range(size)])]
    all_to_all x1, starting transfers between devices: 11.6 us -> 4.39 us  [body(): lax.all_to_all(row_out.reshape(row_span, col_span, -1), 'cols', 0, 0, til...]
    ppermute x14, starting transfers between devices: 19.6 us -> 26 us  [swap_pieces(): lax.ppermute(pieces[s], 'rows', [(d, d ^ s) for d in range(peers)])]
    all_to_all x1, starting transfers between devices: 4.98 us -> 8.55 us  [body(): lines = lax.all_to_all(packed, 'cols', 0, 0, tiled=True)]
  transfers between devices with their start and end apart: 21 -> 29, of which waited for: 14 -> 18; matrix products, arithmetic and copies ran while one was open for 1% -> 3% of each run, Pallas kernels for 15% -> 16%
where the time goes in v2:
time: 202 us; the launch traced here: 201 us
  waiting for transfers between devices  89.5 us (44%)
  starting transfers between devices  57 us (28%)
  Pallas kernels  45.8 us (23%)
  local copies, waits for them, and re-layouts  4.95 us (2%)
  other arithmetic  3.58 us (2%)
    ppermute x14, waiting for transfers between devices, swap_pieces(): lax.ppermute(pieces[s], 'rows', [(d, d ^ s) for d in range(peers)])  57.9 us
    ppermute x13, waiting for transfers between devices, by_xor(): lax.ppermute(x, axis, [(d, d ^ s) for d in range(size)])  31.6 us
    ppermute x14, starting transfers between devices, swap_pieces(): lax.ppermute(pieces[s], 'rows', [(d, d ^ s) for d in range(peers)])  26 us
    ppermute x13, starting transfers between devices, by_xor(): lax.ppermute(x, axis, [(d, d ^ s) for d in range(size)])  18.1 us
    pallas_call x1, Pallas kernels, row_attend(): pl.pallas_call(functools.partial(row_attend_kernel, chosen=chosen), grid_...  9.69 us
    pallas_call x1, Pallas kernels, project_first(): pl.pallas_call(functools.partial(project_first_kernel, quarter=len(weight...  9.54 us
    pallas_call x1, Pallas kernels, project_second(): pl.pallas_call(functools.partial(project_second_kernel, quarter=len(weigh...  9.38 us
    all_to_all x1, starting transfers between devices, body(): lines = lax.all_to_all(packed, 'cols', 0, 0, tiled=True)  8.55 us
  transfers between devices with their start and end apart: 29, of which 18 were waited for; matrix products, arithmetic and copies ran while one was open for 3% of the time, Pallas kernels for 16%

profile of v2, /device:TPU:1, one launch (start us, length us, event | category | flops | bytes accessed | tf_op | source)
XLA Modules:
  0.0 201.0 jit_solution(3537544471449877625)
XLA Ops:
  0.0 4.2 %row_pack.1 = bf16[16,64,1536]{2,1,0:T(8,128)(2,1)} custom-call(bf16[16,64,1024]{2,1,0:T(8,128)(2,1)} %q_ref.3, bf16[16,64,1024]{2,1,0:T(8,128)(2,1)} %k_ref.3, bf16[16,64,1024]{2,1,0:T(8,128)(2,1)} %v_ref.3), custom_call_target="tpu_custom_call" | custom-call | tf_op jit(solution)/shard_map/row_pack/pallas_call | solution.py:33
  4.2 8.5 %all-to-all-start = ((bf16[16,64,1536]{2,1,0:T(8,128)(2,1)}), bf16[16,64,1536]{2,1,0:T(8,128)(2,1)S(1)}, u32[]{:S(2)}, u32[]{:S(2)}) async-start(bf16[16,64,1536]{2,1,0:T(8,128)(2,1)} %row_pack.1), calls=%async_computation | async-start | bytes 6291456 | tf_op jit(solution)/shard_map/all_to_all | solution.py:398
  25.3 6.8 %col_pack.1 = (bf16[8,16,1536]{2,1,0:T(8,128)(2,1)}, bf16[8,16,1536]{2,1,0:T(8,128)(2,1)}, bf16[8,16,1536]{2,1,0:T(8,128)(2,1)}, bf16[8,16,1536]{2,1,0:T(8,128)(...) custom-call(s32[1]{0:T(128)} %bitcast.me_ref, ...), custom_call_target="tpu_custom_call" | custom-call | tf_op jit(solution)/shard_map/col_pack/pallas_call | solution.py:83
  32.1 3.3 %collective-permute-start = (bf16[8,16,1536]{2,1,0:T(8,128)(2,1)}, bf16[8,16,1536]{2,1,0:T(8,128)(2,1)}, u32[]{:S(2)}, u32[]{:S(2)}) collective-permute-start(bf16[8,16,1536]{2,1,0:T(8,128)(2,1)} %get-tuple-element.24), channel_id=1, source_target_pairs={{0,16},{16,0},{32,48},{48,32},{64,80},{80,64},{96,112},{112,96},{1... | collective-permute-start | bytes 1179656 | tf_op jit(solution)/shard_map/ppermute | solution.py:377
  35.4 16.5 %collective-permute-done.18 = bf16[4,32,1024]{2,1,0:T(8,128)(2,1)} collective-permute-done((bf16[4,32,1024]{2,1,0:T(8,128)(2,1)}, bf16[4,32,1024]{2,1,0:T(8,128)(2,1)}, u32[]{:S(2)}, u32[]{:S(2)}) %collective-permute-start.18) | collective-permute-done | bytes 262176 | tf_op jit(solution)/shard_map/ppermute | solution.py:371
  51.9 8.2 %collective-permute-done.17 = bf16[4,32,1024]{2,1,0:T(8,128)(2,1)} collective-permute-done((bf16[4,32,1024]{2,1,0:T(8,128)(2,1)}, bf16[4,32,1024]{2,1,0:T(8,128)(2,1)}, u32[]{:S(2)}, u32[]{:S(2)}) %collective-permute-start.17) | collective-permute-done | bytes 262176 | tf_op jit(solution)/shard_map/ppermute | solution.py:371
  63.6 3.9 %collective-permute-start.22 = (bf16[4,4,32,1024]{3,2,1,0:T(8,128)(2,1)}, bf16[4,4,32,1024]{3,2,1,0:T(8,128)(2,1)}, u32[]{:S(2)}, u32[]{:S(2)}) collective-permute-start(bf16[4,4,32,1024]{3,2,1,0:T(8,128)(2,1)} %pad_maximum_fusion.rest_8_), channel_id=1, source_target_pairs={{0,12},{1,13},{2,14},{3,15},{4,8},{5,9},{6,10},{7,11},{8,4},{9,5},... | collective-permute-start | bytes 3145736 | tf_op jit(solution)/shard_map/ppermute | solution.py:371
  70.2 3.6 %collective-permute-start.2 = (bf16[8,16,1536]{2,1,0:T(8,128)(2,1)}, bf16[8,16,1536]{2,1,0:T(8,128)(2,1)}, u32[]{:S(2)}, u32[]{:S(2)}) collective-permute-start(bf16[8,16,1536]{2,1,0:T(8,128)(2,1)} %get-tuple-element.26), channel_id=1, source_target_pairs={{0,48},{16,32},{32,16},{48,0},{64,112},{80,96},{96,80},{112,64},{1... | collective-permute-start | bytes 1179656 | tf_op jit(solution)/shard_map/ppermute | solution.py:377
  76.4 7.7 %collective-permute-done.2.rest_3_ = bf16[8,16,1536]{2,1,0:T(8,128)(2,1)} collective-permute-done((bf16[8,16,1536]{2,1,0:T(8,128)(2,1)}, bf16[8,16,1536]{2,1,0:T(8,128)(2,1)}, u32[]{:S(2)}, u32[]{:S(2)}) %collective-permute-start.2) | collective-permute-done | bytes 393248 | tf_op jit(solution)/shard_map/ppermute | solution.py:377
  87.1 7.7 %collective-permute-done.3.rest_4_ = bf16[8,16,1536]{2,1,0:T(8,128)(2,1)} collective-permute-done((bf16[8,16,1536]{2,1,0:T(8,128)(2,1)}, bf16[8,16,1536]{2,1,0:T(8,128)(2,1)}, u32[]{:S(2)}, u32[]{:S(2)}) %collective-permute-start.3) | collective-permute-done | bytes 393248 | tf_op jit(solution)/shard_map/ppermute | solution.py:377
  94.8 7.1 %collective-permute-done.4.rest_5_ = bf16[8,16,1536]{2,1,0:T(8,128)(2,1)} collective-permute-done((bf16[8,16,1536]{2,1,0:T(8,128)(2,1)}, bf16[8,16,1536]{2,1,0:T(8,128)(2,1)}, u32[]{:S(2)}, u32[]{:S(2)}) %collective-permute-start.4) | collective-permute-done | bytes 393248 | tf_op jit(solution)/shard_map/ppermute | solution.py:377
  104.0 6.9 %collective-permute-done.5.rest_6_ = bf16[8,16,1536]{2,1,0:T(8,128)(2,1)} collective-permute-done((bf16[8,16,1536]{2,1,0:T(8,128)(2,1)}, bf16[8,16,1536]{2,1,0:T(8,128)(2,1)}, u32[]{:S(2)}, u32[]{:S(2)}) %collective-permute-start.5) | collective-permute-done | bytes 393248 | tf_op jit(solution)/shard_map/ppermute | solution.py:377
  118.8 9.7 %row_attend.1 = bf16[1024,512]{1,0:T(8,128)(2,1)} custom-call(s32[192]{0:T(256)} %reshape.16.pattern_ref, s32[1]{0:T(128)} %dynamic_slice.7.count_ref, bf16[1024,1536]{1,0:T(8,128)(2,1)} %bitcast.16), custom_call_target="tpu_custom_call" | custom-call | tf_op jit(solution)/shard_map/row_attend/pallas_call | solution.py:177
  128.5 4.4 %all-to-all-start.1 = ((bf16[16,64,512]{2,1,0:T(8,128)(2,1)}), bf16[16,64,512]{2,1,0:T(8,128)(2,1)S(1)}, u32[]{:S(2)}, u32[]{:S(2)}) async-start(bf16[16,64,512]{2,1,0:T(8,128)(2,1)} %bitcast.17), calls=%async_computation.1 | async-start | bytes 2097152 | tf_op jit(solution)/shard_map/all_to_all | solution.py:406
  133.8 6.2 %col_attend.1 = (bf16[16,8,512]{2,1,0:T(8,128)(2,1)}, bf16[16,8,512]{2,1,0:T(8,128)(2,1)}, bf16[16,8,512]{2,1,0:T(8,128)(2,1)}, bf16[16,8,512]{2,1,0:T(8,128)(2,...) custom-call(s32[1]{0:T(128)} %bitcast.me_ref, ...), custom_call_target="tpu_custom_call" | custom-call | tf_op jit(solution)/shard_map/col_attend/pallas_call | solution.py:256
  142.9 3.7 %collective-permute-done.8.rest_2_ = bf16[16,8,512]{2,1,0:T(8,128)(2,1)S(1)} collective-permute-done((bf16[16,8,512]{2,1,0:T(8,128)(2,1)}, bf16[16,8,512]{2,1,0:T(8,128)(2,1)S(1)}, u32[]{:S(2)}, u32[]{:S(2)}) %collective-permute-start.8) | collective-permute-done | bytes 131104 | tf_op jit(solution)/shard_map/ppermute | solution.py:377
  148.9 4.3 %collective-permute-done.9.rest_3_ = bf16[16,8,512]{2,1,0:T(8,128)(2,1)S(1)} collective-permute-done((bf16[16,8,512]{2,1,0:T(8,128)(2,1)}, bf16[16,8,512]{2,1,0:T(8,128)(2,1)S(1)}, u32[]{:S(2)}, u32[]{:S(2)}) %collective-permute-start.9) | collective-permute-done | bytes 131104 | tf_op jit(solution)/shard_map/ppermute | solution.py:377
  155.9 3.7 %collective-permute-done.10.rest_4_ = bf16[16,8,512]{2,1,0:T(8,128)(2,1)S(1)} collective-permute-done((bf16[16,8,512]{2,1,0:T(8,128)(2,1)}, bf16[16,8,512]{2,1,0:T(8,128)(2,1)S(1)}, u32[]{:S(2)}, u32[]{:S(2)}) %collective-permute-start.10) | collective-permute-done | bytes 131104 | tf_op jit(solution)/shard_map/ppermute | solution.py:377
  159.6 3.8 %collective-permute-start.11 = (bf16[16,8,512]{2,1,0:T(8,128)(2,1)}, bf16[16,8,512]{2,1,0:T(8,128)(2,1)S(1)}, u32[]{:S(2)}, u32[]{:S(2)}) collective-permute-start(bf16[16,8,512]{2,1,0:T(8,128)(2,1)} %get-tuple-element.36), channel_id=1, source_target_pairs={{0,80},{16,64},{32,112},{48,96},{64,16},{80,0},{96,48},{112,32},{1... | collective-permute-start | bytes 393224 | tf_op jit(solution)/shard_map/ppermute | solution.py:377
  163.4 4.6 %collective-permute-done.11.rest_5_ = bf16[16,8,512]{2,1,0:T(8,128)(2,1)S(1)} collective-permute-done((bf16[16,8,512]{2,1,0:T(8,128)(2,1)}, bf16[16,8,512]{2,1,0:T(8,128)(2,1)S(1)}, u32[]{:S(2)}, u32[]{:S(2)}) %collective-permute-start.11) | collective-permute-done | bytes 131104 | tf_op jit(solution)/shard_map/ppermute | solution.py:377
  168.0 6.1 %collective-permute-done.12.rest_6_ = bf16[16,8,512]{2,1,0:T(8,128)(2,1)S(1)} collective-permute-done((bf16[16,8,512]{2,1,0:T(8,128)(2,1)}, bf16[16,8,512]{2,1,0:T(8,128)(2,1)S(1)}, u32[]{:S(2)}, u32[]{:S(2)}) %collective-permute-start.12) | collective-permute-done | bytes 131104 | tf_op jit(solution)/shard_map/ppermute | solution.py:377
  176.2 4.9 %collective-permute-done.13.rest_7_ = bf16[16,8,512]{2,1,0:T(8,128)(2,1)S(1)} collective-permute-done((bf16[16,8,512]{2,1,0:T(8,128)(2,1)}, bf16[16,8,512]{2,1,0:T(8,128)(2,1)S(1)}, u32[]{:S(2)}, u32[]{:S(2)}) %collective-permute-start.13) | collective-permute-done | bytes 131104 | tf_op jit(solution)/shard_map/ppermute | solution.py:377
  182.0 9.5 %project_first.1 = (bf16[1024,4096]{1,0:T(8,128)(2,1)}, bf16[16,64,1024]{2,1,0:T(8,128)(2,1)}) custom-call(s32[2]{0:T(128)} %pad_add_fusion.me_ref, bf16[16,64,512]{2,1,0:T(8,128)(2,1)} %copy-done.2, bf16[16,8,512]{2,1,0:T(8,128)(2,1)} %get-tuple-element.31.rest_0_, bf16[16,8,512]{2,1,0:T(8,128)(2,1)} %copy-done.3, bf16[16,8,512]{2,1,0:T(8,128)(2,1)} %copy-done.4, ...), custom_call_target="tpu_custom_call" | custom-call | tf_op jit(solution)/shard_map/project_first/pallas_call | solution.py:328
  191.6 9.4 %project_second.1 = bf16[1024,4096]{1,0:T(8,128)(2,1)} custom-call(s32[2]{0:T(128)} %pad_add_fusion.me_ref, bf16[16,64,1024]{2,1,0:T(8,128)(2,1)} %get-tuple-element.39.heads, bf16[4,4,32,1024]{3,2,1,0:T(8,128)(2,1)} %collective-permute-done.23.rest_0_, bf16[4,4,32,1024]{3,2,1,0:T(8,128)(2,1)} %collective-permute-done.24.rest_1_, ...), custom_call_target="tpu_custom_call", output_to_operand_aliasing={{}: (6, {})} | custom-call | tf_op jit(solution)/shard_map/project_second/pallas_call | solution.py:352
  (75 shorter events, 46.4 us)
Async XLA Ops:
  4.2 113.0 %all-to-all-start = ((bf16[16,64,1536]{2,1,0:T(8,128)(2,1)}), bf16[16,64,1536]{2,1,0:T(8,128)(2,1)S(1)}, u32[]{:S(2)}, u32[]{:S(2)}) async-start(bf16[16,64,1536]{2,1,0:T(8,128)(2,1)} %row_pack.1), calls=%async_computation | async-start | bytes 6291456 | tf_op jit(solution)/shard_map/all_to_all | solution.py:398
  21.5 30.3 %collective-permute-start.18 = (bf16[4,32,1024]{2,1,0:T(8,128)(2,1)}, bf16[4,32,1024]{2,1,0:T(8,128)(2,1)}, u32[]{:S(2)}, u32[]{:S(2)}) collective-permute-start(bf16[4,32,1024]{2,1,0:T(8,128)(2,1)} %get-tuple-element.42), channel_id=1, source_target_pairs={{0,2},{1,3},{2,0},{3,1},{4,6},{5,7},{6,4},{7,5},{8,10},{9,11},{10,... | collective-permute-start | bytes 786440 | tf_op jit(solution)/shard_map/ppermute | solution.py:371
  24.4 35.6 %collective-permute-start.17 = (bf16[4,32,1024]{2,1,0:T(8,128)(2,1)}, bf16[4,32,1024]{2,1,0:T(8,128)(2,1)}, u32[]{:S(2)}, u32[]{:S(2)}) collective-permute-start(bf16[4,32,1024]{2,1,0:T(8,128)(2,1)} %get-tuple-element.42), channel_id=1, source_target_pairs={{0,1},{1,0},{2,3},{3,2},{4,5},{5,4},{6,7},{7,6},{8,9},{9,8},{10,11... | collective-permute-start | bytes 786440 | tf_op jit(solution)/shard_map/ppermute | solution.py:371
  24.7 36.7 %collective-permute-start.19 = (bf16[4,32,1024]{2,1,0:T(8,128)(2,1)}, bf16[4,32,1024]{2,1,0:T(8,128)(2,1)}, u32[]{:S(2)}, u32[]{:S(2)}) collective-permute-start(bf16[4,32,1024]{2,1,0:T(8,128)(2,1)} %get-tuple-element.42), channel_id=1, source_target_pairs={{0,3},{1,2},{2,1},{3,0},{4,7},{5,6},{6,5},{7,4},{8,11},{9,10},{10,... | collective-permute-start | bytes 786440 | tf_op jit(solution)/shard_map/ppermute | solution.py:371
  32.1 38.1 %collective-permute-start = (bf16[8,16,1536]{2,1,0:T(8,128)(2,1)}, bf16[8,16,1536]{2,1,0:T(8,128)(2,1)}, u32[]{:S(2)}, u32[]{:S(2)}) collective-permute-start(bf16[8,16,1536]{2,1,0:T(8,128)(2,1)} %get-tuple-element.24), channel_id=1, source_target_pairs={{0,16},{16,0},{32,48},{48,32},{64,80},{80,64},{96,112},{112,96},{1... | collective-permute-start | bytes 1179656 | tf_op jit(solution)/shard_map/ppermute | solution.py:377
  35.4 38.3 %collective-permute-start.1 = (bf16[8,16,1536]{2,1,0:T(8,128)(2,1)}, bf16[8,16,1536]{2,1,0:T(8,128)(2,1)}, u32[]{:S(2)}, u32[]{:S(2)}) collective-permute-start(bf16[8,16,1536]{2,1,0:T(8,128)(2,1)} %get-tuple-element.25), channel_id=1, source_target_pairs={{0,32},{16,48},{32,0},{48,16},{64,96},{80,112},{96,64},{112,80},{1... | collective-permute-start | bytes 1179656 | tf_op jit(solution)/shard_map/ppermute | solution.py:377
  63.6 49.0 %collective-permute-start.22 = (bf16[4,4,32,1024]{3,2,1,0:T(8,128)(2,1)}, bf16[4,4,32,1024]{3,2,1,0:T(8,128)(2,1)}, u32[]{:S(2)}, u32[]{:S(2)}) collective-permute-start(bf16[4,4,32,1024]{3,2,1,0:T(8,128)(2,1)} %pad_maximum_fusion.rest_8_), channel_id=1, source_target_pairs={{0,12},{1,13},{2,14},{3,15},{4,8},{5,9},{6,10},{7,11},{8,4},{9,5},... | collective-permute-start | bytes 3145736 | tf_op jit(solution)/shard_map/ppermute | solution.py:371
  67.5 46.9 %collective-permute-start.21 = (bf16[4,4,32,1024]{3,2,1,0:T(8,128)(2,1)}, bf16[4,4,32,1024]{3,2,1,0:T(8,128)(2,1)}, u32[]{:S(2)}, u32[]{:S(2)}) collective-permute-start(bf16[4,4,32,1024]{3,2,1,0:T(8,128)(2,1)} %pad_maximum_fusion.rest_8_), channel_id=1, source_target_pairs={{0,8},{1,9},{2,10},{3,11},{4,12},{5,13},{6,14},{7,15},{8,0},{9,1},... | collective-permute-start | bytes 3145736 | tf_op jit(solution)/shard_map/ppermute | solution.py:371
  70.2 44.3 %collective-permute-start.20 = (bf16[4,4,32,1024]{3,2,1,0:T(8,128)(2,1)}, bf16[4,4,32,1024]{3,2,1,0:T(8,128)(2,1)}, u32[]{:S(2)}, u32[]{:S(2)}) collective-permute-start(bf16[4,4,32,1024]{3,2,1,0:T(8,128)(2,1)} %pad_maximum_fusion.rest_8_), channel_id=1, source_target_pairs={{0,4},{1,5},{2,6},{3,7},{4,0},{5,1},{6,2},{7,3},{8,12},{9,13},{10,... | collective-permute-start | bytes 3145736 | tf_op jit(solution)/shard_map/ppermute | solution.py:371
  70.2 13.8 %collective-permute-start.2 = (bf16[8,16,1536]{2,1,0:T(8,128)(2,1)}, bf16[8,16,1536]{2,1,0:T(8,128)(2,1)}, u32[]{:S(2)}, u32[]{:S(2)}) collective-permute-start(bf16[8,16,1536]{2,1,0:T(8,128)(2,1)} %get-tuple-element.26), channel_id=1, source_target_pairs={{0,48},{16,32},{32,16},{48,0},{64,112},{80,96},{96,80},{112,64},{1... | collective-permute-start | bytes 1179656 | tf_op jit(solution)/shard_map/ppermute | solution.py:377
  73.7 21.0 %collective-permute-start.3 = (bf16[8,16,1536]{2,1,0:T(8,128)(2,1)}, bf16[8,16,1536]{2,1,0:T(8,128)(2,1)}, u32[]{:S(2)}, u32[]{:S(2)}) collective-permute-start(bf16[8,16,1536]{2,1,0:T(8,128)(2,1)} %get-tuple-element.27), channel_id=1, source_target_pairs={{0,64},{16,80},{32,96},{48,112},{64,0},{80,16},{96,32},{112,48},{1... | collective-permute-start | bytes 1179656 | tf_op jit(solution)/shard_map/ppermute | solution.py:377
  84.0 17.8 %collective-permute-start.4 = (bf16[8,16,1536]{2,1,0:T(8,128)(2,1)}, bf16[8,16,1536]{2,1,0:T(8,128)(2,1)}, u32[]{:S(2)}, u32[]{:S(2)}) collective-permute-start(bf16[8,16,1536]{2,1,0:T(8,128)(2,1)} %get-tuple-element.28), channel_id=1, source_target_pairs={{0,80},{16,64},{32,112},{48,96},{64,16},{80,0},{96,48},{112,32},{1... | collective-permute-start | bytes 1179656 | tf_op jit(solution)/shard_map/ppermute | solution.py:377
  94.8 16.2 %collective-permute-start.5 = (bf16[8,16,1536]{2,1,0:T(8,128)(2,1)}, bf16[8,16,1536]{2,1,0:T(8,128)(2,1)}, u32[]{:S(2)}, u32[]{:S(2)}) collective-permute-start(bf16[8,16,1536]{2,1,0:T(8,128)(2,1)} %get-tuple-element.29), channel_id=1, source_target_pairs={{0,96},{16,112},{32,64},{48,80},{64,32},{80,48},{96,0},{112,16},{1... | collective-permute-start | bytes 1179656 | tf_op jit(solution)/shard_map/ppermute | solution.py:377
  101.8 32.0 %collective-permute-start.6 = (bf16[8,16,1536]{2,1,0:T(8,128)(2,1)}, bf16[8,16,1536]{2,1,0:T(8,128)(2,1)}, u32[]{:S(2)}, u32[]{:S(2)}) collective-permute-start(bf16[8,16,1536]{2,1,0:T(8,128)(2,1)} %get-tuple-element.30), channel_id=1, source_target_pairs={{0,112},{16,96},{32,80},{48,64},{64,48},{80,32},{96,16},{112,0},{1... | collective-permute-start | bytes 1179656 | tf_op jit(solution)/shard_map/ppermute | solution.py:377
  111.0 80.6 %collective-permute-start.23 = (bf16[4,4,32,1024]{3,2,1,0:T(8,128)(2,1)}, bf16[4,4,32,1024]{3,2,1,0:T(8,128)(2,1)}, u32[]{:S(2)}, u32[]{:S(2)}) collective-permute-start(bf16[4,4,32,1024]{3,2,1,0:T(8,128)(2,1)} %pad_maximum_fusion.rest_8_), channel_id=1, source_target_pairs={{0,16},{16,0},{32,48},{48,32},{64,80},{80,64},{96,112},{112,96},{1... | collective-permute-start | bytes 3145736 | tf_op jit(solution)/shard_map/ppermute | solution.py:371
  112.6 78.9 %collective-permute-start.26 = (bf16[4,4,32,1024]{3,2,1,0:T(8,128)(2,1)}, bf16[4,4,32,1024]{3,2,1,0:T(8,128)(2,1)}, u32[]{:S(2)}, u32[]{:S(2)}) collective-permute-start(bf16[4,4,32,1024]{3,2,1,0:T(8,128)(2,1)} %collective-permute-done.22.rest_11_), channel_id=1, source_target_pairs={{0,16},{16,0},{32,48},{48,32},{64,80},{80,64},{96,112},{112,96},{1... | collective-permute-start | bytes 3145736 | tf_op jit(solution)/shard_map/ppermute | solution.py:371
  114.4 77.1 %collective-permute-start.25 = (bf16[4,4,32,1024]{3,2,1,0:T(8,128)(2,1)}, bf16[4,4,32,1024]{3,2,1,0:T(8,128)(2,1)}, u32[]{:S(2)}, u32[]{:S(2)}) collective-permute-start(bf16[4,4,32,1024]{3,2,1,0:T(8,128)(2,1)} %collective-permute-done.21.rest_10_), channel_id=1, source_target_pairs={{0,16},{16,0},{32,48},{48,32},{64,80},{80,64},{96,112},{112,96},{1... | collective-permute-start | bytes 3145736 | tf_op jit(solution)/shard_map/ppermute | solution.py:371
  114.5 77.1 %collective-permute-start.24 = (bf16[4,4,32,1024]{3,2,1,0:T(8,128)(2,1)}, bf16[4,4,32,1024]{3,2,1,0:T(8,128)(2,1)}, u32[]{:S(2)}, u32[]{:S(2)}) collective-permute-start(bf16[4,4,32,1024]{3,2,1,0:T(8,128)(2,1)} %collective-permute-done.20.rest_9_), channel_id=1, source_target_pairs={{0,16},{16,0},{32,48},{48,32},{64,80},{80,64},{96,112},{112,96},{1... | collective-permute-start | bytes 3145736 | tf_op jit(solution)/shard_map/ppermute | solution.py:371
  128.5 52.5 %all-to-all-start.1 = ((bf16[16,64,512]{2,1,0:T(8,128)(2,1)}), bf16[16,64,512]{2,1,0:T(8,128)(2,1)S(1)}, u32[]{:S(2)}, u32[]{:S(2)}) async-start(bf16[16,64,512]{2,1,0:T(8,128)(2,1)} %bitcast.17), calls=%async_computation.1 | async-start | bytes 2097152 | tf_op jit(solution)/shard_map/all_to_all | solution.py:406
  146.6 6.6 %collective-permute-start.9 = (bf16[16,8,512]{2,1,0:T(8,128)(2,1)}, bf16[16,8,512]{2,1,0:T(8,128)(2,1)S(1)}, u32[]{:S(2)}, u32[]{:S(2)}) collective-permute-start(bf16[16,8,512]{2,1,0:T(8,128)(2,1)} %get-tuple-element.34), channel_id=1, source_target_pairs={{0,48},{16,32},{32,16},{48,0},{64,112},{80,96},{96,80},{112,64},{1... | collective-permute-start | bytes 393224 | tf_op jit(solution)/shard_map/ppermute | solution.py:377
  153.2 6.4 %collective-permute-start.10 = (bf16[16,8,512]{2,1,0:T(8,128)(2,1)}, bf16[16,8,512]{2,1,0:T(8,128)(2,1)S(1)}, u32[]{:S(2)}, u32[]{:S(2)}) collective-permute-start(bf16[16,8,512]{2,1,0:T(8,128)(2,1)} %get-tuple-element.35), channel_id=1, source_target_pairs={{0,64},{16,80},{32,96},{48,112},{64,0},{80,16},{96,32},{112,48},{1... | collective-permute-start | bytes 393224 | tf_op jit(solution)/shard_map/ppermute | solution.py:377
  159.6 8.4 %collective-permute-start.11 = (bf16[16,8,512]{2,1,0:T(8,128)(2,1)}, bf16[16,8,512]{2,1,0:T(8,128)(2,1)S(1)}, u32[]{:S(2)}, u32[]{:S(2)}) collective-permute-start(bf16[16,8,512]{2,1,0:T(8,128)(2,1)} %get-tuple-element.36), channel_id=1, source_target_pairs={{0,80},{16,64},{32,112},{48,96},{64,16},{80,0},{96,48},{112,32},{1... | collective-permute-start | bytes 393224 | tf_op jit(solution)/shard_map/ppermute | solution.py:377
  168.0 6.1 %collective-permute-start.12 = (bf16[16,8,512]{2,1,0:T(8,128)(2,1)}, bf16[16,8,512]{2,1,0:T(8,128)(2,1)S(1)}, u32[]{:S(2)}, u32[]{:S(2)}) collective-permute-start(bf16[16,8,512]{2,1,0:T(8,128)(2,1)} %get-tuple-element.37), channel_id=1, source_target_pairs={{0,96},{16,112},{32,64},{48,80},{64,32},{80,48},{96,0},{112,16},{1... | collective-permute-start | bytes 393224 | tf_op jit(solution)/shard_map/ppermute | solution.py:377
  174.1 6.9 %collective-permute-start.13 = (bf16[16,8,512]{2,1,0:T(8,128)(2,1)}, bf16[16,8,512]{2,1,0:T(8,128)(2,1)S(1)}, u32[]{:S(2)}, u32[]{:S(2)}) collective-permute-start(bf16[16,8,512]{2,1,0:T(8,128)(2,1)} %get-tuple-element.38), channel_id=1, source_target_pairs={{0,112},{16,96},{32,80},{48,64},{64,48},{80,32},{96,16},{112,0},{1... | collective-permute-start | bytes 393224 | tf_op jit(solution)/shard_map/ppermute | solution.py:377
  (18 other events, 383.3 us)

commit v3 on v2

--- a/solution.py
+++ b/solution.py
@@ -16,6 +16,10 @@
 NEG_FILL = -1e30
 UNROLL = 4
 EXP_SCALE = HD ** (-0.5) * math.log2(math.e)
+
+
+def in_place(x):
+    return pltpu.with_memory_space_constraint(x, pltpu.VMEM)
 
 
 def row_pack_kernel(q_ref, k_ref, v_ref, out_ref):
@@ -101,22 +105,25 @@
 def row_attend_kernel(pattern_ref, count_ref, x_ref, out_ref, *, chosen):
     width = HR * HD
     count = count_ref[0]
-    blocks = x_ref.shape[0] // BLK
+    per = x_ref.shape[1] // BLK
+    blocks = x_ref.shape[0] * per
     key_lane = lax.broadcasted_iota(jnp.int32, (1, chosen * BLK), 1)
     slot_of = key_lane // BLK
     in_block = key_lane - slot_of * BLK
     query_row = lax.broadcasted_iota(jnp.int32, (BLK, 1), 0)
     zero = jnp.zeros((BLK, HD), jnp.bfloat16)
 
+    def block(b, lanes):
+        at = pl.multiple_of(lax.rem(b, per) * BLK, BLK)
+        return x_ref[lax.div(b, per), pl.ds(at, BLK), lanes]
+
     def stage_scores(n):
-        at = pl.multiple_of(n * BLK, BLK)
-        q = x_ref[pl.ds(at, BLK), 0:width]
+        q = block(n, slice(0, width))
         keys = []
         limit = jnp.zeros((1, chosen * BLK), jnp.int32)
         for s in range(chosen):
             b = pattern_ref[n * chosen + s]
-            k_at = pl.multiple_of(b * BLK, BLK)
-            keys.append(x_ref[pl.ds(k_at, BLK), width : 2 * width])
+            keys.append(block(b, slice(width, 2 * width)))
             limit = jnp.where(slot_of == s, count - b * BLK, limit)
         keys = jnp.concatenate(keys, axis=0)
         live = in_block < limit
@@ -138,8 +145,7 @@
         at = pl.multiple_of(n * BLK, BLK)
         values = []
         for s in range(chosen):
-            k_at = pl.multiple_of(pattern_ref[n * chosen + s] * BLK, BLK)
-            values.append(x_ref[pl.ds(k_at, BLK), 2 * width : 3 * width])
+            values.append(block(pattern_ref[n * chosen + s], slice(2 * width, 3 * width)))
         values = jnp.concatenate(values, axis=0)
         query_live = (query_row + n * BLK) < count
         for pair in range(HR // 2):
@@ -172,7 +178,7 @@
 
 
 def row_attend(pattern, count, x):
-    cells = x.shape[0]
+    cells = x.shape[0] * x.shape[1]
     chosen = pattern.shape[-1]
     return pl.pallas_call(
         functools.partial(row_attend_kernel, chosen=chosen),
@@ -184,7 +190,7 @@
         ),
         out_shape=jax.ShapeDtypeStruct((cells, HR * HD), x.dtype),
         name="row_attend",
-    )(pattern.reshape(-1), count, x)
+    )(pattern.reshape(-1), count, in_place(x))
 
 
 def col_attend_kernel(me_ref, pattern_ref, count_ref, *rest, chosen, lines):
@@ -202,7 +208,7 @@
     query_row = lax.broadcasted_iota(jnp.int32, (cells, 1), 0)
     for u in range(lines):
         for s in range(peers):
-            line[u, pl.ds(pl.multiple_of((me ^ s) * span, span), span), :] = pieces[s][u]
+            line[u, pl.ds(pl.multiple_of((me ^ s) * span, span), span), :] = pieces[s][step * lines + u]
     jobs, scores = [], []
     for u in range(lines):
         j = step * lines + u
@@ -258,7 +264,7 @@
         grid_spec=pltpu.PrefetchScalarGridSpec(
             num_scalar_prefetch=3,
             grid=(own // lines,),
-            in_specs=[pl.BlockSpec((lines, span, wide), lambda j, *_: (j, 0, 0))] * peers,
+            in_specs=[pl.BlockSpec(memory_space=pltpu.VMEM)] * peers,
             out_specs=[pl.BlockSpec(result, lambda j, *_: (0, 0, 0))] * peers,
             scratch_shapes=[
                 pltpu.VMEM((lines, peers * span, wide), jnp.bfloat16),
@@ -267,33 +273,51 @@
         ),
         out_shape=[jax.ShapeDtypeStruct(result, jnp.bfloat16)] * peers,
         name="col_attend",
-    )(me, pattern.reshape(-1), count, *pieces)
-
-
-def project_block(plane, heads, weights, line, out_ref):
-    quarter = len(weights)
-    near, span, channels = weights[0].shape
-    for sx in range(quarter):
+    )(me, pattern.reshape(-1), count, *[in_place(p) for p in pieces])
+
+
+def weight_copies(place, weights, line, sem, turn, slot):
+    _, near, span, _ = weights[0].shape
+    plane = place[1]
+    copies = []
+    for sx, weight in enumerate(weights):
         for sz in range(near):
             at = ((plane // near ^ sx) * near + (lax.rem(plane, near) ^ sz)) * span
-            line[pl.ds(pl.multiple_of(at, span), span), :] = weights[sx][sz]
+            target = line.at[slot, pl.ds(pl.multiple_of(at, span), span), :]
+            copies.append(pltpu.make_async_copy(weight.at[turn, sz], target, sem.at[slot]))
+    return copies
+
+
+def project_block(place, heads, weights, line, sem, out_ref):
+    turn = pl.program_id(0)
+    slot = lax.rem(turn, 2)
+
+    @pl.when(turn + 1 < pl.num_programs(0))
+    def _():
+        for copy in weight_copies(place, weights, line, sem, turn + 1, 1 - slot):
+            copy.start()
+
+    for copy in weight_copies(place, weights, line, sem, turn, slot):
+        copy.wait()
     out_ref[...] = lax.dot_general(
-        heads[...].reshape(-1, channels),
-        line[...],
+        heads[...].reshape(-1, heads.shape[2]),
+        line[slot],
         (((1,), (1,)), ((), ())),
         preferred_element_type=jnp.float32,
     ).astype(jnp.bfloat16)
 
 
-def project_first_kernel(me_ref, row_ref, *rest, quarter):
-    pieces, weights = rest[: -3 - quarter], rest[-3 - quarter : -3]
-    out_ref, heads, line = rest[-3:]
+def project_first_kernel(place, row_ref, *rest, quarter):
+    pieces, weights = rest[: -4 - quarter], rest[-4 - quarter : -4]
+    out_ref, heads, line, sem = rest[-4:]
     width = HR * HD
     own = pieces[0].shape[1]
 
     @pl.when(pl.program_id(0) == 0)
     def _():
-        me = me_ref[0]
+        for copy in weight_copies(place, weights, line, sem, 0, 0):
+            copy.start()
+        me = place[0]
         odd = lax.rem(me, 2) == 1
         heads[:, :, 0:width] = row_ref[...]
         for s in range(0, len(pieces), 2):
@@ -303,67 +327,72 @@
             at = pl.multiple_of(((me ^ s) // 2) * 2 * own, 2 * own)
             heads[:, pl.ds(at, 2 * own), width:] = both.astype(jnp.bfloat16)
 
-    project_block(me_ref[1], heads, weights, line, out_ref)
-
-
-def project_second_kernel(me_ref, heads, *rest, quarter):
-    weights, (_, out_ref, line) = rest[:quarter], rest[quarter:]
-    project_block(me_ref[1], heads, weights, line, out_ref)
-
-
-def weight_spec(weight):
-    near, _, span, channels = weight.shape
-    return pl.BlockSpec((near, None, span, channels), lambda j, *_: (0, j, 0, 0))
+    project_block(place, heads, weights, line, sem, out_ref)
+
+
+def project_second_kernel(place, heads, *rest, quarter):
+    weights, (_, out_ref, line, sem) = rest[:quarter], rest[quarter:]
+
+    @pl.when(pl.program_id(0) == 0)
+    def _():
+        for copy in weight_copies(place, weights, line, sem, 0, 0):
+            copy.start()
+
+    project_block(place, heads, weights, line, sem, out_ref)
 
 
 def whole(a):
     return pl.BlockSpec(a.shape, lambda j, *_: (0,) * a.ndim)
 
 
-def project_first(me, row_out, pieces, weights, outs):
+def project_first(place, row_out, pieces, weights, outs):
     span, cells, _ = row_out.shape
-    near, turns, part, channels = weights[0].shape
+    turns, near, part, channels = weights[0].shape
     tile = len(weights) * near * part
-    held = pl.BlockSpec(memory_space=pltpu.VMEM)
     return pl.pallas_call(
         functools.partial(project_first_kernel, quarter=len(weights)),
         grid_spec=pltpu.PrefetchScalarGridSpec(
             num_scalar_prefetch=1,
             grid=(turns,),
-            in_specs=[held] * (1 + len(pieces)) + [weight_spec(w) for w in weights],
+            in_specs=[pl.BlockSpec(memory_space=pltpu.VMEM)] * (1 + len(pieces))
+            + [pl.BlockSpec(memory_space=pl.ANY)] * len(weights),
             out_specs=[
-                pl.BlockSpec((span * cells, tile), lambda j, me: (0, me[0] ^ (2 * j))),
+                pl.BlockSpec((span * cells, tile), lambda j, at: (0, at[0] ^ (2 * j))),
                 pl.BlockSpec((span, cells, channels), lambda j, *_: (0, 0, 0)),
             ],
-            scratch_shapes=[pltpu.VMEM((tile, channels), jnp.bfloat16)],
+            scratch_shapes=[
+                pltpu.VMEM((2, tile, channels), jnp.bfloat16),
+                pltpu.SemaphoreType.DMA((2,)),
+            ],
         ),
         out_shape=[
             jax.ShapeDtypeStruct((span * cells, outs), jnp.bfloat16),
             jax.ShapeDtypeStruct((span, cells, channels), jnp.bfloat16),
         ],
         name="project_first",
-    )(me, row_out, *pieces, *weights)
-
-
-def project_second(me, heads, weights, kept):
+    )(place, in_place(row_out), *[in_place(p) for p in pieces], *weights)
+
+
+def project_second(place, heads, weights, kept):
     span, cells, channels = heads.shape
-    near, turns, part, _ = weights[0].shape
+    turns, near, part, _ = weights[0].shape
     tile = len(weights) * near * part
     return pl.pallas_call(
         functools.partial(project_second_kernel, quarter=len(weights)),
         grid_spec=pltpu.PrefetchScalarGridSpec(
             num_scalar_prefetch=1,
             grid=(turns,),
-            in_specs=[whole(heads)]
-            + [weight_spec(w) for w in weights]
-            + [pl.BlockSpec(memory_space=pl.ANY)],
-            out_specs=pl.BlockSpec((span * cells, tile), lambda j, me: (0, me[0] ^ (2 * j + 1))),
-            scratch_shapes=[pltpu.VMEM((tile, channels), jnp.bfloat16)],
+            in_specs=[whole(heads)] + [pl.BlockSpec(memory_space=pl.ANY)] * (1 + len(weights)),
+            out_specs=pl.BlockSpec((span * cells, tile), lambda j, at: (0, at[0] ^ (2 * j + 1))),
+            scratch_shapes=[
+                pltpu.VMEM((2, tile, channels), jnp.bfloat16),
+                pltpu.SemaphoreType.DMA((2,)),
+            ],
         ),
         out_shape=jax.ShapeDtypeStruct(kept.shape, jnp.bfloat16),
         input_output_aliases={2 + len(weights): 0},
         name="project_second",
-    )(me, heads, *weights, kept)
+    )(place, heads, *weights, kept)
 
 
 def by_xor(x, axis, masks):
@@ -393,16 +422,16 @@
     place = jnp.stack([lax.axis_index("rows"), lax.axis_index("cols")]).astype(jnp.int32)
 
     shard = out_weight.T
-    along_y = [shard] + by_xor(shard, "rows", (2, 4, 6))
+    along_z = [shard] + by_xor(shard, "cols", (1, 2, 3))
     packed = row_pack(query_cells, key_cells, value_cells)
     lines = lax.all_to_all(packed, "cols", 0, 0, tiled=True)
-    held = jnp.stack(along_y)
-    along_z = [held] + by_xor(held, "cols", (1, 2, 3))
+    held = jnp.stack(along_z)
+    along_y = [held] + by_xor(held, "rows", (2, 4, 6))
     sent = col_pack(me, query_cells, key_cells, value_cells, peers)
     pieces = swap_pieces(sent)
-    held = jnp.stack(along_z)
+    held = jnp.stack(along_y)
     weights = [held] + by_xor(held, "cols", (4, 8, 12))
-    row_out = row_attend(pattern, count, lines.reshape(-1, lines.shape[-1]))
+    row_out = row_attend(pattern, count, lines)
     row_out = lax.all_to_all(row_out.reshape(row_span, col_span, -1), "cols", 0, 0, tiled=True)
     col_out = col_attend(me, col_pattern, col_count, pieces)
     col_out = swap_pieces(col_out)

time: 202 us -> 211 us (1.045)
  local copies, waits for them, and re-layouts: 4.95 us -> 13 us
  starting transfers between devices: 57 us -> 59.9 us
    unnamed x27 -> x33, local copies, waits for them, and re-layouts: 2.78 us -> 10.8 us
    ppermute x14, waiting for transfers between devices: 57.9 us -> 53.1 us  [swap_pieces(): lax.ppermute(pieces[s], 'rows', [(d, d ^ s) for d in range(peers)])]
    ppermute x13, waiting for transfers between devices: 31.6 us -> 36.1 us  [by_xor(): lax.ppermute(x, axis, [(d, d ^ s) for d in range(size)])]
  transfers between devices with their start and end apart: 29 -> 29, of which waited for: 18 -> 16; matrix products, arithmetic and copies ran while one was open for 3% -> 3% of each run, Pallas kernels for 16% -> 14%
where the time goes in v3:
time: 211 us; the launch traced here: 210 us
  waiting for transfers between devices  89.2 us (42%)
  starting transfers between devices  59.9 us (28%)
  Pallas kernels  44 us (21%)
  local copies, waits for them, and re-layouts  13 us (6%)
  other arithmetic  3.56 us (2%)
    ppermute x14, waiting for transfers between devices, swap_pieces(): lax.ppermute(pieces[s], 'rows', [(d, d ^ s) for d in range(peers)])  53.1 us
    ppermute x13, waiting for transfers between devices, by_xor(): lax.ppermute(x, axis, [(d, d ^ s) for d in range(size)])  36.1 us
    ppermute x14, starting transfers between devices, swap_pieces(): lax.ppermute(pieces[s], 'rows', [(d, d ^ s) for d in range(peers)])  27.6 us
    ppermute x13, starting transfers between devices, by_xor(): lax.ppermute(x, axis, [(d, d ^ s) for d in range(size)])  18.1 us
    unnamed x33, local copies, waits for them, and re-layouts  10.8 us
    pallas_call x1, Pallas kernels, project_second(): pl.pallas_call(functools.partial(project_second_kernel, quarter=len(weigh...  10 us
    pallas_call x1, Pallas kernels, project_first(): pl.pallas_call(functools.partial(project_first_kernel, quarter=len(weight...  9.69 us
    all_to_all x1, starting transfers between devices, body(): lines = lax.all_to_all(packed, 'cols', 0, 0, tiled=True)  8.55 us
  transfers between devices with their start and end apart: 29, of which 16 were waited for; matrix products, arithmetic and copies ran while one was open for 3% of the time, Pallas kernels for 14%

profile of v3, /device:TPU:1, one launch (start us, length us, event | category | flops | bytes accessed | tf_op | source)
XLA Modules:
  0.0 209.9 jit_solution(13167752511966685496)
XLA Ops:
  0.0 4.2 %row_pack.1 = bf16[16,64,1536]{2,1,0:T(8,128)(2,1)} custom-call(bf16[16,64,1024]{2,1,0:T(8,128)(2,1)} %q_ref.3, bf16[16,64,1024]{2,1,0:T(8,128)(2,1)} %k_ref.3, bf16[16,64,1024]{2,1,0:T(8,128)(2,1)} %v_ref.3), custom_call_target="tpu_custom_call" | custom-call | tf_op jit(solution)/shard_map/row_pack/pallas_call | solution.py:37
  4.2 8.5 %all-to-all-start = ((bf16[16,64,1536]{2,1,0:T(8,128)(2,1)}), bf16[16,64,1536]{2,1,0:T(8,128)(2,1)S(1)}, u32[]{:S(2)}, u32[]{:S(2)}) async-start(bf16[16,64,1536]{2,1,0:T(8,128)(2,1)} %row_pack.1), calls=%async_computation | async-start | bytes 6291456 | tf_op jit(solution)/shard_map/all_to_all | solution.py:427
  16.6 20.9 %collective-permute-done.15 = bf16[32,1024]{1,0:T(8,128)(2,1)S(1)} collective-permute-done((bf16[32,1024]{1,0:T(8,128)(2,1)S(1)}, bf16[32,1024]{1,0:T(8,128)(2,1)S(1)}, u32[]{:S(2)}, u32[]{:S(2)}) %collective-permute-start.15) | collective-permute-done | bytes 65568 | tf_op jit(solution)/shard_map/ppermute | solution.py:400
  37.5 5.6 %collective-permute-done.14 = bf16[32,1024]{1,0:T(8,128)(2,1)S(1)} collective-permute-done((bf16[32,1024]{1,0:T(8,128)(2,1)S(1)}, bf16[32,1024]{1,0:T(8,128)(2,1)S(1)}, u32[]{:S(2)}, u32[]{:S(2)}) %collective-permute-start.14) | collective-permute-done | bytes 65568 | tf_op jit(solution)/shard_map/ppermute | solution.py:400
  43.1 6.0 %collective-permute-done.16 = bf16[32,1024]{1,0:T(8,128)(2,1)S(1)} collective-permute-done((bf16[32,1024]{1,0:T(8,128)(2,1)S(1)}, bf16[32,1024]{1,0:T(8,128)(2,1)S(1)}, u32[]{:S(2)}, u32[]{:S(2)}) %collective-permute-start.16) | collective-permute-done | bytes 65568 | tf_op jit(solution)/shard_map/ppermute | solution.py:400
  53.5 6.8 %col_pack.1 = (bf16[8,16,1536]{2,1,0:T(8,128)(2,1)}, bf16[8,16,1536]{2,1,0:T(8,128)(2,1)}, bf16[8,16,1536]{2,1,0:T(8,128)(2,1)}, bf16[8,16,1536]{2,1,0:T(8,128)(...) custom-call(s32[1]{0:T(128)} %bitcast.me_ref, ...), custom_call_target="tpu_custom_call" | custom-call | tf_op jit(solution)/shard_map/col_pack/pallas_call | solution.py:87
  66.9 7.4 %collective-permute-start.22 = (bf16[4,4,32,1024]{3,2,1,0:T(8,128)(2,1)}, bf16[4,4,32,1024]{3,2,1,0:T(8,128)(2,1)}, u32[]{:S(2)}, u32[]{:S(2)}) collective-permute-start(bf16[4,4,32,1024]{3,2,1,0:T(8,128)(2,1)} %pad_maximum_fusion.rest_8_), channel_id=1, source_target_pairs={{0,12},{1,13},{2,14},{3,15},{4,8},{5,9},{6,10},{7,11},{8,4},{9,5},... | collective-permute-start | bytes 3145736 | tf_op jit(solution)/shard_map/ppermute | solution.py:400
  82.2 7.0 %collective-permute-done.2.rest_3_ = bf16[8,16,1536]{2,1,0:T(8,128)(2,1)S(1)} collective-permute-done((bf16[8,16,1536]{2,1,0:T(8,128)(2,1)}, bf16[8,16,1536]{2,1,0:T(8,128)(2,1)S(1)}, u32[]{:S(2)}, u32[]{:S(2)}) %collective-permute-start.2) | collective-permute-done | bytes 393248 | tf_op jit(solution)/shard_map/ppermute | solution.py:406
  92.8 7.0 %collective-permute-done.3.rest_4_ = bf16[8,16,1536]{2,1,0:T(8,128)(2,1)S(1)} collective-permute-done((bf16[8,16,1536]{2,1,0:T(8,128)(2,1)}, bf16[8,16,1536]{2,1,0:T(8,128)(2,1)S(1)}, u32[]{:S(2)}, u32[]{:S(2)}) %collective-permute-start.3) | collective-permute-done | bytes 393248 | tf_op jit(solution)/shard_map/ppermute | solution.py:406
  100.9 6.0 %collective-permute-done.4.rest_5_ = bf16[8,16,1536]{2,1,0:T(8,128)(2,1)S(1)} collective-permute-done((bf16[8,16,1536]{2,1,0:T(8,128)(2,1)}, bf16[8,16,1536]{2,1,0:T(8,128)(2,1)S(1)}, u32[]{:S(2)}, u32[]{:S(2)}) %collective-permute-start.4) | collective-permute-done | bytes 393248 | tf_op jit(solution)/shard_map/ppermute | solution.py:406
  110.1 6.0 %collective-permute-done.5.rest_6_ = bf16[8,16,1536]{2,1,0:T(8,128)(2,1)} collective-permute-done((bf16[8,16,1536]{2,1,0:T(8,128)(2,1)}, bf16[8,16,1536]{2,1,0:T(8,128)(2,1)}, u32[]{:S(2)}, u32[]{:S(2)}) %collective-permute-start.5) | collective-permute-done | bytes 393248 | tf_op jit(solution)/shard_map/ppermute | solution.py:406
  122.6 7.7 %row_attend.1 = bf16[1024,512]{1,0:T(8,128)(2,1)} custom-call(s32[192]{0:T(256)} %reshape.13.pattern_ref, s32[1]{0:T(128)} %dynamic_slice.7.count_ref, bf16[16,64,1536]{2,1,0:T(8,128)(2,1)S(1)} %all-to-all-done.x_ref), custom_call_target="tpu_custom_call" | custom-call | tf_op jit(solution)/shard_map/row_attend/pallas_call | solution.py:183
  130.3 5.7 %all-to-all-start.1 = ((bf16[16,64,512]{2,1,0:T(8,128)(2,1)}), bf16[16,64,512]{2,1,0:T(8,128)(2,1)}, u32[]{:S(2)}, u32[]{:S(2)}) async-start(bf16[16,64,512]{2,1,0:T(8,128)(2,1)} %bitcast.15), calls=%async_computation.1 | async-start | bytes 2097152 | tf_op jit(solution)/shard_map/all_to_all | solution.py:435
  142.9 5.6 %col_attend.1 = (bf16[16,8,512]{2,1,0:T(8,128)(2,1)}, bf16[16,8,512]{2,1,0:T(8,128)(2,1)}, bf16[16,8,512]{2,1,0:T(8,128)(2,1)}, bf16[16,8,512]{2,1,0:T(8,128)(2,...) custom-call(s32[1]{0:T(128)} %bitcast.me_ref, ...), custom_call_target="tpu_custom_call" | custom-call | tf_op jit(solution)/shard_map/col_attend/pallas_call | solution.py:262
  150.9 4.0 %collective-permute-done.8.rest_2_ = bf16[16,8,512]{2,1,0:T(8,128)(2,1)S(1)} collective-permute-done((bf16[16,8,512]{2,1,0:T(8,128)(2,1)}, bf16[16,8,512]{2,1,0:T(8,128)(2,1)S(1)}, u32[]{:S(2)}, u32[]{:S(2)}) %collective-permute-start.8) | collective-permute-done | bytes 131104 | tf_op jit(solution)/shard_map/ppermute | solution.py:406
  156.9 4.3 %collective-permute-done.9.rest_3_ = bf16[16,8,512]{2,1,0:T(8,128)(2,1)S(1)} collective-permute-done((bf16[16,8,512]{2,1,0:T(8,128)(2,1)}, bf16[16,8,512]{2,1,0:T(8,128)(2,1)S(1)}, u32[]{:S(2)}, u32[]{:S(2)}) %collective-permute-start.9) | collective-permute-done | bytes 131104 | tf_op jit(solution)/shard_map/ppermute | solution.py:406
  161.3 3.3 %collective-permute-start.10 = (bf16[16,8,512]{2,1,0:T(8,128)(2,1)}, bf16[16,8,512]{2,1,0:T(8,128)(2,1)S(1)}, u32[]{:S(2)}, u32[]{:S(2)}) collective-permute-start(bf16[16,8,512]{2,1,0:T(8,128)(2,1)} %get-tuple-element.35), channel_id=1, source_target_pairs={{0,64},{16,80},{32,96},{48,112},{64,0},{80,16},{96,32},{112,48},{1... | collective-permute-start | bytes 393224 | tf_op jit(solution)/shard_map/ppermute | solution.py:406
  164.6 3.5 %collective-permute-done.10.rest_4_ = bf16[16,8,512]{2,1,0:T(8,128)(2,1)S(1)} collective-permute-done((bf16[16,8,512]{2,1,0:T(8,128)(2,1)}, bf16[16,8,512]{2,1,0:T(8,128)(2,1)S(1)}, u32[]{:S(2)}, u32[]{:S(2)}) %collective-permute-start.10) | collective-permute-done | bytes 131104 | tf_op jit(solution)/shard_map/ppermute | solution.py:406
  168.1 4.0 %collective-permute-start.11 = (bf16[16,8,512]{2,1,0:T(8,128)(2,1)}, bf16[16,8,512]{2,1,0:T(8,128)(2,1)S(1)}, u32[]{:S(2)}, u32[]{:S(2)}) collective-permute-start(bf16[16,8,512]{2,1,0:T(8,128)(2,1)} %get-tuple-element.36), channel_id=1, source_target_pairs={{0,80},{16,64},{32,112},{48,96},{64,16},{80,0},{96,48},{112,32},{1... | collective-permute-start | bytes 393224 | tf_op jit(solution)/shard_map/ppermute | solution.py:406
  172.1 4.0 %collective-permute-done.11.rest_5_ = bf16[16,8,512]{2,1,0:T(8,128)(2,1)S(1)} collective-permute-done((bf16[16,8,512]{2,1,0:T(8,128)(2,1)}, bf16[16,8,512]{2,1,0:T(8,128)(2,1)S(1)}, u32[]{:S(2)}, u32[]{:S(2)}) %collective-permute-start.11) | collective-permute-done | bytes 131104 | tf_op jit(solution)/shard_map/ppermute | solution.py:406
  176.5 5.6 %collective-permute-done.12.rest_6_ = bf16[16,8,512]{2,1,0:T(8,128)(2,1)S(1)} collective-permute-done((bf16[16,8,512]{2,1,0:T(8,128)(2,1)}, bf16[16,8,512]{2,1,0:T(8,128)(2,1)S(1)}, u32[]{:S(2)}, u32[]{:S(2)}) %collective-permute-start.12) | collective-permute-done | bytes 131104 | tf_op jit(solution)/shard_map/ppermute | solution.py:406
  184.8 4.3 %collective-permute-done.13.rest_7_ = bf16[16,8,512]{2,1,0:T(8,128)(2,1)S(1)} collective-permute-done((bf16[16,8,512]{2,1,0:T(8,128)(2,1)}, bf16[16,8,512]{2,1,0:T(8,128)(2,1)S(1)}, u32[]{:S(2)}, u32[]{:S(2)}) %collective-permute-start.13) | collective-permute-done | bytes 131104 | tf_op jit(solution)/shard_map/ppermute | solution.py:406
  190.0 9.7 %project_first.1 = (bf16[1024,4096]{1,0:T(8,128)(2,1)}, bf16[16,64,1024]{2,1,0:T(8,128)(2,1)}) custom-call(s32[2]{0:T(128)} %pad_add_fusion.place, bf16[16,64,512]{2,1,0:T(8,128)(2,1)} %all-to-all-done.1.row_ref, bf16[16,8,512]{2,1,0:T(8,128)(2,1)S(1)} %copy-done.12, bf16[16,8,512]{2,1,0:T(8,128)(2,1)S(1)} %collective-permute-done.7.rest_1_, ...), custom_call_target="tpu_custom_call" | custom-call | tf_op jit(solution)/shard_map/project_first/pallas_call | solution.py:352
  199.8 10.0 %project_second.1 = bf16[1024,4096]{1,0:T(8,128)(2,1)} custom-call(s32[2]{0:T(128)} %pad_add_fusion.place, bf16[16,64,1024]{2,1,0:T(8,128)(2,1)} %get-tuple-element.39.heads, bf16[4,4,32,1024]{3,2,1,0:T(8,128)(2,1)} %collective-permute-done.23.rest_0_, bf16[4,4,32,1024]{3,2,1,0:T(8,128)(2,1)} %collective-permute-done.24.rest_1_, ...), custom_call_target="tpu_custom_call", output_to_operand_aliasing={{}: (6, {})} | custom-call | tf_op jit(solution)/shard_map/project_second/pallas_call | solution.py:380
  (81 shorter events, 52.5 us)
Async XLA Ops:
  4.2 118.4 %all-to-all-start = ((bf16[16,64,1536]{2,1,0:T(8,128)(2,1)}), bf16[16,64,1536]{2,1,0:T(8,128)(2,1)S(1)}, u32[]{:S(2)}, u32[]{:S(2)}) async-start(bf16[16,64,1536]{2,1,0:T(8,128)(2,1)} %row_pack.1), calls=%async_computation | async-start | bytes 6291456 | tf_op jit(solution)/shard_map/all_to_all | solution.py:427
  12.7 24.7 %collective-permute-start.15 = (bf16[32,1024]{1,0:T(8,128)(2,1)S(1)}, bf16[32,1024]{1,0:T(8,128)(2,1)S(1)}, u32[]{:S(2)}, u32[]{:S(2)}) collective-permute-start(bf16[32,1024]{1,0:T(8,128)(2,1)S(1)} %bitcast.16), channel_id=1, source_target_pairs={{0,2},{1,3},{2,0},{3,1},{4,6},{5,7},{6,4},{7,5},{8,10},{9,11},{10,... | collective-permute-start | bytes 196616 | tf_op jit(solution)/shard_map/ppermute | solution.py:400
  15.7 27.4 %collective-permute-start.14 = (bf16[32,1024]{1,0:T(8,128)(2,1)S(1)}, bf16[32,1024]{1,0:T(8,128)(2,1)S(1)}, u32[]{:S(2)}, u32[]{:S(2)}) collective-permute-start(bf16[32,1024]{1,0:T(8,128)(2,1)S(1)} %bitcast.17), channel_id=1, source_target_pairs={{0,1},{1,0},{2,3},{3,2},{4,5},{5,4},{6,7},{7,6},{8,9},{9,8},{10,11... | collective-permute-start | bytes 196616 | tf_op jit(solution)/shard_map/ppermute | solution.py:400
  16.0 33.1 %collective-permute-start.16 = (bf16[32,1024]{1,0:T(8,128)(2,1)S(1)}, bf16[32,1024]{1,0:T(8,128)(2,1)S(1)}, u32[]{:S(2)}, u32[]{:S(2)}) collective-permute-start(bf16[32,1024]{1,0:T(8,128)(2,1)S(1)} %bitcast.18), channel_id=1, source_target_pairs={{0,3},{1,2},{2,1},{3,0},{4,7},{5,6},{6,5},{7,4},{8,11},{9,10},{10,... | collective-permute-start | bytes 196616 | tf_op jit(solution)/shard_map/ppermute | solution.py:400
  49.8 14.5 %collective-permute-start.18 = (bf16[4,32,1024]{2,1,0:T(8,128)(2,1)}, bf16[4,32,1024]{2,1,0:T(8,128)(2,1)}, u32[]{:S(2)}, u32[]{:S(2)}) collective-permute-start(bf16[4,32,1024]{2,1,0:T(8,128)(2,1)} %get-tuple-element.42), channel_id=1, source_target_pairs={{0,64},{16,80},{32,96},{48,112},{64,0},{80,16},{96,32},{112,48},{1... | collective-permute-start | bytes 786440 | tf_op jit(solution)/shard_map/ppermute | solution.py:400
  52.7 11.6 %collective-permute-start.17 = (bf16[4,32,1024]{2,1,0:T(8,128)(2,1)}, bf16[4,32,1024]{2,1,0:T(8,128)(2,1)}, u32[]{:S(2)}, u32[]{:S(2)}) collective-permute-start(bf16[4,32,1024]{2,1,0:T(8,128)(2,1)} %get-tuple-element.42), channel_id=1, source_target_pairs={{0,32},{16,48},{32,0},{48,16},{64,96},{80,112},{96,64},{112,80},{1... | collective-permute-start | bytes 786440 | tf_op jit(solution)/shard_map/ppermute | solution.py:400
  53.1 11.5 %collective-permute-start.19 = (bf16[4,32,1024]{2,1,0:T(8,128)(2,1)}, bf16[4,32,1024]{2,1,0:T(8,128)(2,1)}, u32[]{:S(2)}, u32[]{:S(2)}) collective-permute-start(bf16[4,32,1024]{2,1,0:T(8,128)(2,1)} %get-tuple-element.42), channel_id=1, source_target_pairs={{0,96},{16,112},{32,64},{48,80},{64,32},{80,48},{96,0},{112,16},{1... | collective-permute-start | bytes 786440 | tf_op jit(solution)/shard_map/ppermute | solution.py:400
  60.4 14.6 %collective-permute-start = (bf16[8,16,1536]{2,1,0:T(8,128)(2,1)}, bf16[8,16,1536]{2,1,0:T(8,128)(2,1)S(1)}, u32[]{:S(2)}, u32[]{:S(2)}) collective-permute-start(bf16[8,16,1536]{2,1,0:T(8,128)(2,1)} %get-tuple-element.24), channel_id=1, source_target_pairs={{0,16},{16,0},{32,48},{48,32},{64,80},{80,64},{96,112},{112,96},{1... | collective-permute-start | bytes 1179656 | tf_op jit(solution)/shard_map/ppermute | solution.py:406
  63.2 15.8 %collective-permute-start.1 = (bf16[8,16,1536]{2,1,0:T(8,128)(2,1)}, bf16[8,16,1536]{2,1,0:T(8,128)(2,1)S(1)}, u32[]{:S(2)}, u32[]{:S(2)}) collective-permute-start(bf16[8,16,1536]{2,1,0:T(8,128)(2,1)} %get-tuple-element.25), channel_id=1, source_target_pairs={{0,32},{16,48},{32,0},{48,16},{64,96},{80,112},{96,64},{112,80},{1... | collective-permute-start | bytes 1179656 | tf_op jit(solution)/shard_map/ppermute | solution.py:406
  66.9 52.8 %collective-permute-start.22 = (bf16[4,4,32,1024]{3,2,1,0:T(8,128)(2,1)}, bf16[4,4,32,1024]{3,2,1,0:T(8,128)(2,1)}, u32[]{:S(2)}, u32[]{:S(2)}) collective-permute-start(bf16[4,4,32,1024]{3,2,1,0:T(8,128)(2,1)} %pad_maximum_fusion.rest_8_), channel_id=1, source_target_pairs={{0,12},{1,13},{2,14},{3,15},{4,8},{5,9},{6,10},{7,11},{8,4},{9,5},... | collective-permute-start | bytes 3145736 | tf_op jit(solution)/shard_map/ppermute | solution.py:400
  74.3 46.9 %collective-permute-start.21 = (bf16[4,4,32,1024]{3,2,1,0:T(8,128)(2,1)}, bf16[4,4,32,1024]{3,2,1,0:T(8,128)(2,1)}, u32[]{:S(2)}, u32[]{:S(2)}) collective-permute-start(bf16[4,4,32,1024]{3,2,1,0:T(8,128)(2,1)} %pad_maximum_fusion.rest_8_), channel_id=1, source_target_pairs={{0,8},{1,9},{2,10},{3,11},{4,12},{5,13},{6,14},{7,15},{8,0},{9,1},... | collective-permute-start | bytes 3145736 | tf_op jit(solution)/shard_map/ppermute | solution.py:400
  75.0 46.2 %collective-permute-start.20 = (bf16[4,4,32,1024]{3,2,1,0:T(8,128)(2,1)}, bf16[4,4,32,1024]{3,2,1,0:T(8,128)(2,1)}, u32[]{:S(2)}, u32[]{:S(2)}) collective-permute-start(bf16[4,4,32,1024]{3,2,1,0:T(8,128)(2,1)} %pad_maximum_fusion.rest_8_), channel_id=1, source_target_pairs={{0,4},{1,5},{2,6},{3,7},{4,0},{5,1},{6,2},{7,3},{8,12},{9,13},{10,... | collective-permute-start | bytes 3145736 | tf_op jit(solution)/shard_map/ppermute | solution.py:400
  75.7 13.4 %collective-permute-start.2 = (bf16[8,16,1536]{2,1,0:T(8,128)(2,1)}, bf16[8,16,1536]{2,1,0:T(8,128)(2,1)S(1)}, u32[]{:S(2)}, u32[]{:S(2)}) collective-permute-start(bf16[8,16,1536]{2,1,0:T(8,128)(2,1)} %get-tuple-element.26), channel_id=1, source_target_pairs={{0,48},{16,32},{32,16},{48,0},{64,112},{80,96},{96,80},{112,64},{1... | collective-permute-start | bytes 1179656 | tf_op jit(solution)/shard_map/ppermute | solution.py:406
  79.7 20.1 %collective-permute-start.3 = (bf16[8,16,1536]{2,1,0:T(8,128)(2,1)}, bf16[8,16,1536]{2,1,0:T(8,128)(2,1)S(1)}, u32[]{:S(2)}, u32[]{:S(2)}) collective-permute-start(bf16[8,16,1536]{2,1,0:T(8,128)(2,1)} %get-tuple-element.27), channel_id=1, source_target_pairs={{0,64},{16,80},{32,96},{48,112},{64,0},{80,16},{96,32},{112,48},{1... | collective-permute-start | bytes 1179656 | tf_op jit(solution)/shard_map/ppermute | solution.py:406
  89.9 17.0 %collective-permute-start.4 = (bf16[8,16,1536]{2,1,0:T(8,128)(2,1)}, bf16[8,16,1536]{2,1,0:T(8,128)(2,1)S(1)}, u32[]{:S(2)}, u32[]{:S(2)}) collective-permute-start(bf16[8,16,1536]{2,1,0:T(8,128)(2,1)} %get-tuple-element.28), channel_id=1, source_target_pairs={{0,80},{16,64},{32,112},{48,96},{64,16},{80,0},{96,48},{112,32},{1... | collective-permute-start | bytes 1179656 | tf_op jit(solution)/shard_map/ppermute | solution.py:406
  100.6 15.5 %collective-permute-start.5 = (bf16[8,16,1536]{2,1,0:T(8,128)(2,1)}, bf16[8,16,1536]{2,1,0:T(8,128)(2,1)}, u32[]{:S(2)}, u32[]{:S(2)}) collective-permute-start(bf16[8,16,1536]{2,1,0:T(8,128)(2,1)} %get-tuple-element.29), channel_id=1, source_target_pairs={{0,96},{16,112},{32,64},{48,80},{64,32},{80,48},{96,0},{112,16},{1... | collective-permute-start | bytes 1179656 | tf_op jit(solution)/shard_map/ppermute | solution.py:406
  107.7 29.2 %collective-permute-start.6 = (bf16[8,16,1536]{2,1,0:T(8,128)(2,1)}, bf16[8,16,1536]{2,1,0:T(8,128)(2,1)}, u32[]{:S(2)}, u32[]{:S(2)}) collective-permute-start(bf16[8,16,1536]{2,1,0:T(8,128)(2,1)} %get-tuple-element.30), channel_id=1, source_target_pairs={{0,112},{16,96},{32,80},{48,64},{64,48},{80,32},{96,16},{112,0},{1... | collective-permute-start | bytes 1179656 | tf_op jit(solution)/shard_map/ppermute | solution.py:406
  116.1 83.6 %collective-permute-start.23 = (bf16[4,4,32,1024]{3,2,1,0:T(8,128)(2,1)}, bf16[4,4,32,1024]{3,2,1,0:T(8,128)(2,1)}, u32[]{:S(2)}, u32[]{:S(2)}) collective-permute-start(bf16[4,4,32,1024]{3,2,1,0:T(8,128)(2,1)} %pad_maximum_fusion.rest_8_), channel_id=1, source_target_pairs={{0,16},{16,0},{32,48},{48,32},{64,80},{80,64},{96,112},{112,96},{1... | collective-permute-start | bytes 3145736 | tf_op jit(solution)/shard_map/ppermute | solution.py:400
  119.6 80.1 %collective-permute-start.26 = (bf16[4,4,32,1024]{3,2,1,0:T(8,128)(2,1)}, bf16[4,4,32,1024]{3,2,1,0:T(8,128)(2,1)}, u32[]{:S(2)}, u32[]{:S(2)}) collective-permute-start(bf16[4,4,32,1024]{3,2,1,0:T(8,128)(2,1)} %collective-permute-done.22.rest_11_), channel_id=1, source_target_pairs={{0,16},{16,0},{32,48},{48,32},{64,80},{80,64},{96,112},{112,96},{1... | collective-permute-start | bytes 3145736 | tf_op jit(solution)/shard_map/ppermute | solution.py:400
  121.2 78.6 %collective-permute-start.25 = (bf16[4,4,32,1024]{3,2,1,0:T(8,128)(2,1)}, bf16[4,4,32,1024]{3,2,1,0:T(8,128)(2,1)}, u32[]{:S(2)}, u32[]{:S(2)}) collective-permute-start(bf16[4,4,32,1024]{3,2,1,0:T(8,128)(2,1)} %collective-permute-done.21.rest_10_), channel_id=1, source_target_pairs={{0,16},{16,0},{32,48},{48,32},{64,80},{80,64},{96,112},{112,96},{1... | collective-permute-start | bytes 3145736 | tf_op jit(solution)/shard_map/ppermute | solution.py:400
  121.2 78.6 %collective-permute-start.24 = (bf16[4,4,32,1024]{3,2,1,0:T(8,128)(2,1)}, bf16[4,4,32,1024]{3,2,1,0:T(8,128)(2,1)}, u32[]{:S(2)}, u32[]{:S(2)}) collective-permute-start(bf16[4,4,32,1024]{3,2,1,0:T(8,128)(2,1)} %collective-permute-done.20.rest_9_), channel_id=1, source_target_pairs={{0,16},{16,0},{32,48},{48,32},{64,80},{80,64},{96,112},{112,96},{1... | collective-permute-start | bytes 3145736 | tf_op jit(solution)/shard_map/ppermute | solution.py:400
  130.3 58.8 %all-to-all-start.1 = ((bf16[16,64,512]{2,1,0:T(8,128)(2,1)}), bf16[16,64,512]{2,1,0:T(8,128)(2,1)}, u32[]{:S(2)}, u32[]{:S(2)}) async-start(bf16[16,64,512]{2,1,0:T(8,128)(2,1)} %bitcast.15), calls=%async_computation.1 | async-start | bytes 2097152 | tf_op jit(solution)/shard_map/all_to_all | solution.py:435
  168.1 8.0 %collective-permute-start.11 = (bf16[16,8,512]{2,1,0:T(8,128)(2,1)}, bf16[16,8,512]{2,1,0:T(8,128)(2,1)S(1)}, u32[]{:S(2)}, u32[]{:S(2)}) collective-permute-start(bf16[16,8,512]{2,1,0:T(8,128)(2,1)} %get-tuple-element.36), channel_id=1, source_target_pairs={{0,80},{16,64},{32,112},{48,96},{64,16},{80,0},{96,48},{112,32},{1... | collective-permute-start | bytes 393224 | tf_op jit(solution)/shard_map/ppermute | solution.py:406
  182.2 6.9 %collective-permute-start.13 = (bf16[16,8,512]{2,1,0:T(8,128)(2,1)}, bf16[16,8,512]{2,1,0:T(8,128)(2,1)S(1)}, u32[]{:S(2)}, u32[]{:S(2)}) collective-permute-start(bf16[16,8,512]{2,1,0:T(8,128)(2,1)} %get-tuple-element.38), channel_id=1, source_target_pairs={{0,112},{16,96},{32,80},{48,64},{64,48},{80,32},{96,16},{112,0},{1... | collective-permute-start | bytes 393224 | tf_op jit(solution)/shard_map/ppermute | solution.py:406
  (21 other events, 236.2 us)

commit v4 on v3

--- a/solution.py
+++ b/solution.py
@@ -273,32 +273,56 @@
         ),
         out_shape=[jax.ShapeDtypeStruct(result, jnp.bfloat16)] * peers,
         name="col_attend",
-    )(me, pattern.reshape(-1), count, *[in_place(p) for p in pieces])
-
-
-def weight_copies(place, weights, line, sem, turn, slot):
-    _, near, span, _ = weights[0].shape
-    plane = place[1]
-    copies = []
-    for sx, weight in enumerate(weights):
-        for sz in range(near):
-            at = ((plane // near ^ sx) * near + (lax.rem(plane, near) ^ sz)) * span
-            target = line.at[slot, pl.ds(pl.multiple_of(at, span), span), :]
-            copies.append(pltpu.make_async_copy(weight.at[turn, sz], target, sem.at[slot]))
-    return copies
-
-
-def project_block(place, heads, weights, line, sem, out_ref):
-    turn = pl.program_id(0)
-    slot = lax.rem(turn, 2)
-
-    @pl.when(turn + 1 < pl.num_programs(0))
+    )(me, pattern.reshape(-1), count, pieces[0], *[in_place(p) for p in pieces[1:]])
+
+
+def project_kernel(place, row_ref, *rest, peers, near):
+    pieces, (out_ref, heads, line, sem) = rest[:peers], rest[-4:]
+    weights = rest[peers:-4]
+    width = HR * HD
+    own = pieces[0].shape[1]
+    me, plane = place[0], place[1]
+    step = pl.program_id(0)
+    slot = lax.rem(step, 2)
+    at_x, at_z = lax.div(plane, near), lax.rem(plane, near)
+
+    def fetch(step, slot):
+        turn = lax.rem(step, near)
+        for core in range(2):
+
+            @pl.when(lax.div(step, near) == core)
+            def _(core=core):
+                group = weights[2 * near * core : 2 * near * (core + 1)]
+                for a in range(near):
+                    for b in range(near):
+                        for half, (x, z) in enumerate(((a, b), (b, a))):
+                            source = group[half * near + a].at[turn, b]
+                            span, wide = source.shape
+                            at = ((at_x ^ x) * near + (at_z ^ z)) * span
+                            target = line.at[
+                                slot,
+                                pl.ds(pl.multiple_of(at, span), span),
+                                pl.ds(half * wide, wide),
+                            ]
+                            pltpu.make_async_copy(source, target, sem.at[slot]).start()
+
+    @pl.when(step == 0)
     def _():
-        for copy in weight_copies(place, weights, line, sem, turn + 1, 1 - slot):
-            copy.start()
-
-    for copy in weight_copies(place, weights, line, sem, turn, slot):
-        copy.wait()
+        fetch(step, slot)
+        odd = lax.rem(me, 2) == 1
+        heads[:, :, 0:width] = row_ref[...]
+        for s in range(0, peers, 2):
+            a = pieces[s][...].astype(jnp.float32)
+            b = pieces[s + 1][...].astype(jnp.float32)
+            both = jnp.concatenate([jnp.where(odd, b, a), jnp.where(odd, a, b)], axis=1)
+            at = pl.multiple_of(((me ^ s) // 2) * 2 * own, 2 * own)
+            heads[:, pl.ds(at, 2 * own), width:] = both.astype(jnp.bfloat16)
+
+    @pl.when(step + 1 < pl.num_programs(0))
+    def _():
+        fetch(step + 1, 1 - slot)
+
+    pltpu.make_async_copy(line.at[slot], line.at[slot], sem.at[slot]).wait()
     out_ref[...] = lax.dot_general(
         heads[...].reshape(-1, heads.shape[2]),
         line[slot],
@@ -307,92 +331,33 @@
     ).astype(jnp.bfloat16)
 
 
-def project_first_kernel(place, row_ref, *rest, quarter):
-    pieces, weights = rest[: -4 - quarter], rest[-4 - quarter : -4]
-    out_ref, heads, line, sem = rest[-4:]
-    width = HR * HD
-    own = pieces[0].shape[1]
-
-    @pl.when(pl.program_id(0) == 0)
-    def _():
-        for copy in weight_copies(place, weights, line, sem, 0, 0):
-            copy.start()
-        me = place[0]
-        odd = lax.rem(me, 2) == 1
-        heads[:, :, 0:width] = row_ref[...]
-        for s in range(0, len(pieces), 2):
-            a = pieces[s][...].astype(jnp.float32)
-            b = pieces[s + 1][...].astype(jnp.float32)
-            both = jnp.concatenate([jnp.where(odd, b, a), jnp.where(odd, a, b)], axis=1)
-            at = pl.multiple_of(((me ^ s) // 2) * 2 * own, 2 * own)
-            heads[:, pl.ds(at, 2 * own), width:] = both.astype(jnp.bfloat16)
-
-    project_block(place, heads, weights, line, sem, out_ref)
-
-
-def project_second_kernel(place, heads, *rest, quarter):
-    weights, (_, out_ref, line, sem) = rest[:quarter], rest[quarter:]
-
-    @pl.when(pl.program_id(0) == 0)
-    def _():
-        for copy in weight_copies(place, weights, line, sem, 0, 0):
-            copy.start()
-
-    project_block(place, heads, weights, line, sem, out_ref)
-
-
-def whole(a):
-    return pl.BlockSpec(a.shape, lambda j, *_: (0,) * a.ndim)
-
-
-def project_first(place, row_out, pieces, weights, outs):
+def project(place, row_out, pieces, weights, outs):
     span, cells, _ = row_out.shape
-    turns, near, part, channels = weights[0].shape
-    tile = len(weights) * near * part
-    return pl.pallas_call(
-        functools.partial(project_first_kernel, quarter=len(weights)),
+    turns, near, part, wide = weights[0].shape
+    channels = 2 * wide
+    tile = near * near * part
+    held = pl.BlockSpec(memory_space=pltpu.VMEM)
+
+    def target(j, at):
+        return 0, at[0] ^ (2 * lax.rem(j, turns) + lax.div(j, turns))
+
+    return pl.pallas_call(
+        functools.partial(project_kernel, peers=len(pieces), near=near),
         grid_spec=pltpu.PrefetchScalarGridSpec(
             num_scalar_prefetch=1,
-            grid=(turns,),
-            in_specs=[pl.BlockSpec(memory_space=pltpu.VMEM)] * (1 + len(pieces))
+            grid=(2 * turns,),
+            in_specs=[held] * (1 + len(pieces))
             + [pl.BlockSpec(memory_space=pl.ANY)] * len(weights),
-            out_specs=[
-                pl.BlockSpec((span * cells, tile), lambda j, at: (0, at[0] ^ (2 * j))),
-                pl.BlockSpec((span, cells, channels), lambda j, *_: (0, 0, 0)),
-            ],
+            out_specs=pl.BlockSpec((span * cells, tile), target),
             scratch_shapes=[
+                pltpu.VMEM((span, cells, channels), jnp.bfloat16),
                 pltpu.VMEM((2, tile, channels), jnp.bfloat16),
                 pltpu.SemaphoreType.DMA((2,)),
             ],
         ),
-        out_shape=[
-            jax.ShapeDtypeStruct((span * cells, outs), jnp.bfloat16),
-            jax.ShapeDtypeStruct((span, cells, channels), jnp.bfloat16),
-        ],
-        name="project_first",
-    )(place, in_place(row_out), *[in_place(p) for p in pieces], *weights)
-
-
-def project_second(place, heads, weights, kept):
-    span, cells, channels = heads.shape
-    turns, near, part, _ = weights[0].shape
-    tile = len(weights) * near * part
-    return pl.pallas_call(
-        functools.partial(project_second_kernel, quarter=len(weights)),
-        grid_spec=pltpu.PrefetchScalarGridSpec(
-            num_scalar_prefetch=1,
-            grid=(turns,),
-            in_specs=[whole(heads)] + [pl.BlockSpec(memory_space=pl.ANY)] * (1 + len(weights)),
-            out_specs=pl.BlockSpec((span * cells, tile), lambda j, at: (0, at[0] ^ (2 * j + 1))),
-            scratch_shapes=[
-                pltpu.VMEM((2, tile, channels), jnp.bfloat16),
-                pltpu.SemaphoreType.DMA((2,)),
-            ],
-        ),
-        out_shape=jax.ShapeDtypeStruct(kept.shape, jnp.bfloat16),
-        input_output_aliases={2 + len(weights): 0},
-        name="project_second",
-    )(place, heads, *weights, kept)
+        out_shape=jax.ShapeDtypeStruct((span * cells, outs), jnp.bfloat16),
+        name="project",
+    )(place, in_place(row_out), pieces[0], *[in_place(p) for p in pieces[1:]], *weights)
 
 
 def by_xor(x, axis, masks):
@@ -406,6 +371,21 @@
         lax.ppermute(pieces[s], "rows", [(d, d ^ s) for d in range(peers)])
         for s in range(1, peers)
     ]
+
+
+def join_kernel(*refs):
+    for i, ref in enumerate(refs[:-1]):
+        refs[-1][i] = ref[...]
+
+
+def join(parts):
+    return pl.pallas_call(
+        join_kernel,
+        in_specs=[pl.BlockSpec(memory_space=pltpu.VMEM)] * len(parts),
+        out_specs=pl.BlockSpec(memory_space=pltpu.VMEM),
+        out_shape=jax.ShapeDtypeStruct((len(parts),) + parts[0].shape, parts[0].dtype),
+        name="join",
+    )(*[in_place(p) for p in parts])
 
 
 def body(
@@ -422,28 +402,28 @@
     place = jnp.stack([lax.axis_index("rows"), lax.axis_index("cols")]).astype(jnp.int32)
 
     shard = out_weight.T
-    along_z = [shard] + by_xor(shard, "cols", (1, 2, 3))
+    middle = shard.shape[1] // 2
+    upper, lower = shard[:, :middle], shard[:, middle:]
+    along_z = [upper] + by_xor(upper, "cols", (1, 2, 3))
+    along_x = [lower] + by_xor(lower, "cols", (4, 8, 12))
     packed = row_pack(query_cells, key_cells, value_cells)
     lines = lax.all_to_all(packed, "cols", 0, 0, tiled=True)
-    held = jnp.stack(along_z)
+    held = join(along_z + along_x)
     along_y = [held] + by_xor(held, "rows", (2, 4, 6))
     sent = col_pack(me, query_cells, key_cells, value_cells, peers)
     pieces = swap_pieces(sent)
-    held = jnp.stack(along_y)
-    weights = [held] + by_xor(held, "cols", (4, 8, 12))
+    near = len(along_z)
+    upper = jnp.stack([h[:near] for h in along_y])
+    lower = jnp.stack([h[near:] for h in along_y])
+    weights = [upper] + by_xor(upper, "cols", (4, 8, 12))
+    weights += [lower] + by_xor(lower, "cols", (1, 2, 3))
     row_out = row_attend(pattern, count, lines)
     row_out = lax.all_to_all(row_out.reshape(row_span, col_span, -1), "cols", 0, 0, tiled=True)
     col_out = col_attend(me, col_pattern, col_count, pieces)
     col_out = swap_pieces(col_out)
-    others = [by_xor(w, "rows", (1,))[0] for w in weights]
-    half, heads = project_first(
-        place,
-        row_out,
-        col_out,
-        weights,
-        out_weight.shape[1] * peers * lax.axis_size("cols"),
-    )
-    projected = project_second(place, heads, others, half)
+    weights += [by_xor(w, "rows", (1,))[0] for w in weights]
+    outs = out_weight.shape[1] * peers * lax.axis_size("cols")
+    projected = project(place, row_out, col_out, weights, outs)
     return projected.reshape(row_span, col_span, projected.shape[-1])
 
 

time: 211 us -> 221 us (1.047)
  starting transfers between devices: 59.9 us -> 66.2 us
  local copies, waits for them, and re-layouts: 13 us -> 16.2 us
  waiting for transfers between devices: 89.2 us -> 91.8 us
  Pallas kernels: 44 us -> 41.7 us
    ppermute x13 -> x23, starting transfers between devices: 18.1 us -> 35 us  [by_xor(): lax.ppermute(x, axis, [(d, d ^ s) for d in range(size)])]
    ppermute x13 -> x23, waiting for transfers between devices: 36.1 us -> 47 us  [by_xor(): lax.ppermute(x, axis, [(d, d ^ s) for d in range(size)])]
    ppermute x14, starting transfers between devices: 27.6 us -> 18.6 us  [swap_pieces(): lax.ppermute(pieces[s], 'rows', [(d, d ^ s) for d in range(peers)])]
    ppermute x14, waiting for transfers between devices: 53.1 us -> 44.9 us  [swap_pieces(): lax.ppermute(pieces[s], 'rows', [(d, d ^ s) for d in range(peers)])]
    another operation x0 -> x4, local copies, waits for them, and re-layouts: none -> 4.61 us  [body(): lower = jnp.stack([h[near:] for h in along_y])]
    pallas_call x2, Pallas kernels: 19.7 us -> 15.7 us  [the longest x1 14.9 us: project(): pl.pallas_call(functools.partial(project_kernel, peers=len(pieces), near=...]
    unnamed x33 -> x49, local copies, waits for them, and re-layouts: 10.8 us -> 9.43 us
  transfers between devices with their start and end apart: 29 -> 39, of which waited for: 16 -> 18; matrix products, arithmetic and copies ran while one was open for 3% -> 4% of each run, Pallas kernels for 14% -> 10%
where the time goes in v4:
time: 221 us; the launch traced here: 219 us
  waiting for transfers between devices  91.8 us (42%)
  starting transfers between devices  66.2 us (30%)
  Pallas kernels  41.7 us (19%)
  local copies, waits for them, and re-layouts  16.2 us (7%)
  other arithmetic  2.44 us (1%)
    ppermute x23, waiting for transfers between devices, by_xor(): lax.ppermute(x, axis, [(d, d ^ s) for d in range(size)])  47 us
    ppermute x14, waiting for transfers between devices, swap_pieces(): lax.ppermute(pieces[s], 'rows', [(d, d ^ s) for d in range(peers)])  44.9 us
    ppermute x23, starting transfers between devices, by_xor(): lax.ppermute(x, axis, [(d, d ^ s) for d in range(size)])  35 us
    ppermute x14, starting transfers between devices, swap_pieces(): lax.ppermute(pieces[s], 'rows', [(d, d ^ s) for d in range(peers)])  18.6 us
    pallas_call x1, Pallas kernels, project(): pl.pallas_call(functools.partial(project_kernel, peers=len(pieces), near=...  14.9 us
    pallas_call x1, Pallas kernels, row_attend(): pl.pallas_call(functools.partial(row_attend_kernel, chosen=chosen), grid_...  9.58 us
    unnamed x49, local copies, waits for them, and re-layouts  9.43 us
    all_to_all x1, starting transfers between devices, body(): lines = lax.all_to_all(packed, 'cols', 0, 0, tiled=True)  8.46 us
  transfers between devices with their start and end apart: 39, of which 18 were waited for; matrix products, arithmetic and copies ran while one was open for 4% of the time, Pallas kernels for 10%

profile of v4, /device:TPU:1, one launch (start us, length us, event | category | flops | bytes accessed | tf_op | source)
XLA Modules:
  0.0 218.8 jit_solution(8049083253906886414)
XLA Ops:
  0.0 4.2 %row_pack.1 = bf16[16,64,1536]{2,1,0:T(8,128)(2,1)} custom-call(bf16[16,64,1024]{2,1,0:T(8,128)(2,1)} %q_ref.3, bf16[16,64,1024]{2,1,0:T(8,128)(2,1)} %k_ref.3, bf16[16,64,1024]{2,1,0:T(8,128)(2,1)} %v_ref.3), custom_call_target="tpu_custom_call" | custom-call | tf_op jit(solution)/shard_map/row_pack/pallas_call | solution.py:37
  4.2 8.5 %all-to-all-start = ((bf16[16,64,1536]{2,1,0:T(8,128)(2,1)}), bf16[16,64,1536]{2,1,0:T(8,128)(2,1)}, u32[]{:S(2)}, u32[]{:S(2)}) async-start(bf16[16,64,1536]{2,1,0:T(8,128)(2,1)} %row_pack.1), calls=%async_computation | async-start | bytes 6291456 | tf_op jit(solution)/shard_map/all_to_all | solution.py:410
  12.7 6.9 %col_pack.1 = (bf16[8,16,1536]{2,1,0:T(8,128)(2,1)}, bf16[8,16,1536]{2,1,0:T(8,128)(2,1)}, bf16[8,16,1536]{2,1,0:T(8,128)(2,1)}, bf16[8,16,1536]{2,1,0:T(8,128)(...) custom-call(s32[1]{0:T(128)} %bitcast.me_ref, ...), custom_call_target="tpu_custom_call" | custom-call | tf_op jit(solution)/shard_map/col_pack/pallas_call | solution.py:87
  22.3 2.9 %collective-permute-start.19 = (bf16[32,512]{1,0:T(8,128)(2,1)S(1)}, bf16[32,512]{1,0:T(8,128)(2,1)S(1)}, u32[]{:S(2)}, u32[]{:S(2)}) collective-permute-start(bf16[32,512]{1,0:T(8,128)(2,1)S(1)} %get-tuple-element.45.refs_4_), channel_id=1, source_target_pairs={{0,12},{1,13},{2,14},{3,15},{4,8},{5,9},{6,10},{7,11},{8,4},{9,5},... | collective-permute-start | bytes 98312 | tf_op jit(solution)/shard_map/ppermute | solution.py:365
  25.7 22.8 %collective-permute-done.19.refs_7_ = bf16[32,512]{1,0:T(8,128)(2,1)S(1)} collective-permute-done((bf16[32,512]{1,0:T(8,128)(2,1)S(1)}, bf16[32,512]{1,0:T(8,128)(2,1)S(1)}, u32[]{:S(2)}, u32[]{:S(2)}) %collective-permute-start.19) | collective-permute-done | bytes 32800 | tf_op jit(solution)/shard_map/ppermute | solution.py:365
  48.6 7.1 %collective-permute-start.17 = (bf16[32,512]{1,0:T(8,128)(2,1)S(1)}, bf16[32,512]{1,0:T(8,128)(2,1)S(1)}, u32[]{:S(2)}, u32[]{:S(2)}) collective-permute-start(bf16[32,512]{1,0:T(8,128)(2,1)S(1)} %get-tuple-element.45.refs_4_), channel_id=1, source_target_pairs={{0,4},{1,5},{2,6},{3,7},{4,0},{5,1},{6,2},{7,3},{8,12},{9,13},{10,... | collective-permute-start | bytes 98312 | tf_op jit(solution)/shard_map/ppermute | solution.py:365
  63.2 2.7 %collective-permute-start.22 = (bf16[8,32,512]{2,1,0:T(8,128)(2,1)}, bf16[8,32,512]{2,1,0:T(8,128)(2,1)S(1)}, u32[]{:S(2)}, u32[]{:S(2)}) collective-permute-start(bf16[8,32,512]{2,1,0:T(8,128)(2,1)} %join.1), channel_id=1, source_target_pairs={{0,96},{16,112},{32,64},{48,80},{64,32},{80,48},{96,0},{112,16},{1... | collective-permute-start | bytes 786440 | tf_op jit(solution)/shard_map/ppermute | solution.py:365
  68.2 8.3 %collective-permute-done.22 = bf16[8,32,512]{2,1,0:T(8,128)(2,1)S(1)} collective-permute-done((bf16[8,32,512]{2,1,0:T(8,128)(2,1)}, bf16[8,32,512]{2,1,0:T(8,128)(2,1)S(1)}, u32[]{:S(2)}, u32[]{:S(2)}) %collective-permute-start.22) | collective-permute-done | bytes 262176 | tf_op jit(solution)/shard_map/ppermute | solution.py:365
  79.2 3.8 %collective-permute-start.4 = (bf16[8,16,1536]{2,1,0:T(8,128)(2,1)}, bf16[8,16,1536]{2,1,0:T(8,128)(2,1)S(1)}, u32[]{:S(2)}, u32[]{:S(2)}) collective-permute-start(bf16[8,16,1536]{2,1,0:T(8,128)(2,1)} %get-tuple-element.26), channel_id=1, source_target_pairs={{0,80},{16,64},{32,112},{48,96},{64,16},{80,0},{96,48},{112,32},{1... | collective-permute-start | bytes 1179656 | tf_op jit(solution)/shard_map/ppermute | solution.py:371
  83.0 2.5 %collective-permute-start.5 = (bf16[8,16,1536]{2,1,0:T(8,128)(2,1)}, bf16[8,16,1536]{2,1,0:T(8,128)(2,1)S(1)}, u32[]{:S(2)}, u32[]{:S(2)}) collective-permute-start(bf16[8,16,1536]{2,1,0:T(8,128)(2,1)} %get-tuple-element.27), channel_id=1, source_target_pairs={{0,96},{16,112},{32,64},{48,80},{64,32},{80,48},{96,0},{112,16},{1... | collective-permute-start | bytes 1179656 | tf_op jit(solution)/shard_map/ppermute | solution.py:371
  88.3 12.0 %collective-permute-done.4.rest_5_ = bf16[8,16,1536]{2,1,0:T(8,128)(2,1)S(1)} collective-permute-done((bf16[8,16,1536]{2,1,0:T(8,128)(2,1)}, bf16[8,16,1536]{2,1,0:T(8,128)(2,1)S(1)}, u32[]{:S(2)}, u32[]{:S(2)}) %collective-permute-start.4) | collective-permute-done | bytes 393248 | tf_op jit(solution)/shard_map/ppermute | solution.py:371
  100.4 6.0 %collective-permute-done.5.rest_6_ = bf16[8,16,1536]{2,1,0:T(8,128)(2,1)S(1)} collective-permute-done((bf16[8,16,1536]{2,1,0:T(8,128)(2,1)}, bf16[8,16,1536]{2,1,0:T(8,128)(2,1)S(1)}, u32[]{:S(2)}, u32[]{:S(2)}) %collective-permute-start.5) | collective-permute-done | bytes 393248 | tf_op jit(solution)/shard_map/ppermute | solution.py:371
  106.3 8.4 %collective-permute-done.6.rest_7_ = bf16[8,16,1536]{2,1,0:T(8,128)(2,1)S(1)} collective-permute-done((bf16[8,16,1536]{2,1,0:T(8,128)(2,1)}, bf16[8,16,1536]{2,1,0:T(8,128)(2,1)S(1)}, u32[]{:S(2)}, u32[]{:S(2)}) %collective-permute-start.6) | collective-permute-done | bytes 393248 | tf_op jit(solution)/shard_map/ppermute | solution.py:371
  114.7 5.5 %col_attend.1 = (bf16[16,8,512]{2,1,0:T(8,128)(2,1)}, bf16[16,8,512]{2,1,0:T(8,128)(2,1)}, bf16[16,8,512]{2,1,0:T(8,128)(2,1)}, bf16[16,8,512]{2,1,0:T(8,128)(2,...) custom-call(s32[1]{0:T(128)} %bitcast.me_ref, ...), custom_call_target="tpu_custom_call" | custom-call | tf_op jit(solution)/shard_map/col_attend/pallas_call | solution.py:262
  123.3 2.8 %collective-permute-start.10 = (bf16[16,8,512]{2,1,0:T(8,128)(2,1)}, bf16[16,8,512]{2,1,0:T(8,128)(2,1)S(1)}, u32[]{:S(2)}, u32[]{:S(2)}) collective-permute-start(bf16[16,8,512]{2,1,0:T(8,128)(2,1)} %get-tuple-element.33), channel_id=1, source_target_pairs={{0,64},{16,80},{32,96},{48,112},{64,0},{80,16},{96,32},{112,48},{1... | collective-permute-start | bytes 393224 | tf_op jit(solution)/shard_map/ppermute | solution.py:371
  128.7 2.9 %collective-permute-start.24 = (bf16[4,4,32,512]{3,2,1,0:T(8,128)(2,1)S(1)}, bf16[4,4,32,512]{3,2,1,0:T(8,128)(2,1)S(1)}, u32[]{:S(2)}, u32[]{:S(2)}) collective-permute-start(bf16[4,4,32,512]{3,2,1,0:T(8,128)(2,1)S(1)} %pad_maximum_fusion.rest_8_), channel_id=1, source_target_pairs={{0,8},{1,9},{2,10},{3,11},{4,12},{5,13},{6,14},{7,15},{8,0},{9,1},... | collective-permute-start | bytes 1572872 | tf_op jit(solution)/shard_map/ppermute | solution.py:365
  135.8 6.9 %collective-permute-done.11.rest_5_ = bf16[16,8,512]{2,1,0:T(8,128)(2,1)S(1)} collective-permute-done((bf16[16,8,512]{2,1,0:T(8,128)(2,1)}, bf16[16,8,512]{2,1,0:T(8,128)(2,1)S(1)}, u32[]{:S(2)}, u32[]{:S(2)}) %collective-permute-start.11) | collective-permute-done | bytes 131104 | tf_op jit(solution)/shard_map/ppermute | solution.py:371
  143.6 5.7 %collective-permute-done.12.rest_6_ = bf16[16,8,512]{2,1,0:T(8,128)(2,1)S(1)} collective-permute-done((bf16[16,8,512]{2,1,0:T(8,128)(2,1)}, bf16[16,8,512]{2,1,0:T(8,128)(2,1)S(1)}, u32[]{:S(2)}, u32[]{:S(2)}) %collective-permute-start.12) | collective-permute-done | bytes 131104 | tf_op jit(solution)/shard_map/ppermute | solution.py:371
  153.0 3.8 %collective-permute-done.13.rest_7_ = bf16[16,8,512]{2,1,0:T(8,128)(2,1)S(1)} collective-permute-done((bf16[16,8,512]{2,1,0:T(8,128)(2,1)}, bf16[16,8,512]{2,1,0:T(8,128)(2,1)S(1)}, u32[]{:S(2)}, u32[]{:S(2)}) %collective-permute-start.13) | collective-permute-done | bytes 131104 | tf_op jit(solution)/shard_map/ppermute | solution.py:371
  163.6 9.6 %row_attend.1 = bf16[1024,512]{1,0:T(8,128)(2,1)} custom-call(s32[192]{0:T(256)} %reshape.13.pattern_ref, s32[1]{0:T(128)} %dynamic_slice.7.count_ref, bf16[16,64,1536]{2,1,0:T(8,128)(2,1)} %all-to-all-done.x_ref), custom_call_target="tpu_custom_call" | custom-call | tf_op jit(solution)/shard_map/row_attend/pallas_call | solution.py:183
  173.1 4.2 %all-to-all-start.1 = ((bf16[16,64,512]{2,1,0:T(8,128)(2,1)}), bf16[16,64,512]{2,1,0:T(8,128)(2,1)S(1)}, u32[]{:S(2)}, u32[]{:S(2)}) async-start(bf16[16,64,512]{2,1,0:T(8,128)(2,1)} %bitcast.21), calls=%async_computation.1 | async-start | bytes 2097152 | tf_op jit(solution)/shard_map/all_to_all | solution.py:421
  178.5 8.2 %collective-permute-done.28.rest_15_ = bf16[4,4,32,512]{3,2,1,0:T(8,128)(2,1)} collective-permute-done((bf16[4,4,32,512]{3,2,1,0:T(8,128)(2,1)}, bf16[4,4,32,512]{3,2,1,0:T(8,128)(2,1)}, u32[]{:S(2)}, u32[]{:S(2)}) %collective-permute-start.28) | collective-permute-done | bytes 524320 | tf_op jit(solution)/shard_map/ppermute | solution.py:365
  186.8 8.2 %collective-permute-start.30 = (bf16[4,4,32,512]{3,2,1,0:T(8,128)(2,1)}, bf16[4,4,32,512]{3,2,1,0:T(8,128)(2,1)S(1)}, u32[]{:S(2)}, u32[]{:S(2)}) collective-permute-start(bf16[4,4,32,512]{3,2,1,0:T(8,128)(2,1)} %copy-done.14), channel_id=1, source_target_pairs={{0,16},{16,0},{32,48},{48,32},{64,80},{80,64},{96,112},{112,96},{1... | collective-permute-start | bytes 1572872 | tf_op jit(solution)/shard_map/ppermute | solution.py:365
  203.6 14.9 %project.1 = bf16[1024,4096]{1,0:T(8,128)(2,1)} custom-call(s32[2]{0:T(128)} %pad_add_fusion.place, bf16[16,64,512]{2,1,0:T(8,128)(2,1)S(1)} %all-to-all-done.1.row_ref, bf16[16,8,512]{2,1,0:T(8,128)(2,1)} %get-tuple-element.29.rest_0_, bf16[16,8,512]{2,1,0:T(8,128)(2,1)S(1)} %collective-permute-done.7.rest_1_, ...), custom_call_target="tpu_custom_call" | custom-call | tf_op jit(solution)/shard_map/project/pallas_call | solution.py:344
  (122 shorter events, 49.7 us)
Async XLA Ops:
  4.2 159.4 %all-to-all-start = ((bf16[16,64,1536]{2,1,0:T(8,128)(2,1)}), bf16[16,64,1536]{2,1,0:T(8,128)(2,1)}, u32[]{:S(2)}, u32[]{:S(2)}) async-start(bf16[16,64,1536]{2,1,0:T(8,128)(2,1)} %row_pack.1), calls=%async_computation | async-start | bytes 6291456 | tf_op jit(solution)/shard_map/all_to_all | solution.py:410
  19.5 63.5 %collective-permute-start = (bf16[8,16,1536]{2,1,0:T(8,128)(2,1)}, bf16[8,16,1536]{2,1,0:T(8,128)(2,1)S(1)}, u32[]{:S(2)}, u32[]{:S(2)}) collective-permute-start(bf16[8,16,1536]{2,1,0:T(8,128)(2,1)} %get-tuple-element.22), channel_id=1, source_target_pairs={{0,16},{16,0},{32,48},{48,32},{64,80},{80,64},{96,112},{112,96},{1... | collective-permute-start | bytes 1179656 | tf_op jit(solution)/shard_map/ppermute | solution.py:371
  20.6 65.0 %collective-permute-start.1 = (bf16[8,16,1536]{2,1,0:T(8,128)(2,1)}, bf16[8,16,1536]{2,1,0:T(8,128)(2,1)S(1)}, u32[]{:S(2)}, u32[]{:S(2)}) collective-permute-start(bf16[8,16,1536]{2,1,0:T(8,128)(2,1)} %get-tuple-element.23), channel_id=1, source_target_pairs={{0,32},{16,48},{32,0},{48,16},{64,96},{80,112},{96,64},{112,80},{1... | collective-permute-start | bytes 1179656 | tf_op jit(solution)/shard_map/ppermute | solution.py:371
  21.8 63.7 %collective-permute-start.2 = (bf16[8,16,1536]{2,1,0:T(8,128)(2,1)}, bf16[8,16,1536]{2,1,0:T(8,128)(2,1)S(1)}, u32[]{:S(2)}, u32[]{:S(2)}) collective-permute-start(bf16[8,16,1536]{2,1,0:T(8,128)(2,1)} %get-tuple-element.24), channel_id=1, source_target_pairs={{0,48},{16,32},{32,16},{48,0},{64,112},{80,96},{96,80},{112,64},{1... | collective-permute-start | bytes 1179656 | tf_op jit(solution)/shard_map/ppermute | solution.py:371
  22.3 26.3 %collective-permute-start.19 = (bf16[32,512]{1,0:T(8,128)(2,1)S(1)}, bf16[32,512]{1,0:T(8,128)(2,1)S(1)}, u32[]{:S(2)}, u32[]{:S(2)}) collective-permute-start(bf16[32,512]{1,0:T(8,128)(2,1)S(1)} %get-tuple-element.45.refs_4_), channel_id=1, source_target_pairs={{0,12},{1,13},{2,14},{3,15},{4,8},{5,9},{6,10},{7,11},{8,4},{9,5},... | collective-permute-start | bytes 98312 | tf_op jit(solution)/shard_map/ppermute | solution.py:365
  25.2 30.5 %collective-permute-start.18 = (bf16[32,512]{1,0:T(8,128)(2,1)S(1)}, bf16[32,512]{1,0:T(8,128)(2,1)S(1)}, u32[]{:S(2)}, u32[]{:S(2)}) collective-permute-start(bf16[32,512]{1,0:T(8,128)(2,1)S(1)} %get-tuple-element.45.refs_4_), channel_id=1, source_target_pairs={{0,8},{1,9},{2,10},{3,11},{4,12},{5,13},{6,14},{7,15},{8,0},{9,1},... | collective-permute-start | bytes 98312 | tf_op jit(solution)/shard_map/ppermute | solution.py:365
  63.2 13.3 %collective-permute-start.22 = (bf16[8,32,512]{2,1,0:T(8,128)(2,1)}, bf16[8,32,512]{2,1,0:T(8,128)(2,1)S(1)}, u32[]{:S(2)}, u32[]{:S(2)}) collective-permute-start(bf16[8,32,512]{2,1,0:T(8,128)(2,1)} %join.1), channel_id=1, source_target_pairs={{0,96},{16,112},{32,64},{48,80},{64,32},{80,48},{96,0},{112,16},{1... | collective-permute-start | bytes 786440 | tf_op jit(solution)/shard_map/ppermute | solution.py:365
  66.0 12.6 %collective-permute-start.21 = (bf16[8,32,512]{2,1,0:T(8,128)(2,1)}, bf16[8,32,512]{2,1,0:T(8,128)(2,1)S(1)}, u32[]{:S(2)}, u32[]{:S(2)}) collective-permute-start(bf16[8,32,512]{2,1,0:T(8,128)(2,1)} %join.1), channel_id=1, source_target_pairs={{0,64},{16,80},{32,96},{48,112},{64,0},{80,16},{96,32},{112,48},{1... | collective-permute-start | bytes 786440 | tf_op jit(solution)/shard_map/ppermute | solution.py:365
  76.5 11.8 %collective-permute-start.3 = (bf16[8,16,1536]{2,1,0:T(8,128)(2,1)}, bf16[8,16,1536]{2,1,0:T(8,128)(2,1)S(1)}, u32[]{:S(2)}, u32[]{:S(2)}) collective-permute-start(bf16[8,16,1536]{2,1,0:T(8,128)(2,1)} %get-tuple-element.25), channel_id=1, source_target_pairs={{0,64},{16,80},{32,96},{48,112},{64,0},{80,16},{96,32},{112,48},{1... | collective-permute-start | bytes 1179656 | tf_op jit(solution)/shard_map/ppermute | solution.py:371
  79.2 21.1 %collective-permute-start.4 = (bf16[8,16,1536]{2,1,0:T(8,128)(2,1)}, bf16[8,16,1536]{2,1,0:T(8,128)(2,1)S(1)}, u32[]{:S(2)}, u32[]{:S(2)}) collective-permute-start(bf16[8,16,1536]{2,1,0:T(8,128)(2,1)} %get-tuple-element.26), channel_id=1, source_target_pairs={{0,80},{16,64},{32,112},{48,96},{64,16},{80,0},{96,48},{112,32},{1... | collective-permute-start | bytes 1179656 | tf_op jit(solution)/shard_map/ppermute | solution.py:371
  83.0 23.3 %collective-permute-start.5 = (bf16[8,16,1536]{2,1,0:T(8,128)(2,1)}, bf16[8,16,1536]{2,1,0:T(8,128)(2,1)S(1)}, u32[]{:S(2)}, u32[]{:S(2)}) collective-permute-start(bf16[8,16,1536]{2,1,0:T(8,128)(2,1)} %get-tuple-element.27), channel_id=1, source_target_pairs={{0,96},{16,112},{32,64},{48,80},{64,32},{80,48},{96,0},{112,16},{1... | collective-permute-start | bytes 1179656 | tf_op jit(solution)/shard_map/ppermute | solution.py:371
  85.6 29.1 %collective-permute-start.6 = (bf16[8,16,1536]{2,1,0:T(8,128)(2,1)}, bf16[8,16,1536]{2,1,0:T(8,128)(2,1)S(1)}, u32[]{:S(2)}, u32[]{:S(2)}) collective-permute-start(bf16[8,16,1536]{2,1,0:T(8,128)(2,1)} %get-tuple-element.28), channel_id=1, source_target_pairs={{0,112},{16,96},{32,80},{48,64},{64,48},{80,32},{96,16},{112,0},{1... | collective-permute-start | bytes 1179656 | tf_op jit(solution)/shard_map/ppermute | solution.py:371
  85.6 36.7 %collective-permute-start.20 = (bf16[8,32,512]{2,1,0:T(8,128)(2,1)}, bf16[8,32,512]{2,1,0:T(8,128)(2,1)}, u32[]{:S(2)}, u32[]{:S(2)}) collective-permute-start(bf16[8,32,512]{2,1,0:T(8,128)(2,1)} %join.1), channel_id=1, source_target_pairs={{0,32},{16,48},{32,0},{48,16},{64,96},{80,112},{96,64},{112,80},{1... | collective-permute-start | bytes 786440 | tf_op jit(solution)/shard_map/ppermute | solution.py:365
  127.1 31.5 %collective-permute-start.29 = (bf16[4,4,32,512]{3,2,1,0:T(8,128)(2,1)S(1)}, bf16[4,4,32,512]{3,2,1,0:T(8,128)(2,1)S(1)}, u32[]{:S(2)}, u32[]{:S(2)}) collective-permute-start(bf16[4,4,32,512]{3,2,1,0:T(8,128)(2,1)S(1)} %pad_maximum_fusion.rest_8_), channel_id=1, source_target_pairs={{0,16},{16,0},{32,48},{48,32},{64,80},{80,64},{96,112},{112,96},{1... | collective-permute-start | bytes 1572872 | tf_op jit(solution)/shard_map/ppermute | solution.py:365
  127.8 31.4 %collective-permute-start.25 = (bf16[4,4,32,512]{3,2,1,0:T(8,128)(2,1)S(1)}, bf16[4,4,32,512]{3,2,1,0:T(8,128)(2,1)}, u32[]{:S(2)}, u32[]{:S(2)}) collective-permute-start(bf16[4,4,32,512]{3,2,1,0:T(8,128)(2,1)S(1)} %pad_maximum_fusion.rest_8_), channel_id=1, source_target_pairs={{0,12},{1,13},{2,14},{3,15},{4,8},{5,9},{6,10},{7,11},{8,4},{9,5},... | collective-permute-start | bytes 1572872 | tf_op jit(solution)/shard_map/ppermute | solution.py:365
  128.7 31.7 %collective-permute-start.24 = (bf16[4,4,32,512]{3,2,1,0:T(8,128)(2,1)S(1)}, bf16[4,4,32,512]{3,2,1,0:T(8,128)(2,1)S(1)}, u32[]{:S(2)}, u32[]{:S(2)}) collective-permute-start(bf16[4,4,32,512]{3,2,1,0:T(8,128)(2,1)S(1)} %pad_maximum_fusion.rest_8_), channel_id=1, source_target_pairs={{0,8},{1,9},{2,10},{3,11},{4,12},{5,13},{6,14},{7,15},{8,0},{9,1},... | collective-permute-start | bytes 1572872 | tf_op jit(solution)/shard_map/ppermute | solution.py:365
  132.3 29.5 %collective-permute-start.23 = (bf16[4,4,32,512]{3,2,1,0:T(8,128)(2,1)S(1)}, bf16[4,4,32,512]{3,2,1,0:T(8,128)(2,1)S(1)}, u32[]{:S(2)}, u32[]{:S(2)}) collective-permute-start(bf16[4,4,32,512]{3,2,1,0:T(8,128)(2,1)S(1)} %pad_maximum_fusion.rest_8_), channel_id=1, source_target_pairs={{0,4},{1,5},{2,6},{3,7},{4,0},{5,1},{6,2},{7,3},{8,12},{9,13},{10,... | collective-permute-start | bytes 1572872 | tf_op jit(solution)/shard_map/ppermute | solution.py:365
  157.5 19.8 %collective-permute-start.33 = (bf16[4,4,32,512]{3,2,1,0:T(8,128)(2,1)}, bf16[4,4,32,512]{3,2,1,0:T(8,128)(2,1)}, u32[]{:S(2)}, u32[]{:S(2)}) collective-permute-start(bf16[4,4,32,512]{3,2,1,0:T(8,128)(2,1)} %pad_maximum_fusion.1.rest_12_), channel_id=1, source_target_pairs={{0,16},{16,0},{32,48},{48,32},{64,80},{80,64},{96,112},{112,96},{1... | collective-permute-start | bytes 1572872 | tf_op jit(solution)/shard_map/ppermute | solution.py:365
  158.5 28.3 %collective-permute-start.28 = (bf16[4,4,32,512]{3,2,1,0:T(8,128)(2,1)}, bf16[4,4,32,512]{3,2,1,0:T(8,128)(2,1)}, u32[]{:S(2)}, u32[]{:S(2)}) collective-permute-start(bf16[4,4,32,512]{3,2,1,0:T(8,128)(2,1)} %pad_maximum_fusion.1.rest_12_), channel_id=1, source_target_pairs={{0,3},{1,2},{2,1},{3,0},{4,7},{5,6},{6,5},{7,4},{8,11},{9,10},{10,... | collective-permute-start | bytes 1572872 | tf_op jit(solution)/shard_map/ppermute | solution.py:365
  159.2 35.8 %collective-permute-start.27 = (bf16[4,4,32,512]{3,2,1,0:T(8,128)(2,1)}, bf16[4,4,32,512]{3,2,1,0:T(8,128)(2,1)}, u32[]{:S(2)}, u32[]{:S(2)}) collective-permute-start(bf16[4,4,32,512]{3,2,1,0:T(8,128)(2,1)} %pad_maximum_fusion.1.rest_12_), channel_id=1, source_target_pairs={{0,2},{1,3},{2,0},{3,1},{4,6},{5,7},{6,4},{7,5},{8,10},{9,11},{10,... | collective-permute-start | bytes 1572872 | tf_op jit(solution)/shard_map/ppermute | solution.py:365
  160.4 34.6 %collective-permute-start.26 = (bf16[4,4,32,512]{3,2,1,0:T(8,128)(2,1)}, bf16[4,4,32,512]{3,2,1,0:T(8,128)(2,1)}, u32[]{:S(2)}, u32[]{:S(2)}) collective-permute-start(bf16[4,4,32,512]{3,2,1,0:T(8,128)(2,1)} %pad_maximum_fusion.1.rest_12_), channel_id=1, source_target_pairs={{0,1},{1,0},{2,3},{3,2},{4,5},{5,4},{6,7},{7,6},{8,9},{9,8},{10,11... | collective-permute-start | bytes 1572872 | tf_op jit(solution)/shard_map/ppermute | solution.py:365
  161.8 33.7 %collective-permute-start.32 = (bf16[4,4,32,512]{3,2,1,0:T(8,128)(2,1)}, bf16[4,4,32,512]{3,2,1,0:T(8,128)(2,1)}, u32[]{:S(2)}, u32[]{:S(2)}) collective-permute-start(bf16[4,4,32,512]{3,2,1,0:T(8,128)(2,1)} %collective-permute-done.25.rest_11_), channel_id=1, source_target_pairs={{0,16},{16,0},{32,48},{48,32},{64,80},{80,64},{96,112},{112,96},{1... | collective-permute-start | bytes 1572872 | tf_op jit(solution)/shard_map/ppermute | solution.py:365
  173.1 26.0 %all-to-all-start.1 = ((bf16[16,64,512]{2,1,0:T(8,128)(2,1)}), bf16[16,64,512]{2,1,0:T(8,128)(2,1)S(1)}, u32[]{:S(2)}, u32[]{:S(2)}) async-start(bf16[16,64,512]{2,1,0:T(8,128)(2,1)} %bitcast.21), calls=%async_computation.1 | async-start | bytes 2097152 | tf_op jit(solution)/shard_map/all_to_all | solution.py:421
  177.3 18.9 %collective-permute-start.31 = (bf16[4,4,32,512]{3,2,1,0:T(8,128)(2,1)}, bf16[4,4,32,512]{3,2,1,0:T(8,128)(2,1)S(1)}, u32[]{:S(2)}, u32[]{:S(2)}) collective-permute-start(bf16[4,4,32,512]{3,2,1,0:T(8,128)(2,1)} %copy-done.13), channel_id=1, source_target_pairs={{0,16},{16,0},{32,48},{48,32},{64,80},{80,64},{96,112},{112,96},{1... | collective-permute-start | bytes 1572872 | tf_op jit(solution)/shard_map/ppermute | solution.py:365
  (39 other events, 468.7 us)

commit v5 on v4

--- a/solution.py
+++ b/solution.py
@@ -18,6 +18,10 @@
 EXP_SCALE = HD ** (-0.5) * math.log2(math.e)
 
 
+def grant(mebibytes):
+    return pltpu.CompilerParams(vmem_limit_bytes=mebibytes << 20)
+
+
 def in_place(x):
     return pltpu.with_memory_space_constraint(x, pltpu.VMEM)
 
@@ -40,6 +44,7 @@
         in_specs=[part, part, part],
         out_specs=pl.BlockSpec((step, cells, 3 * width), lambda i: (i, 0, 0)),
         out_shape=jax.ShapeDtypeStruct((span, cells, 3 * width), q.dtype),
+        compiler_params=grant(56),
         name="row_pack",
     )(q, k, v)
 
@@ -98,6 +103,7 @@
             ],
         ),
         out_shape=[jax.ShapeDtypeStruct(piece, q.dtype)] * peers,
+        compiler_params=grant(56),
         name="col_pack",
     )(me, q, k, v)
 
@@ -189,6 +195,7 @@
             out_specs=pl.BlockSpec((cells, HR * HD), lambda i, *_: (0, 0)),
         ),
         out_shape=jax.ShapeDtypeStruct((cells, HR * HD), x.dtype),
+        compiler_params=grant(56),
         name="row_attend",
     )(pattern.reshape(-1), count, in_place(x))
 
@@ -272,6 +279,7 @@
             ],
         ),
         out_shape=[jax.ShapeDtypeStruct(result, jnp.bfloat16)] * peers,
+        compiler_params=grant(56),
         name="col_attend",
     )(me, pattern.reshape(-1), count, pieces[0], *[in_place(p) for p in pieces[1:]])
 
@@ -296,7 +304,7 @@
                 for a in range(near):
                     for b in range(near):
                         for half, (x, z) in enumerate(((a, b), (b, a))):
-                            source = group[half * near + a].at[turn, b]
+                            source = group[half * near + a].at[b, turn]
                             span, wide = source.shape
                             at = ((at_x ^ x) * near + (at_z ^ z)) * span
                             target = line.at[
@@ -356,6 +364,7 @@
             ],
         ),
         out_shape=jax.ShapeDtypeStruct((span * cells, outs), jnp.bfloat16),
+        compiler_params=grant(56),
         name="project",
     )(place, in_place(row_out), pieces[0], *[in_place(p) for p in pieces[1:]], *weights)
 
@@ -373,19 +382,26 @@
     ]
 
 
-def join_kernel(*refs):
-    for i, ref in enumerate(refs[:-1]):
-        refs[-1][i] = ref[...]
-
-
-def join(parts):
-    return pl.pallas_call(
-        join_kernel,
-        in_specs=[pl.BlockSpec(memory_space=pltpu.VMEM)] * len(parts),
-        out_specs=pl.BlockSpec(memory_space=pltpu.VMEM),
-        out_shape=jax.ShapeDtypeStruct((len(parts),) + parts[0].shape, parts[0].dtype),
-        name="join",
-    )(*[in_place(p) for p in parts])
+def halve_kernel(*refs):
+    parts, (upper, lower) = refs[:-2], refs[-2:]
+    middle = upper.shape[2]
+    for i, part in enumerate(parts):
+        upper[i] = part[:, :middle]
+        lower[i] = part[:, middle:]
+
+
+def halve(parts):
+    span, channels = parts[0].shape
+    half = jax.ShapeDtypeStruct((len(parts), span, channels // 2), parts[0].dtype)
+    held = pl.BlockSpec(memory_space=pltpu.VMEM)
+    return pl.pallas_call(
+        halve_kernel,
+        in_specs=[held] * len(parts),
+        out_specs=[held, held],
+        out_shape=[half, half],
+        compiler_params=grant(56),
+        name="halve",
+    )(parts[0], *[in_place(p) for p in parts[1:]])
 
 
 def body(
@@ -402,19 +418,15 @@
     place = jnp.stack([lax.axis_index("rows"), lax.axis_index("cols")]).astype(jnp.int32)
 
     shard = out_weight.T
-    middle = shard.shape[1] // 2
-    upper, lower = shard[:, :middle], shard[:, middle:]
+    packed = row_pack(query_cells, key_cells, value_cells)
+    lines = lax.all_to_all(packed, "cols", 0, 0, tiled=True)
+    along_y = [shard] + by_xor(shard, "rows", (2, 4, 6))
+    sent = col_pack(me, query_cells, key_cells, value_cells, peers)
+    pieces = swap_pieces(sent)
+    upper, lower = halve(along_y)
     along_z = [upper] + by_xor(upper, "cols", (1, 2, 3))
     along_x = [lower] + by_xor(lower, "cols", (4, 8, 12))
-    packed = row_pack(query_cells, key_cells, value_cells)
-    lines = lax.all_to_all(packed, "cols", 0, 0, tiled=True)
-    held = join(along_z + along_x)
-    along_y = [held] + by_xor(held, "rows", (2, 4, 6))
-    sent = col_pack(me, query_cells, key_cells, value_cells, peers)
-    pieces = swap_pieces(sent)
-    near = len(along_z)
-    upper = jnp.stack([h[:near] for h in along_y])
-    lower = jnp.stack([h[near:] for h in along_y])
+    upper, lower = jnp.stack(along_z), jnp.stack(along_x)
     weights = [upper] + by_xor(upper, "cols", (4, 8, 12))
     weights += [lower] + by_xor(lower, "cols", (1, 2, 3))
     row_out = row_attend(pattern, count, lines)

time: 221 us -> 191 us (0.86)
  waiting for transfers between devices: 91.8 us -> 56.5 us
  local copies, waits for them, and re-layouts: 16.2 us -> 21.6 us
    ppermute x23, waiting for transfers between devices: 47 us -> 18.7 us  [by_xor(): lax.ppermute(x, axis, [(d, d ^ s) for d in range(size)])]
    ppermute x14, waiting for transfers between devices: 44.9 us -> 31.4 us  [swap_pieces(): lax.ppermute(pieces[s], 'rows', [(d, d ^ s) for d in range(peers)])]
    unnamed x49 -> x67, local copies, waits for them, and re-layouts: 9.43 us -> 19.4 us
    all_to_all x1, waiting for transfers between devices: 0.01 us -> 6.45 us  [body(): lax.all_to_all(row_out.reshape(row_span, col_span, -1), 'cols', 0, 0, til...]
    ppermute x23, starting transfers between devices: 35 us -> 29.8 us  [by_xor(): lax.ppermute(x, axis, [(d, d ^ s) for d in range(size)])]
    another operation x4 -> x0, local copies, waits for them, and re-layouts: 4.61 us -> none  [body(): lower = jnp.stack([h[near:] for h in along_y])]
  transfers between devices with their start and end apart: 39 -> 39, of which waited for: 18 -> 17; matrix products, arithmetic and copies ran while one was open for 4% -> 4% of each run, Pallas kernels for 10% -> 12%
where the time goes in v5:
time: 191 us; the launch traced here: 188 us
  starting transfers between devices  64 us (34%)
  waiting for transfers between devices  56.5 us (30%)
  Pallas kernels  40.9 us (21%)
  local copies, waits for them, and re-layouts  21.6 us (11%)
  other arithmetic  4.45 us (2%)
    ppermute x14, waiting for transfers between devices, swap_pieces(): lax.ppermute(pieces[s], 'rows', [(d, d ^ s) for d in range(peers)])  31.4 us
    ppermute x23, starting transfers between devices, by_xor(): lax.ppermute(x, axis, [(d, d ^ s) for d in range(size)])  29.8 us
    ppermute x14, starting transfers between devices, swap_pieces(): lax.ppermute(pieces[s], 'rows', [(d, d ^ s) for d in range(peers)])  20 us
    unnamed x67, local copies, waits for them, and re-layouts  19.4 us
    ppermute x23, waiting for transfers between devices, by_xor(): lax.ppermute(x, axis, [(d, d ^ s) for d in range(size)])  18.7 us
    pallas_call x1, Pallas kernels, project(): pl.pallas_call(functools.partial(project_kernel, peers=len(pieces), near=...  15 us
    all_to_all x1, starting transfers between devices, body(): lines = lax.all_to_all(packed, 'cols', 0, 0, tiled=True)  8.42 us
    pallas_call x1, Pallas kernels, row_attend(): pl.pallas_call(functools.partial(row_attend_kernel, chosen=chosen), grid_...  7.68 us
  transfers between devices with their start and end apart: 39, of which 17 were waited for; matrix products, arithmetic and copies ran while one was open for 4% of the time, Pallas kernels for 12%

profile of v5, /device:TPU:1, one launch (start us, length us, event | category | flops | bytes accessed | tf_op | source)
XLA Modules:
  0.0 187.7 jit_solution(5354174381421260546)
XLA Ops:
  0.0 4.2 %row_pack.1 = bf16[16,64,1536]{2,1,0:T(8,128)(2,1)} custom-call(bf16[16,64,1024]{2,1,0:T(8,128)(2,1)} %q_ref.3, bf16[16,64,1024]{2,1,0:T(8,128)(2,1)} %k_ref.3, bf16[16,64,1024]{2,1,0:T(8,128)(2,1)} %v_ref.3), custom_call_target="tpu_custom_call" | custom-call | tf_op jit(solution)/shard_map/row_pack/pallas_call | solution.py:41
  4.2 8.4 %all-to-all-start = ((bf16[16,64,1536]{2,1,0:T(8,128)(2,1)}), bf16[16,64,1536]{2,1,0:T(8,128)(2,1)S(1)}, u32[]{:S(2)}, u32[]{:S(2)}) async-start(bf16[16,64,1536]{2,1,0:T(8,128)(2,1)} %row_pack.1), calls=%async_computation | async-start | bytes 6291456 | tf_op jit(solution)/shard_map/all_to_all | solution.py:422
  12.6 6.9 %col_pack.1 = (bf16[8,16,1536]{2,1,0:T(8,128)(2,1)}, bf16[8,16,1536]{2,1,0:T(8,128)(2,1)}, bf16[8,16,1536]{2,1,0:T(8,128)(2,1)}, bf16[8,16,1536]{2,1,0:T(8,128)(...) custom-call(s32[1]{0:T(128)} %bitcast.me_ref, ...), custom_call_target="tpu_custom_call" | custom-call | tf_op jit(solution)/shard_map/col_pack/pallas_call | solution.py:92
  27.1 8.1 %collective-permute-done.15.refs_2_ = bf16[32,1024]{1,0:T(8,128)(2,1)S(1)} collective-permute-done((bf16[32,1024]{1,0:T(8,128)(2,1)S(1)}, bf16[32,1024]{1,0:T(8,128)(2,1)S(1)}, u32[]{:S(2)}, u32[]{:S(2)}) %collective-permute-start.15) | collective-permute-done | bytes 65568 | tf_op jit(solution)/shard_map/ppermute | solution.py:374
  35.6 4.3 %collective-permute-start.4 = (bf16[8,16,1536]{2,1,0:T(8,128)(2,1)}, bf16[8,16,1536]{2,1,0:T(8,128)(2,1)S(1)}, u32[]{:S(2)}, u32[]{:S(2)}) collective-permute-start(bf16[8,16,1536]{2,1,0:T(8,128)(2,1)} %get-tuple-element.28), channel_id=1, source_target_pairs={{0,80},{16,64},{32,112},{48,96},{64,16},{80,0},{96,48},{112,32},{1... | collective-permute-start | bytes 1179656 | tf_op jit(solution)/shard_map/ppermute | solution.py:380
  45.3 2.8 %collective-permute-start.19 = (bf16[4,32,512]{2,1,0:T(8,128)(2,1)}, bf16[4,32,512]{2,1,0:T(8,128)(2,1)S(1)}, u32[]{:S(2)}, u32[]{:S(2)}) collective-permute-start(bf16[4,32,512]{2,1,0:T(8,128)(2,1)} %get-tuple-element.39), channel_id=1, source_target_pairs={{0,3},{1,2},{2,1},{3,0},{4,7},{5,6},{6,5},{7,4},{8,11},{9,10},{10,... | collective-permute-start | bytes 393224 | tf_op jit(solution)/shard_map/ppermute | solution.py:374
  48.1 5.4 %collective-permute-done.3.rest_4_ = bf16[8,16,1536]{2,1,0:T(8,128)(2,1)S(1)} collective-permute-done((bf16[8,16,1536]{2,1,0:T(8,128)(2,1)}, bf16[8,16,1536]{2,1,0:T(8,128)(2,1)S(1)}, u32[]{:S(2)}, u32[]{:S(2)}) %collective-permute-start.3) | collective-permute-done | bytes 393248 | tf_op jit(solution)/shard_map/ppermute | solution.py:380
  54.3 3.1 %collective-permute-start.18 = (bf16[4,32,512]{2,1,0:T(8,128)(2,1)}, bf16[4,32,512]{2,1,0:T(8,128)(2,1)}, u32[]{:S(2)}, u32[]{:S(2)}) collective-permute-start(bf16[4,32,512]{2,1,0:T(8,128)(2,1)} %get-tuple-element.39), channel_id=1, source_target_pairs={{0,2},{1,3},{2,0},{3,1},{4,6},{5,7},{6,4},{7,5},{8,10},{9,11},{10,... | collective-permute-start | bytes 393224 | tf_op jit(solution)/shard_map/ppermute | solution.py:374
  57.4 4.9 %collective-permute-done.4.rest_5_ = bf16[8,16,1536]{2,1,0:T(8,128)(2,1)S(1)} collective-permute-done((bf16[8,16,1536]{2,1,0:T(8,128)(2,1)}, bf16[8,16,1536]{2,1,0:T(8,128)(2,1)S(1)}, u32[]{:S(2)}, u32[]{:S(2)}) %collective-permute-start.4) | collective-permute-done | bytes 393248 | tf_op jit(solution)/shard_map/ppermute | solution.py:380
  63.0 2.9 %collective-permute-start.25 = (bf16[4,32,512]{2,1,0:T(8,128)(2,1)}, bf16[4,32,512]{2,1,0:T(8,128)(2,1)}, u32[]{:S(2)}, u32[]{:S(2)}) collective-permute-start(bf16[4,32,512]{2,1,0:T(8,128)(2,1)} %get-tuple-element.40), channel_id=1, source_target_pairs={{0,12},{1,13},{2,14},{3,15},{4,8},{5,9},{6,10},{7,11},{8,4},{9,5},... | collective-permute-start | bytes 393224 | tf_op jit(solution)/shard_map/ppermute | solution.py:374
  65.8 4.3 %collective-permute-done.5.rest_6_ = bf16[8,16,1536]{2,1,0:T(8,128)(2,1)S(1)} collective-permute-done((bf16[8,16,1536]{2,1,0:T(8,128)(2,1)}, bf16[8,16,1536]{2,1,0:T(8,128)(2,1)S(1)}, u32[]{:S(2)}, u32[]{:S(2)}) %collective-permute-start.5) | collective-permute-done | bytes 393248 | tf_op jit(solution)/shard_map/ppermute | solution.py:380
  70.9 2.7 %collective-permute-start.24 = (bf16[4,32,512]{2,1,0:T(8,128)(2,1)}, bf16[4,32,512]{2,1,0:T(8,128)(2,1)}, u32[]{:S(2)}, u32[]{:S(2)}) collective-permute-start(bf16[4,32,512]{2,1,0:T(8,128)(2,1)} %get-tuple-element.40), channel_id=1, source_target_pairs={{0,8},{1,9},{2,10},{3,11},{4,12},{5,13},{6,14},{7,15},{8,0},{9,1},... | collective-permute-start | bytes 393224 | tf_op jit(solution)/shard_map/ppermute | solution.py:374
  73.6 3.2 %collective-permute-done.6.rest_7_ = bf16[8,16,1536]{2,1,0:T(8,128)(2,1)S(1)} collective-permute-done((bf16[8,16,1536]{2,1,0:T(8,128)(2,1)}, bf16[8,16,1536]{2,1,0:T(8,128)(2,1)S(1)}, u32[]{:S(2)}, u32[]{:S(2)}) %collective-permute-start.6) | collective-permute-done | bytes 393248 | tf_op jit(solution)/shard_map/ppermute | solution.py:380
  87.1 5.5 %col_attend.1 = (bf16[16,8,512]{2,1,0:T(8,128)(2,1)}, bf16[16,8,512]{2,1,0:T(8,128)(2,1)}, bf16[16,8,512]{2,1,0:T(8,128)(2,1)}, bf16[16,8,512]{2,1,0:T(8,128)(2,...) custom-call(s32[1]{0:T(128)} %bitcast.me_ref, ...), custom_call_target="tpu_custom_call" | custom-call | tf_op jit(solution)/shard_map/col_attend/pallas_call | solution.py:269
  107.5 2.0 %collective-permute-start.11 = (bf16[16,8,512]{2,1,0:T(8,128)(2,1)}, bf16[16,8,512]{2,1,0:T(8,128)(2,1)S(1)}, u32[]{:S(2)}, u32[]{:S(2)}) collective-permute-start(bf16[16,8,512]{2,1,0:T(8,128)(2,1)} %get-tuple-element.36), channel_id=1, source_target_pairs={{0,80},{16,64},{32,112},{48,96},{64,16},{80,0},{96,48},{112,32},{1... | collective-permute-start | bytes 393224 | tf_op jit(solution)/shard_map/ppermute | solution.py:380
  109.5 5.7 %collective-permute-done.11.rest_5_ = bf16[16,8,512]{2,1,0:T(8,128)(2,1)S(1)} collective-permute-done((bf16[16,8,512]{2,1,0:T(8,128)(2,1)}, bf16[16,8,512]{2,1,0:T(8,128)(2,1)S(1)}, u32[]{:S(2)}, u32[]{:S(2)}) %collective-permute-start.11) | collective-permute-done | bytes 131104 | tf_op jit(solution)/shard_map/ppermute | solution.py:380
  115.8 2.0 %collective-permute-start.12 = (bf16[16,8,512]{2,1,0:T(8,128)(2,1)}, bf16[16,8,512]{2,1,0:T(8,128)(2,1)S(1)}, u32[]{:S(2)}, u32[]{:S(2)}) collective-permute-start(bf16[16,8,512]{2,1,0:T(8,128)(2,1)} %get-tuple-element.37), channel_id=1, source_target_pairs={{0,96},{16,112},{32,64},{48,80},{64,32},{80,48},{96,0},{112,16},{1... | collective-permute-start | bytes 393224 | tf_op jit(solution)/shard_map/ppermute | solution.py:380
  117.8 4.0 %collective-permute-done.12.rest_6_ = bf16[16,8,512]{2,1,0:T(8,128)(2,1)S(1)} collective-permute-done((bf16[16,8,512]{2,1,0:T(8,128)(2,1)}, bf16[16,8,512]{2,1,0:T(8,128)(2,1)S(1)}, u32[]{:S(2)}, u32[]{:S(2)}) %collective-permute-start.12) | collective-permute-done | bytes 131104 | tf_op jit(solution)/shard_map/ppermute | solution.py:380
  122.5 3.2 %collective-permute-start.13 = (bf16[16,8,512]{2,1,0:T(8,128)(2,1)}, bf16[16,8,512]{2,1,0:T(8,128)(2,1)}, u32[]{:S(2)}, u32[]{:S(2)}) collective-permute-start(bf16[16,8,512]{2,1,0:T(8,128)(2,1)} %get-tuple-element.38), channel_id=1, source_target_pairs={{0,112},{16,96},{32,80},{48,64},{64,48},{80,32},{96,16},{112,0},{1... | collective-permute-start | bytes 393224 | tf_op jit(solution)/shard_map/ppermute | solution.py:380
  135.6 7.7 %row_attend.1 = bf16[1024,512]{1,0:T(8,128)(2,1)} custom-call(s32[192]{0:T(256)} %reshape.13.pattern_ref, s32[1]{0:T(128)} %dynamic_slice.7.count_ref, bf16[16,64,1536]{2,1,0:T(8,128)(2,1)S(1)} %all-to-all-done.x_ref), custom_call_target="tpu_custom_call" | custom-call | tf_op jit(solution)/shard_map/row_attend/pallas_call | solution.py:189
  143.3 5.8 %all-to-all-start.1 = ((bf16[16,64,512]{2,1,0:T(8,128)(2,1)}), bf16[16,64,512]{2,1,0:T(8,128)(2,1)S(1)}, u32[]{:S(2)}, u32[]{:S(2)}) async-start(bf16[16,64,512]{2,1,0:T(8,128)(2,1)} %bitcast.13), calls=%async_computation.1 | async-start | bytes 2097152 | tf_op jit(solution)/shard_map/all_to_all | solution.py:433
  149.6 7.3 %collective-permute-done.22.rest_11_ = bf16[4,4,32,512]{3,2,1,0:T(8,128)(2,1)} collective-permute-done((bf16[4,4,32,512]{3,2,1,0:T(8,128)(2,1)}, bf16[4,4,32,512]{3,2,1,0:T(8,128)(2,1)}, u32[]{:S(2)}, u32[]{:S(2)}) %collective-permute-start.22) | collective-permute-done | bytes 524320 | tf_op jit(solution)/shard_map/ppermute | solution.py:374
  162.4 6.5 %all-to-all-done.1.row_ref = bf16[16,64,512]{2,1,0:T(8,128)(2,1)S(1)} async-done(((bf16[16,64,512]{2,1,0:T(8,128)(2,1)}), bf16[16,64,512]{2,1,0:T(8,128)(2,1)S(1)}, u32[]{:S(2)}, u32[]{:S(2)}) %all-to-all-start.1) | async-done | bytes 1048608 | tf_op jit(solution)/shard_map/all_to_all | solution.py:433
  172.5 15.0 %project.1 = bf16[1024,4096]{1,0:T(8,128)(2,1)} custom-call(s32[2]{0:T(128)} %pad_add_fusion.place, bf16[16,64,512]{2,1,0:T(8,128)(2,1)S(1)} %all-to-all-done.1.row_ref, bf16[16,8,512]{2,1,0:T(8,128)(2,1)} %get-tuple-element.31.rest_0_, bf16[16,8,512]{2,1,0:T(8,128)(2,1)S(1)} %collective-permute-done.7.rest_1_, ...), custom_call_target="tpu_custom_call" | custom-call | tf_op jit(solution)/shard_map/project/pallas_call | solution.py:352
  (135 shorter events, 61.5 us)
Async XLA Ops:
  4.2 131.4 %all-to-all-start = ((bf16[16,64,1536]{2,1,0:T(8,128)(2,1)}), bf16[16,64,1536]{2,1,0:T(8,128)(2,1)S(1)}, u32[]{:S(2)}, u32[]{:S(2)}) async-start(bf16[16,64,1536]{2,1,0:T(8,128)(2,1)} %row_pack.1), calls=%async_computation | async-start | bytes 6291456 | tf_op jit(solution)/shard_map/all_to_all | solution.py:422
  19.5 20.3 %collective-permute-start = (bf16[8,16,1536]{2,1,0:T(8,128)(2,1)}, bf16[8,16,1536]{2,1,0:T(8,128)(2,1)S(1)}, u32[]{:S(2)}, u32[]{:S(2)}) collective-permute-start(bf16[8,16,1536]{2,1,0:T(8,128)(2,1)} %get-tuple-element.24), channel_id=1, source_target_pairs={{0,16},{16,0},{32,48},{48,32},{64,80},{80,64},{96,112},{112,96},{1... | collective-permute-start | bytes 1179656 | tf_op jit(solution)/shard_map/ppermute | solution.py:380
  20.6 20.0 %collective-permute-start.1 = (bf16[8,16,1536]{2,1,0:T(8,128)(2,1)}, bf16[8,16,1536]{2,1,0:T(8,128)(2,1)S(1)}, u32[]{:S(2)}, u32[]{:S(2)}) collective-permute-start(bf16[8,16,1536]{2,1,0:T(8,128)(2,1)} %get-tuple-element.25), channel_id=1, source_target_pairs={{0,32},{16,48},{32,0},{48,16},{64,96},{80,112},{96,64},{112,80},{1... | collective-permute-start | bytes 1179656 | tf_op jit(solution)/shard_map/ppermute | solution.py:380
  23.8 11.4 %collective-permute-start.15 = (bf16[32,1024]{1,0:T(8,128)(2,1)S(1)}, bf16[32,1024]{1,0:T(8,128)(2,1)S(1)}, u32[]{:S(2)}, u32[]{:S(2)}) collective-permute-start(bf16[32,1024]{1,0:T(8,128)(2,1)S(1)} %bitcast.19), channel_id=1, source_target_pairs={{0,64},{16,80},{32,96},{48,112},{64,0},{80,16},{96,32},{112,48},{1... | collective-permute-start | bytes 196616 | tf_op jit(solution)/shard_map/ppermute | solution.py:374
  26.5 18.0 %collective-permute-start.2 = (bf16[8,16,1536]{2,1,0:T(8,128)(2,1)}, bf16[8,16,1536]{2,1,0:T(8,128)(2,1)S(1)}, u32[]{:S(2)}, u32[]{:S(2)}) collective-permute-start(bf16[8,16,1536]{2,1,0:T(8,128)(2,1)} %get-tuple-element.26), channel_id=1, source_target_pairs={{0,48},{16,32},{32,16},{48,0},{64,112},{80,96},{96,80},{112,64},{1... | collective-permute-start | bytes 1179656 | tf_op jit(solution)/shard_map/ppermute | solution.py:380
  35.2 18.3 %collective-permute-start.3 = (bf16[8,16,1536]{2,1,0:T(8,128)(2,1)}, bf16[8,16,1536]{2,1,0:T(8,128)(2,1)S(1)}, u32[]{:S(2)}, u32[]{:S(2)}) collective-permute-start(bf16[8,16,1536]{2,1,0:T(8,128)(2,1)} %get-tuple-element.27), channel_id=1, source_target_pairs={{0,64},{16,80},{32,96},{48,112},{64,0},{80,16},{96,32},{112,48},{1... | collective-permute-start | bytes 1179656 | tf_op jit(solution)/shard_map/ppermute | solution.py:380
  35.6 26.7 %collective-permute-start.4 = (bf16[8,16,1536]{2,1,0:T(8,128)(2,1)}, bf16[8,16,1536]{2,1,0:T(8,128)(2,1)S(1)}, u32[]{:S(2)}, u32[]{:S(2)}) collective-permute-start(bf16[8,16,1536]{2,1,0:T(8,128)(2,1)} %get-tuple-element.28), channel_id=1, source_target_pairs={{0,80},{16,64},{32,112},{48,96},{64,16},{80,0},{96,48},{112,32},{1... | collective-permute-start | bytes 1179656 | tf_op jit(solution)/shard_map/ppermute | solution.py:380
  40.6 29.5 %collective-permute-start.5 = (bf16[8,16,1536]{2,1,0:T(8,128)(2,1)}, bf16[8,16,1536]{2,1,0:T(8,128)(2,1)S(1)}, u32[]{:S(2)}, u32[]{:S(2)}) collective-permute-start(bf16[8,16,1536]{2,1,0:T(8,128)(2,1)} %get-tuple-element.29), channel_id=1, source_target_pairs={{0,96},{16,112},{32,64},{48,80},{64,32},{80,48},{96,0},{112,16},{1... | collective-permute-start | bytes 1179656 | tf_op jit(solution)/shard_map/ppermute | solution.py:380
  41.4 35.4 %collective-permute-start.6 = (bf16[8,16,1536]{2,1,0:T(8,128)(2,1)}, bf16[8,16,1536]{2,1,0:T(8,128)(2,1)S(1)}, u32[]{:S(2)}, u32[]{:S(2)}) collective-permute-start(bf16[8,16,1536]{2,1,0:T(8,128)(2,1)} %get-tuple-element.30), channel_id=1, source_target_pairs={{0,112},{16,96},{32,80},{48,64},{64,48},{80,32},{96,16},{112,0},{1... | collective-permute-start | bytes 1179656 | tf_op jit(solution)/shard_map/ppermute | solution.py:380
  45.3 47.4 %collective-permute-start.19 = (bf16[4,32,512]{2,1,0:T(8,128)(2,1)}, bf16[4,32,512]{2,1,0:T(8,128)(2,1)S(1)}, u32[]{:S(2)}, u32[]{:S(2)}) collective-permute-start(bf16[4,32,512]{2,1,0:T(8,128)(2,1)} %get-tuple-element.39), channel_id=1, source_target_pairs={{0,3},{1,2},{2,1},{3,0},{4,7},{5,6},{6,5},{7,4},{8,11},{9,10},{10,... | collective-permute-start | bytes 393224 | tf_op jit(solution)/shard_map/ppermute | solution.py:374
  54.3 39.6 %collective-permute-start.18 = (bf16[4,32,512]{2,1,0:T(8,128)(2,1)}, bf16[4,32,512]{2,1,0:T(8,128)(2,1)}, u32[]{:S(2)}, u32[]{:S(2)}) collective-permute-start(bf16[4,32,512]{2,1,0:T(8,128)(2,1)} %get-tuple-element.39), channel_id=1, source_target_pairs={{0,2},{1,3},{2,0},{3,1},{4,6},{5,7},{6,4},{7,5},{8,10},{9,11},{10,... | collective-permute-start | bytes 393224 | tf_op jit(solution)/shard_map/ppermute | solution.py:374
  63.0 32.7 %collective-permute-start.25 = (bf16[4,32,512]{2,1,0:T(8,128)(2,1)}, bf16[4,32,512]{2,1,0:T(8,128)(2,1)}, u32[]{:S(2)}, u32[]{:S(2)}) collective-permute-start(bf16[4,32,512]{2,1,0:T(8,128)(2,1)} %get-tuple-element.40), channel_id=1, source_target_pairs={{0,12},{1,13},{2,14},{3,15},{4,8},{5,9},{6,10},{7,11},{8,4},{9,5},... | collective-permute-start | bytes 393224 | tf_op jit(solution)/shard_map/ppermute | solution.py:374
  70.9 24.8 %collective-permute-start.24 = (bf16[4,32,512]{2,1,0:T(8,128)(2,1)}, bf16[4,32,512]{2,1,0:T(8,128)(2,1)}, u32[]{:S(2)}, u32[]{:S(2)}) collective-permute-start(bf16[4,32,512]{2,1,0:T(8,128)(2,1)} %get-tuple-element.40), channel_id=1, source_target_pairs={{0,8},{1,9},{2,10},{3,11},{4,12},{5,13},{6,14},{7,15},{8,0},{9,1},... | collective-permute-start | bytes 393224 | tf_op jit(solution)/shard_map/ppermute | solution.py:374
  77.6 19.8 %collective-permute-start.23 = (bf16[4,32,512]{2,1,0:T(8,128)(2,1)}, bf16[4,32,512]{2,1,0:T(8,128)(2,1)}, u32[]{:S(2)}, u32[]{:S(2)}) collective-permute-start(bf16[4,32,512]{2,1,0:T(8,128)(2,1)} %get-tuple-element.40), channel_id=1, source_target_pairs={{0,4},{1,5},{2,6},{3,7},{4,0},{5,1},{6,2},{7,3},{8,12},{9,13},{10,... | collective-permute-start | bytes 393224 | tf_op jit(solution)/shard_map/ppermute | solution.py:374
  99.5 31.2 %collective-permute-start.33 = (bf16[4,4,32,512]{3,2,1,0:T(8,128)(2,1)}, bf16[4,4,32,512]{3,2,1,0:T(8,128)(2,1)}, u32[]{:S(2)}, u32[]{:S(2)}) collective-permute-start(bf16[4,4,32,512]{3,2,1,0:T(8,128)(2,1)} %pad_maximum_fusion.1.rest_12_), channel_id=1, source_target_pairs={{0,16},{16,0},{32,48},{48,32},{64,80},{80,64},{96,112},{112,96},{1... | collective-permute-start | bytes 1572872 | tf_op jit(solution)/shard_map/ppermute | solution.py:374
  100.2 32.3 %collective-permute-start.28 = (bf16[4,4,32,512]{3,2,1,0:T(8,128)(2,1)}, bf16[4,4,32,512]{3,2,1,0:T(8,128)(2,1)}, u32[]{:S(2)}, u32[]{:S(2)}) collective-permute-start(bf16[4,4,32,512]{3,2,1,0:T(8,128)(2,1)} %pad_maximum_fusion.1.rest_12_), channel_id=1, source_target_pairs={{0,3},{1,2},{2,1},{3,0},{4,7},{5,6},{6,5},{7,4},{8,11},{9,10},{10,... | collective-permute-start | bytes 1572872 | tf_op jit(solution)/shard_map/ppermute | solution.py:374
  102.0 31.2 %collective-permute-start.27 = (bf16[4,4,32,512]{3,2,1,0:T(8,128)(2,1)}, bf16[4,4,32,512]{3,2,1,0:T(8,128)(2,1)}, u32[]{:S(2)}, u32[]{:S(2)}) collective-permute-start(bf16[4,4,32,512]{3,2,1,0:T(8,128)(2,1)} %pad_maximum_fusion.1.rest_12_), channel_id=1, source_target_pairs={{0,2},{1,3},{2,0},{3,1},{4,6},{5,7},{6,4},{7,5},{8,10},{9,11},{10,... | collective-permute-start | bytes 1572872 | tf_op jit(solution)/shard_map/ppermute | solution.py:374
  105.1 28.9 %collective-permute-start.26 = (bf16[4,4,32,512]{3,2,1,0:T(8,128)(2,1)}, bf16[4,4,32,512]{3,2,1,0:T(8,128)(2,1)}, u32[]{:S(2)}, u32[]{:S(2)}) collective-permute-start(bf16[4,4,32,512]{3,2,1,0:T(8,128)(2,1)} %pad_maximum_fusion.1.rest_12_), channel_id=1, source_target_pairs={{0,1},{1,0},{2,3},{3,2},{4,5},{5,4},{6,7},{7,6},{8,9},{9,8},{10,11... | collective-permute-start | bytes 1572872 | tf_op jit(solution)/shard_map/ppermute | solution.py:374
  130.0 19.1 %collective-permute-start.29 = (bf16[4,4,32,512]{3,2,1,0:T(8,128)(2,1)}, bf16[4,4,32,512]{3,2,1,0:T(8,128)(2,1)}, u32[]{:S(2)}, u32[]{:S(2)}) collective-permute-start(bf16[4,4,32,512]{3,2,1,0:T(8,128)(2,1)} %pad_maximum_fusion.rest_8_), channel_id=1, source_target_pairs={{0,16},{16,0},{32,48},{48,32},{64,80},{80,64},{96,112},{112,96},{1... | collective-permute-start | bytes 1572872 | tf_op jit(solution)/shard_map/ppermute | solution.py:374
  130.7 26.2 %collective-permute-start.22 = (bf16[4,4,32,512]{3,2,1,0:T(8,128)(2,1)}, bf16[4,4,32,512]{3,2,1,0:T(8,128)(2,1)}, u32[]{:S(2)}, u32[]{:S(2)}) collective-permute-start(bf16[4,4,32,512]{3,2,1,0:T(8,128)(2,1)} %pad_maximum_fusion.rest_8_), channel_id=1, source_target_pairs={{0,12},{1,13},{2,14},{3,15},{4,8},{5,9},{6,10},{7,11},{8,4},{9,5},... | collective-permute-start | bytes 1572872 | tf_op jit(solution)/shard_map/ppermute | solution.py:374
  132.5 25.8 %collective-permute-start.21 = (bf16[4,4,32,512]{3,2,1,0:T(8,128)(2,1)}, bf16[4,4,32,512]{3,2,1,0:T(8,128)(2,1)}, u32[]{:S(2)}, u32[]{:S(2)}) collective-permute-start(bf16[4,4,32,512]{3,2,1,0:T(8,128)(2,1)} %pad_maximum_fusion.rest_8_), channel_id=1, source_target_pairs={{0,8},{1,9},{2,10},{3,11},{4,12},{5,13},{6,14},{7,15},{8,0},{9,1},... | collective-permute-start | bytes 1572872 | tf_op jit(solution)/shard_map/ppermute | solution.py:374
  133.2 25.1 %collective-permute-start.20 = (bf16[4,4,32,512]{3,2,1,0:T(8,128)(2,1)}, bf16[4,4,32,512]{3,2,1,0:T(8,128)(2,1)}, u32[]{:S(2)}, u32[]{:S(2)}) collective-permute-start(bf16[4,4,32,512]{3,2,1,0:T(8,128)(2,1)} %pad_maximum_fusion.rest_8_), channel_id=1, source_target_pairs={{0,4},{1,5},{2,6},{3,7},{4,0},{5,1},{6,2},{7,3},{8,12},{9,13},{10,... | collective-permute-start | bytes 1572872 | tf_op jit(solution)/shard_map/ppermute | solution.py:374
  134.0 25.2 %collective-permute-start.36 = (bf16[4,4,32,512]{3,2,1,0:T(8,128)(2,1)}, bf16[4,4,32,512]{3,2,1,0:T(8,128)(2,1)}, u32[]{:S(2)}, u32[]{:S(2)}) collective-permute-start(bf16[4,4,32,512]{3,2,1,0:T(8,128)(2,1)} %collective-permute-done.28.rest_15_), channel_id=1, source_target_pairs={{0,16},{16,0},{32,48},{48,32},{64,80},{80,64},{96,112},{112,96},{1... | collective-permute-start | bytes 1572872 | tf_op jit(solution)/shard_map/ppermute | solution.py:374
  143.3 25.6 %all-to-all-start.1 = ((bf16[16,64,512]{2,1,0:T(8,128)(2,1)}), bf16[16,64,512]{2,1,0:T(8,128)(2,1)S(1)}, u32[]{:S(2)}, u32[]{:S(2)}) async-start(bf16[16,64,512]{2,1,0:T(8,128)(2,1)} %bitcast.13), calls=%async_computation.1 | async-start | bytes 2097152 | tf_op jit(solution)/shard_map/all_to_all | solution.py:433
  (48 other events, 495.4 us)

commit v6 on v5

--- a/solution.py
+++ b/solution.py
@@ -284,89 +284,119 @@
     )(me, pattern.reshape(-1), count, pieces[0], *[in_place(p) for p in pieces[1:]])
 
 
-def project_kernel(place, row_ref, *rest, peers, near):
-    pieces, (out_ref, heads, line, sem) = rest[:peers], rest[-4:]
-    weights = rest[peers:-4]
-    width = HR * HD
-    own = pieces[0].shape[1]
-    me, plane = place[0], place[1]
+def fetch_weights(plane, weights, line, sem, step, slot, flipped):
+    near = weights[0].shape[0]
+    at_x, at_z = lax.div(plane, near), lax.rem(plane, near)
+    turn = lax.rem(step, near)
+    for core in range(2):
+
+        @pl.when(lax.div(step, near) == core)
+        def _(core=core):
+            for a in range(near):
+                for b in range(near):
+                    x, z = (b, a) if flipped else (a, b)
+                    source = weights[core * near + a].at[b, turn]
+                    span = source.shape[0]
+                    at = pl.multiple_of(((at_x ^ x) * near + (at_z ^ z)) * span, span)
+                    target = line.at[slot, pl.ds(at, span), :]
+                    pltpu.make_async_copy(source, target, sem.at[slot]).start()
+
+
+def project_step(plane, weights, line, sem, flipped, heads):
     step = pl.program_id(0)
     slot = lax.rem(step, 2)
-    at_x, at_z = lax.div(plane, near), lax.rem(plane, near)
-
-    def fetch(step, slot):
-        turn = lax.rem(step, near)
-        for core in range(2):
-
-            @pl.when(lax.div(step, near) == core)
-            def _(core=core):
-                group = weights[2 * near * core : 2 * near * (core + 1)]
-                for a in range(near):
-                    for b in range(near):
-                        for half, (x, z) in enumerate(((a, b), (b, a))):
-                            source = group[half * near + a].at[b, turn]
-                            span, wide = source.shape
-                            at = ((at_x ^ x) * near + (at_z ^ z)) * span
-                            target = line.at[
-                                slot,
-                                pl.ds(pl.multiple_of(at, span), span),
-                                pl.ds(half * wide, wide),
-                            ]
-                            pltpu.make_async_copy(source, target, sem.at[slot]).start()
 
     @pl.when(step == 0)
     def _():
-        fetch(step, slot)
+        fetch_weights(plane, weights, line, sem, step, slot, flipped)
+
+    @pl.when(step + 1 < pl.num_programs(0))
+    def _():
+        fetch_weights(plane, weights, line, sem, step + 1, 1 - slot, flipped)
+
+    pltpu.make_async_copy(line.at[slot], line.at[slot], sem.at[slot]).wait()
+    return lax.dot_general(
+        heads[...].reshape(-1, heads.shape[2]),
+        line[slot],
+        (((1,), (1,)), ((), ())),
+        preferred_element_type=jnp.float32,
+    )
+
+
+def project_rows_kernel(place, heads, *rest):
+    weights, (out_ref, line, sem) = rest[:-3], rest[-3:]
+    out_ref[...] = project_step(place[1], weights, line, sem, False, heads)
+
+
+def project_cols_kernel(place, *rest, peers):
+    pieces, weights = rest[:peers], rest[peers:-5]
+    partial_ref, out_ref, heads, line, sem = rest[-5:]
+    own = pieces[0].shape[1]
+
+    @pl.when(pl.program_id(0) == 0)
+    def _():
+        me = place[0]
         odd = lax.rem(me, 2) == 1
-        heads[:, :, 0:width] = row_ref[...]
         for s in range(0, peers, 2):
             a = pieces[s][...].astype(jnp.float32)
             b = pieces[s + 1][...].astype(jnp.float32)
             both = jnp.concatenate([jnp.where(odd, b, a), jnp.where(odd, a, b)], axis=1)
             at = pl.multiple_of(((me ^ s) // 2) * 2 * own, 2 * own)
-            heads[:, pl.ds(at, 2 * own), width:] = both.astype(jnp.bfloat16)
-
-    @pl.when(step + 1 < pl.num_programs(0))
-    def _():
-        fetch(step + 1, 1 - slot)
-
-    pltpu.make_async_copy(line.at[slot], line.at[slot], sem.at[slot]).wait()
-    out_ref[...] = lax.dot_general(
-        heads[...].reshape(-1, heads.shape[2]),
-        line[slot],
-        (((1,), (1,)), ((), ())),
-        preferred_element_type=jnp.float32,
-    ).astype(jnp.bfloat16)
-
-
-def project(place, row_out, pieces, weights, outs):
-    span, cells, _ = row_out.shape
-    turns, near, part, wide = weights[0].shape
-    channels = 2 * wide
+            heads[:, pl.ds(at, 2 * own), :] = both.astype(jnp.bfloat16)
+
+    added = project_step(place[1], weights, line, sem, True, heads)
+    out_ref[...] = (partial_ref[...] + added).astype(jnp.bfloat16)
+
+
+def project_sizes(weights):
+    near, turns, part, width = weights[0].shape
     tile = near * near * part
-    held = pl.BlockSpec(memory_space=pltpu.VMEM)
 
     def target(j, at):
         return 0, at[0] ^ (2 * lax.rem(j, turns) + lax.div(j, turns))
 
-    return pl.pallas_call(
-        functools.partial(project_kernel, peers=len(pieces), near=near),
+    scratch = [pltpu.VMEM((2, tile, width), jnp.bfloat16), pltpu.SemaphoreType.DMA((2,))]
+    return 2 * turns, tile, target, scratch
+
+
+def project_rows(place, row_out, weights, outs):
+    span, cells, _ = row_out.shape
+    steps, tile, target, scratch = project_sizes(weights)
+    return pl.pallas_call(
+        project_rows_kernel,
         grid_spec=pltpu.PrefetchScalarGridSpec(
             num_scalar_prefetch=1,
-            grid=(2 * turns,),
-            in_specs=[held] * (1 + len(pieces))
+            grid=(steps,),
+            in_specs=[pl.BlockSpec(memory_space=pltpu.VMEM)]
             + [pl.BlockSpec(memory_space=pl.ANY)] * len(weights),
             out_specs=pl.BlockSpec((span * cells, tile), target),
-            scratch_shapes=[
-                pltpu.VMEM((span, cells, channels), jnp.bfloat16),
-                pltpu.VMEM((2, tile, channels), jnp.bfloat16),
-                pltpu.SemaphoreType.DMA((2,)),
-            ],
+            scratch_shapes=scratch,
         ),
-        out_shape=jax.ShapeDtypeStruct((span * cells, outs), jnp.bfloat16),
-        compiler_params=grant(56),
-        name="project",
-    )(place, in_place(row_out), pieces[0], *[in_place(p) for p in pieces[1:]], *weights)
+        out_shape=jax.ShapeDtypeStruct((span * cells, outs), jnp.float32),
+        compiler_params=grant(56),
+        name="project_rows",
+    )(place, in_place(row_out), *weights)
+
+
+def project_cols(place, pieces, weights, partial):
+    span, own, width = pieces[0].shape
+    steps, tile, target, scratch = project_sizes(weights)
+    block = pl.BlockSpec((partial.shape[0], tile), target)
+    return pl.pallas_call(
+        functools.partial(project_cols_kernel, peers=len(pieces)),
+        grid_spec=pltpu.PrefetchScalarGridSpec(
+            num_scalar_prefetch=1,
+            grid=(steps,),
+            in_specs=[pl.BlockSpec(memory_space=pltpu.VMEM)] * len(pieces)
+            + [pl.BlockSpec(memory_space=pl.ANY)] * len(weights)
+            + [block],
+            out_specs=block,
+            scratch_shapes=[pltpu.VMEM((span, own * len(pieces), width), jnp.bfloat16)] + scratch,
+        ),
+        out_shape=jax.ShapeDtypeStruct(partial.shape, jnp.bfloat16),
+        compiler_params=grant(56),
+        name="project_cols",
+    )(place, pieces[0], *[in_place(p) for p in pieces[1:]], *weights, partial)
 
 
 def by_xor(x, axis, masks):
@@ -380,6 +410,26 @@
         lax.ppermute(pieces[s], "rows", [(d, d ^ s) for d in range(peers)])
         for s in range(1, peers)
     ]
+
+
+def join_kernel(*refs):
+    parts, outs = refs[:-2], refs[-2:]
+    each = len(parts) // 2
+    for i, part in enumerate(parts):
+        outs[i // each][i % each] = part[...]
+
+
+def join_both(first, second):
+    held = pl.BlockSpec(memory_space=pltpu.VMEM)
+    whole = jax.ShapeDtypeStruct((len(first),) + first[0].shape, first[0].dtype)
+    return pl.pallas_call(
+        join_kernel,
+        in_specs=[held] * (len(first) + len(second)),
+        out_specs=[held, held],
+        out_shape=[whole, whole],
+        compiler_params=grant(56),
+        name="join_both",
+    )(*[in_place(p) for p in first], *[in_place(p) for p in second])
 
 
 def halve_kernel(*refs):
@@ -426,16 +476,18 @@
     upper, lower = halve(along_y)
     along_z = [upper] + by_xor(upper, "cols", (1, 2, 3))
     along_x = [lower] + by_xor(lower, "cols", (4, 8, 12))
-    upper, lower = jnp.stack(along_z), jnp.stack(along_x)
-    weights = [upper] + by_xor(upper, "cols", (4, 8, 12))
-    weights += [lower] + by_xor(lower, "cols", (1, 2, 3))
+    upper, lower = join_both(along_z, along_x)
+    uppers = [upper] + by_xor(upper, "cols", (4, 8, 12))
+    lowers = [lower] + by_xor(lower, "cols", (1, 2, 3))
     row_out = row_attend(pattern, count, lines)
     row_out = lax.all_to_all(row_out.reshape(row_span, col_span, -1), "cols", 0, 0, tiled=True)
     col_out = col_attend(me, col_pattern, col_count, pieces)
     col_out = swap_pieces(col_out)
-    weights += [by_xor(w, "rows", (1,))[0] for w in weights]
+    uppers += [by_xor(w, "rows", (1,))[0] for w in uppers]
+    lowers += [by_xor(w, "rows", (1,))[0] for w in lowers]
     outs = out_weight.shape[1] * peers * lax.axis_size("cols")
-    projected = project(place, row_out, col_out, weights, outs)
+    partial = project_rows(place, row_out, uppers, outs)
+    projected = project_cols(place, col_out, lowers, partial)
     return projected.reshape(row_span, col_span, projected.shape[-1])
 
 

time: 191 us -> 202 us (1.058)
  Pallas kernels: 40.9 us -> 55.5 us
  waiting for transfers between devices: 56.5 us -> 61.3 us
  other arithmetic: 4.45 us -> 0.64 us
  starting transfers between devices: 64 us -> 60.3 us
    pallas_call x1 -> x3, Pallas kernels: 15 us -> 29.5 us  [the longest x1 15.6 us: project_cols(): pl.pallas_call(functools.partial(project_cols_kernel, peers=len(pieces)),...]
    ppermute x23, starting transfers between devices: 29.8 us -> 24.2 us  [by_xor(): lax.ppermute(x, axis, [(d, d ^ s) for d in range(size)])]
    all_to_all x1, waiting for transfers between devices: 6.45 us -> 11.5 us  [body(): lax.all_to_all(row_out.reshape(row_span, col_span, -1), 'cols', 0, 0, til...]
    another operation x2 -> x0, other arithmetic: 3.86 us -> none  [body(): upper, lower = (jnp.stack(along_z), jnp.stack(along_x))]
    ppermute x14, starting transfers between devices: 20 us -> 22.9 us  [swap_pieces(): lax.ppermute(pieces[s], 'rows', [(d, d ^ s) for d in range(peers)])]
  transfers between devices with their start and end apart: 39 -> 39, of which waited for: 17 -> 12; matrix products, arithmetic and copies ran while one was open for 4% -> 2% of each run, Pallas kernels for 12% -> 18%
where the time goes in v6:
time: 202 us; the launch traced here: 199 us
  waiting for transfers between devices  61.3 us (30%)
  starting transfers between devices  60.3 us (30%)
  Pallas kernels  55.5 us (27%)
  local copies, waits for them, and re-layouts  20.7 us (10%)
    ppermute x14, waiting for transfers between devices, swap_pieces(): lax.ppermute(pieces[s], 'rows', [(d, d ^ s) for d in range(peers)])  30 us
    ppermute x23, starting transfers between devices, by_xor(): lax.ppermute(x, axis, [(d, d ^ s) for d in range(size)])  24.2 us
    ppermute x14, starting transfers between devices, swap_pieces(): lax.ppermute(pieces[s], 'rows', [(d, d ^ s) for d in range(peers)])  22.9 us
    ppermute x23, waiting for transfers between devices, by_xor(): lax.ppermute(x, axis, [(d, d ^ s) for d in range(size)])  19.7 us
    unnamed x67, local copies, waits for them, and re-layouts  17.7 us
    pallas_call x1, Pallas kernels, project_cols(): pl.pallas_call(functools.partial(project_cols_kernel, peers=len(pieces)),...  15.6 us
    pallas_call x1, Pallas kernels, project_rows(): pl.pallas_call(project_rows_kernel, grid_spec=pltpu.PrefetchScalarGridSpe...  12 us
    all_to_all x1, waiting for transfers between devices, body(): lax.all_to_all(row_out.reshape(row_span, col_span, -1), 'cols', 0, 0, til...  11.5 us
  transfers between devices with their start and end apart: 39, of which 12 were waited for; matrix products, arithmetic and copies ran while one was open for 2% of the time, Pallas kernels for 18%

profile of v6, /device:TPU:1, one launch (start us, length us, event | category | flops | bytes accessed | tf_op | source)
XLA Modules:
  0.0 198.8 jit_solution(18192217441560314312)
XLA Ops:
  0.0 4.2 %row_pack.1 = bf16[16,64,1536]{2,1,0:T(8,128)(2,1)} custom-call(bf16[16,64,1024]{2,1,0:T(8,128)(2,1)} %q_ref.3, bf16[16,64,1024]{2,1,0:T(8,128)(2,1)} %k_ref.3, bf16[16,64,1024]{2,1,0:T(8,128)(2,1)} %v_ref.3), custom_call_target="tpu_custom_call" | custom-call | tf_op jit(solution)/shard_map/row_pack/pallas_call | solution.py:41
  4.2 8.4 %all-to-all-start = ((bf16[16,64,1536]{2,1,0:T(8,128)(2,1)}), bf16[16,64,1536]{2,1,0:T(8,128)(2,1)S(1)}, u32[]{:S(2)}, u32[]{:S(2)}) async-start(bf16[16,64,1536]{2,1,0:T(8,128)(2,1)} %row_pack.1), calls=%async_computation | async-start | bytes 6291456 | tf_op jit(solution)/shard_map/all_to_all | solution.py:472
  12.6 6.9 %col_pack.1 = (bf16[8,16,1536]{2,1,0:T(8,128)(2,1)}, bf16[8,16,1536]{2,1,0:T(8,128)(2,1)}, bf16[8,16,1536]{2,1,0:T(8,128)(2,1)}, bf16[8,16,1536]{2,1,0:T(8,128)(...) custom-call(s32[1]{0:T(128)} %bitcast.me_ref, ...), custom_call_target="tpu_custom_call" | custom-call | tf_op jit(solution)/shard_map/col_pack/pallas_call | solution.py:92
  26.5 8.7 %collective-permute-done.15.refs_2_ = bf16[32,1024]{1,0:T(8,128)(2,1)S(1)} collective-permute-done((bf16[32,1024]{1,0:T(8,128)(2,1)S(1)}, bf16[32,1024]{1,0:T(8,128)(2,1)S(1)}, u32[]{:S(2)}, u32[]{:S(2)}) %collective-permute-start.15) | collective-permute-done | bytes 65568 | tf_op jit(solution)/shard_map/ppermute | solution.py:404
  36.7 2.8 %collective-permute-start.19 = (bf16[4,32,512]{2,1,0:T(8,128)(2,1)}, bf16[4,32,512]{2,1,0:T(8,128)(2,1)S(1)}, u32[]{:S(2)}, u32[]{:S(2)}) collective-permute-start(bf16[4,32,512]{2,1,0:T(8,128)(2,1)} %get-tuple-element.41.refs_0_), channel_id=1, source_target_pairs={{0,3},{1,2},{2,1},{3,0},{4,7},{5,6},{6,5},{7,4},{8,11},{9,10},{10,... | collective-permute-start | bytes 393224 | tf_op jit(solution)/shard_map/ppermute | solution.py:404
  41.1 2.5 %collective-permute-start.3 = (bf16[8,16,1536]{2,1,0:T(8,128)(2,1)}, bf16[8,16,1536]{2,1,0:T(8,128)(2,1)S(1)}, u32[]{:S(2)}, u32[]{:S(2)}) collective-permute-start(bf16[8,16,1536]{2,1,0:T(8,128)(2,1)} %get-tuple-element.29), channel_id=1, source_target_pairs={{0,64},{16,80},{32,96},{48,112},{64,0},{80,16},{96,32},{112,48},{1... | collective-permute-start | bytes 1179656 | tf_op jit(solution)/shard_map/ppermute | solution.py:410
  43.6 8.9 %collective-permute-done.19.refs_3_ = bf16[4,32,512]{2,1,0:T(8,128)(2,1)S(1)} collective-permute-done((bf16[4,32,512]{2,1,0:T(8,128)(2,1)}, bf16[4,32,512]{2,1,0:T(8,128)(2,1)S(1)}, u32[]{:S(2)}, u32[]{:S(2)}) %collective-permute-start.19) | collective-permute-done | bytes 131104 | tf_op jit(solution)/shard_map/ppermute | solution.py:404
  53.1 3.1 %collective-permute-start.4 = (bf16[8,16,1536]{2,1,0:T(8,128)(2,1)}, bf16[8,16,1536]{2,1,0:T(8,128)(2,1)S(1)}, u32[]{:S(2)}, u32[]{:S(2)}) collective-permute-start(bf16[8,16,1536]{2,1,0:T(8,128)(2,1)} %get-tuple-element.30), channel_id=1, source_target_pairs={{0,80},{16,64},{32,112},{48,96},{64,16},{80,0},{96,48},{112,32},{1... | collective-permute-start | bytes 1179656 | tf_op jit(solution)/shard_map/ppermute | solution.py:410
  62.4 6.9 %collective-permute-done.4.rest_5_ = bf16[8,16,1536]{2,1,0:T(8,128)(2,1)S(1)} collective-permute-done((bf16[8,16,1536]{2,1,0:T(8,128)(2,1)}, bf16[8,16,1536]{2,1,0:T(8,128)(2,1)S(1)}, u32[]{:S(2)}, u32[]{:S(2)}) %collective-permute-start.4) | collective-permute-done | bytes 393248 | tf_op jit(solution)/shard_map/ppermute | solution.py:410
  74.8 3.5 %collective-permute-done.5.rest_6_ = bf16[8,16,1536]{2,1,0:T(8,128)(2,1)} collective-permute-done((bf16[8,16,1536]{2,1,0:T(8,128)(2,1)}, bf16[8,16,1536]{2,1,0:T(8,128)(2,1)}, u32[]{:S(2)}, u32[]{:S(2)}) %collective-permute-start.5) | collective-permute-done | bytes 393248 | tf_op jit(solution)/shard_map/ppermute | solution.py:410
  78.3 2.6 %collective-permute-start.21 = (bf16[4,32,512]{2,1,0:T(8,128)(2,1)}, bf16[4,32,512]{2,1,0:T(8,128)(2,1)S(1)}, u32[]{:S(2)}, u32[]{:S(2)}) collective-permute-start(bf16[4,32,512]{2,1,0:T(8,128)(2,1)} %get-tuple-element.42.refs_4_), channel_id=1, source_target_pairs={{0,8},{1,9},{2,10},{3,11},{4,12},{5,13},{6,14},{7,15},{8,0},{9,1},... | collective-permute-start | bytes 393224 | tf_op jit(solution)/shard_map/ppermute | solution.py:404
  80.9 5.8 %collective-permute-done.6.rest_7_ = bf16[8,16,1536]{2,1,0:T(8,128)(2,1)} collective-permute-done((bf16[8,16,1536]{2,1,0:T(8,128)(2,1)}, bf16[8,16,1536]{2,1,0:T(8,128)(2,1)}, u32[]{:S(2)}, u32[]{:S(2)}) %collective-permute-start.6) | collective-permute-done | bytes 393248 | tf_op jit(solution)/shard_map/ppermute | solution.py:410
  93.7 5.8 %col_attend.1 = (bf16[16,8,512]{2,1,0:T(8,128)(2,1)}, bf16[16,8,512]{2,1,0:T(8,128)(2,1)}, bf16[16,8,512]{2,1,0:T(8,128)(2,1)}, bf16[16,8,512]{2,1,0:T(8,128)(2,...) custom-call(s32[1]{0:T(128)} %bitcast.me_ref, ...), custom_call_target="tpu_custom_call" | custom-call | tf_op jit(solution)/shard_map/col_attend/pallas_call | solution.py:269
  107.0 3.3 %collective-permute-start.25 = (bf16[4,4,32,512]{3,2,1,0:T(8,128)(2,1)}, bf16[4,4,32,512]{3,2,1,0:T(8,128)(2,1)}, u32[]{:S(2)}, u32[]{:S(2)}) collective-permute-start(bf16[4,4,32,512]{3,2,1,0:T(8,128)(2,1)} %get-tuple-element.43.rest_8_), channel_id=1, source_target_pairs={{0,3},{1,2},{2,1},{3,0},{4,7},{5,6},{6,5},{7,4},{8,11},{9,10},{10,... | collective-permute-start | bytes 1572872 | tf_op jit(solution)/shard_map/ppermute | solution.py:404
  112.6 2.6 %collective-permute-start.10 = (bf16[16,8,512]{2,1,0:T(8,128)(2,1)}, bf16[16,8,512]{2,1,0:T(8,128)(2,1)S(1)}, u32[]{:S(2)}, u32[]{:S(2)}) collective-permute-start(bf16[16,8,512]{2,1,0:T(8,128)(2,1)} %get-tuple-element.37), channel_id=1, source_target_pairs={{0,64},{16,80},{32,96},{48,112},{64,0},{80,16},{96,32},{112,48},{1... | collective-permute-start | bytes 393224 | tf_op jit(solution)/shard_map/ppermute | solution.py:410
  115.2 3.3 %collective-permute-done.10.rest_4_ = bf16[16,8,512]{2,1,0:T(8,128)(2,1)S(1)} collective-permute-done((bf16[16,8,512]{2,1,0:T(8,128)(2,1)}, bf16[16,8,512]{2,1,0:T(8,128)(2,1)S(1)}, u32[]{:S(2)}, u32[]{:S(2)}) %collective-permute-start.10) | collective-permute-done | bytes 131104 | tf_op jit(solution)/shard_map/ppermute | solution.py:410
  119.1 4.2 %collective-permute-start.11 = (bf16[16,8,512]{2,1,0:T(8,128)(2,1)}, bf16[16,8,512]{2,1,0:T(8,128)(2,1)S(1)}, u32[]{:S(2)}, u32[]{:S(2)}) collective-permute-start(bf16[16,8,512]{2,1,0:T(8,128)(2,1)} %get-tuple-element.38), channel_id=1, source_target_pairs={{0,80},{16,64},{32,112},{48,96},{64,16},{80,0},{96,48},{112,32},{1... | collective-permute-start | bytes 393224 | tf_op jit(solution)/shard_map/ppermute | solution.py:410
  123.4 4.5 %collective-permute-done.11.rest_5_ = bf16[16,8,512]{2,1,0:T(8,128)(2,1)S(1)} collective-permute-done((bf16[16,8,512]{2,1,0:T(8,128)(2,1)}, bf16[16,8,512]{2,1,0:T(8,128)(2,1)S(1)}, u32[]{:S(2)}, u32[]{:S(2)}) %collective-permute-start.11) | collective-permute-done | bytes 131104 | tf_op jit(solution)/shard_map/ppermute | solution.py:410
  129.3 5.4 %collective-permute-done.12.rest_6_ = bf16[16,8,512]{2,1,0:T(8,128)(2,1)S(1)} collective-permute-done((bf16[16,8,512]{2,1,0:T(8,128)(2,1)}, bf16[16,8,512]{2,1,0:T(8,128)(2,1)S(1)}, u32[]{:S(2)}, u32[]{:S(2)}) %collective-permute-start.12) | collective-permute-done | bytes 131104 | tf_op jit(solution)/shard_map/ppermute | solution.py:410
  141.3 7.6 %row_attend.1 = bf16[1024,512]{1,0:T(8,128)(2,1)} custom-call(s32[192]{0:T(256)} %reshape.14.pattern_ref, s32[1]{0:T(128)} %dynamic_slice.7.count_ref, bf16[16,64,1536]{2,1,0:T(8,128)(2,1)S(1)} %all-to-all-done.x_ref), custom_call_target="tpu_custom_call" | custom-call | tf_op jit(solution)/shard_map/row_attend/pallas_call | solution.py:189
  149.0 4.8 %all-to-all-start.1 = ((bf16[16,64,512]{2,1,0:T(8,128)(2,1)}), bf16[16,64,512]{2,1,0:T(8,128)(2,1)S(1)}, u32[]{:S(2)}, u32[]{:S(2)}) async-start(bf16[16,64,512]{2,1,0:T(8,128)(2,1)} %bitcast.5), calls=%async_computation.1 | async-start | bytes 2097152 | tf_op jit(solution)/shard_map/all_to_all | solution.py:483
  158.6 11.5 %all-to-all-done.1.heads = bf16[16,64,512]{2,1,0:T(8,128)(2,1)S(1)} async-done(((bf16[16,64,512]{2,1,0:T(8,128)(2,1)}), bf16[16,64,512]{2,1,0:T(8,128)(2,1)S(1)}, u32[]{:S(2)}, u32[]{:S(2)}) %all-to-all-start.1) | async-done | bytes 1048608 | tf_op jit(solution)/shard_map/all_to_all | solution.py:483
  170.1 12.0 %project_rows.1.rest_16_ = f32[1024,4096]{1,0:T(8,128)} custom-call(s32[2]{0:T(128)} %pad_add_fusion.place, bf16[16,64,512]{2,1,0:T(8,128)(2,1)S(1)} %all-to-all-done.1.heads, bf16[4,4,32,512]{3,2,1,0:T(8,128)(2,1)} %get-tuple-element.44.rest_0_, bf16[4,4,32,512]{3,2,1,0:T(8,128)(2,1)} %collective-permute-done.30.rest_1_, ...), custom_call_target="tpu_custom_call" | custom-call | tf_op jit(solution)/shard_map/project_rows/pallas_call | solution.py:365
  183.1 15.6 %project_cols.1 = bf16[1024,4096]{1,0:T(8,128)(2,1)} custom-call(s32[2]{0:T(128)} %pad_add_fusion.place, bf16[16,8,512]{2,1,0:T(8,128)(2,1)} %get-tuple-element.33.rest_0_, bf16[16,8,512]{2,1,0:T(8,128)(2,1)S(1)} %collective-permute-done.7.rest_1_, bf16[16,8,512]{2,1,0:T(8,128)(2,1)S(1)} %collective-permute-done.8.rest_2_, ...), custom_call_target="tpu_custom_call" | custom-call | tf_op jit(solution)/shard_map/project_cols/pallas_call | solution.py:385
  (135 shorter events, 53.5 us)
Async XLA Ops:
  4.2 137.2 %all-to-all-start = ((bf16[16,64,1536]{2,1,0:T(8,128)(2,1)}), bf16[16,64,1536]{2,1,0:T(8,128)(2,1)S(1)}, u32[]{:S(2)}, u32[]{:S(2)}) async-start(bf16[16,64,1536]{2,1,0:T(8,128)(2,1)} %row_pack.1), calls=%async_computation | async-start | bytes 6291456 | tf_op jit(solution)/shard_map/all_to_all | solution.py:472
  19.5 36.7 %collective-permute-start = (bf16[8,16,1536]{2,1,0:T(8,128)(2,1)}, bf16[8,16,1536]{2,1,0:T(8,128)(2,1)S(1)}, u32[]{:S(2)}, u32[]{:S(2)}) collective-permute-start(bf16[8,16,1536]{2,1,0:T(8,128)(2,1)} %get-tuple-element.26), channel_id=1, source_target_pairs={{0,16},{16,0},{32,48},{48,32},{64,80},{80,64},{96,112},{112,96},{1... | collective-permute-start | bytes 1179656 | tf_op jit(solution)/shard_map/ppermute | solution.py:410
  20.5 37.2 %collective-permute-start.1 = (bf16[8,16,1536]{2,1,0:T(8,128)(2,1)}, bf16[8,16,1536]{2,1,0:T(8,128)(2,1)S(1)}, u32[]{:S(2)}, u32[]{:S(2)}) collective-permute-start(bf16[8,16,1536]{2,1,0:T(8,128)(2,1)} %get-tuple-element.27), channel_id=1, source_target_pairs={{0,32},{16,48},{32,0},{48,16},{64,96},{80,112},{96,64},{112,80},{1... | collective-permute-start | bytes 1179656 | tf_op jit(solution)/shard_map/ppermute | solution.py:410
  39.6 20.6 %collective-permute-start.2 = (bf16[8,16,1536]{2,1,0:T(8,128)(2,1)}, bf16[8,16,1536]{2,1,0:T(8,128)(2,1)S(1)}, u32[]{:S(2)}, u32[]{:S(2)}) collective-permute-start(bf16[8,16,1536]{2,1,0:T(8,128)(2,1)} %get-tuple-element.28), channel_id=1, source_target_pairs={{0,48},{16,32},{32,16},{48,0},{64,112},{80,96},{96,80},{112,64},{1... | collective-permute-start | bytes 1179656 | tf_op jit(solution)/shard_map/ppermute | solution.py:410
  41.1 20.6 %collective-permute-start.3 = (bf16[8,16,1536]{2,1,0:T(8,128)(2,1)}, bf16[8,16,1536]{2,1,0:T(8,128)(2,1)S(1)}, u32[]{:S(2)}, u32[]{:S(2)}) collective-permute-start(bf16[8,16,1536]{2,1,0:T(8,128)(2,1)} %get-tuple-element.29), channel_id=1, source_target_pairs={{0,64},{16,80},{32,96},{48,112},{64,0},{80,16},{96,32},{112,48},{1... | collective-permute-start | bytes 1179656 | tf_op jit(solution)/shard_map/ppermute | solution.py:410
  57.0 21.3 %collective-permute-start.5 = (bf16[8,16,1536]{2,1,0:T(8,128)(2,1)}, bf16[8,16,1536]{2,1,0:T(8,128)(2,1)}, u32[]{:S(2)}, u32[]{:S(2)}) collective-permute-start(bf16[8,16,1536]{2,1,0:T(8,128)(2,1)} %get-tuple-element.31), channel_id=1, source_target_pairs={{0,96},{16,112},{32,64},{48,80},{64,32},{80,48},{96,0},{112,16},{1... | collective-permute-start | bytes 1179656 | tf_op jit(solution)/shard_map/ppermute | solution.py:410
  58.5 28.2 %collective-permute-start.6 = (bf16[8,16,1536]{2,1,0:T(8,128)(2,1)}, bf16[8,16,1536]{2,1,0:T(8,128)(2,1)}, u32[]{:S(2)}, u32[]{:S(2)}) collective-permute-start(bf16[8,16,1536]{2,1,0:T(8,128)(2,1)} %get-tuple-element.32), channel_id=1, source_target_pairs={{0,112},{16,96},{32,80},{48,64},{64,48},{80,32},{96,16},{112,0},{1... | collective-permute-start | bytes 1179656 | tf_op jit(solution)/shard_map/ppermute | solution.py:410
  61.0 38.6 %collective-permute-start.18 = (bf16[4,32,512]{2,1,0:T(8,128)(2,1)}, bf16[4,32,512]{2,1,0:T(8,128)(2,1)S(1)}, u32[]{:S(2)}, u32[]{:S(2)}) collective-permute-start(bf16[4,32,512]{2,1,0:T(8,128)(2,1)} %get-tuple-element.41.refs_0_), channel_id=1, source_target_pairs={{0,2},{1,3},{2,0},{3,1},{4,6},{5,7},{6,4},{7,5},{8,10},{9,11},{10,... | collective-permute-start | bytes 393224 | tf_op jit(solution)/shard_map/ppermute | solution.py:404
  62.4 38.5 %collective-permute-start.17 = (bf16[4,32,512]{2,1,0:T(8,128)(2,1)}, bf16[4,32,512]{2,1,0:T(8,128)(2,1)S(1)}, u32[]{:S(2)}, u32[]{:S(2)}) collective-permute-start(bf16[4,32,512]{2,1,0:T(8,128)(2,1)} %get-tuple-element.41.refs_0_), channel_id=1, source_target_pairs={{0,1},{1,0},{2,3},{3,2},{4,5},{5,4},{6,7},{7,6},{8,9},{9,8},{10,11... | collective-permute-start | bytes 393224 | tf_op jit(solution)/shard_map/ppermute | solution.py:404
  70.0 32.7 %collective-permute-start.22 = (bf16[4,32,512]{2,1,0:T(8,128)(2,1)}, bf16[4,32,512]{2,1,0:T(8,128)(2,1)}, u32[]{:S(2)}, u32[]{:S(2)}) collective-permute-start(bf16[4,32,512]{2,1,0:T(8,128)(2,1)} %get-tuple-element.42.refs_4_), channel_id=1, source_target_pairs={{0,12},{1,13},{2,14},{3,15},{4,8},{5,9},{6,10},{7,11},{8,4},{9,5},... | collective-permute-start | bytes 393224 | tf_op jit(solution)/shard_map/ppermute | solution.py:404
  78.3 24.9 %collective-permute-start.21 = (bf16[4,32,512]{2,1,0:T(8,128)(2,1)}, bf16[4,32,512]{2,1,0:T(8,128)(2,1)S(1)}, u32[]{:S(2)}, u32[]{:S(2)}) collective-permute-start(bf16[4,32,512]{2,1,0:T(8,128)(2,1)} %get-tuple-element.42.refs_4_), channel_id=1, source_target_pairs={{0,8},{1,9},{2,10},{3,11},{4,12},{5,13},{6,14},{7,15},{8,0},{9,1},... | collective-permute-start | bytes 393224 | tf_op jit(solution)/shard_map/ppermute | solution.py:404
  86.7 16.5 %collective-permute-start.20 = (bf16[4,32,512]{2,1,0:T(8,128)(2,1)}, bf16[4,32,512]{2,1,0:T(8,128)(2,1)S(1)}, u32[]{:S(2)}, u32[]{:S(2)}) collective-permute-start(bf16[4,32,512]{2,1,0:T(8,128)(2,1)} %get-tuple-element.42.refs_4_), channel_id=1, source_target_pairs={{0,4},{1,5},{2,6},{3,7},{4,0},{5,1},{6,2},{7,3},{8,12},{9,13},{10,... | collective-permute-start | bytes 393224 | tf_op jit(solution)/shard_map/ppermute | solution.py:404
  107.0 30.6 %collective-permute-start.25 = (bf16[4,4,32,512]{3,2,1,0:T(8,128)(2,1)}, bf16[4,4,32,512]{3,2,1,0:T(8,128)(2,1)}, u32[]{:S(2)}, u32[]{:S(2)}) collective-permute-start(bf16[4,4,32,512]{3,2,1,0:T(8,128)(2,1)} %get-tuple-element.43.rest_8_), channel_id=1, source_target_pairs={{0,3},{1,2},{2,1},{3,0},{4,7},{5,6},{6,5},{7,4},{8,11},{9,10},{10,... | collective-permute-start | bytes 1572872 | tf_op jit(solution)/shard_map/ppermute | solution.py:404
  110.3 27.9 %collective-permute-start.24 = (bf16[4,4,32,512]{3,2,1,0:T(8,128)(2,1)}, bf16[4,4,32,512]{3,2,1,0:T(8,128)(2,1)}, u32[]{:S(2)}, u32[]{:S(2)}) collective-permute-start(bf16[4,4,32,512]{3,2,1,0:T(8,128)(2,1)} %get-tuple-element.43.rest_8_), channel_id=1, source_target_pairs={{0,2},{1,3},{2,0},{3,1},{4,6},{5,7},{6,4},{7,5},{8,10},{9,11},{10,... | collective-permute-start | bytes 1572872 | tf_op jit(solution)/shard_map/ppermute | solution.py:404
  110.3 29.8 %collective-permute-start.32 = (bf16[4,4,32,512]{3,2,1,0:T(8,128)(2,1)}, bf16[4,4,32,512]{3,2,1,0:T(8,128)(2,1)}, u32[]{:S(2)}, u32[]{:S(2)}) collective-permute-start(bf16[4,4,32,512]{3,2,1,0:T(8,128)(2,1)} %get-tuple-element.44.rest_0_), channel_id=1, source_target_pairs={{0,12},{1,13},{2,14},{3,15},{4,8},{5,9},{6,10},{7,11},{8,4},{9,5},... | collective-permute-start | bytes 1572872 | tf_op jit(solution)/shard_map/ppermute | solution.py:404
  110.3 29.8 %collective-permute-start.31 = (bf16[4,4,32,512]{3,2,1,0:T(8,128)(2,1)}, bf16[4,4,32,512]{3,2,1,0:T(8,128)(2,1)}, u32[]{:S(2)}, u32[]{:S(2)}) collective-permute-start(bf16[4,4,32,512]{3,2,1,0:T(8,128)(2,1)} %get-tuple-element.44.rest_0_), channel_id=1, source_target_pairs={{0,8},{1,9},{2,10},{3,11},{4,12},{5,13},{6,14},{7,15},{8,0},{9,1},... | collective-permute-start | bytes 1572872 | tf_op jit(solution)/shard_map/ppermute | solution.py:404
  135.4 18.4 %collective-permute-start.30 = (bf16[4,4,32,512]{3,2,1,0:T(8,128)(2,1)}, bf16[4,4,32,512]{3,2,1,0:T(8,128)(2,1)}, u32[]{:S(2)}, u32[]{:S(2)}) collective-permute-start(bf16[4,4,32,512]{3,2,1,0:T(8,128)(2,1)} %get-tuple-element.44.rest_0_), channel_id=1, source_target_pairs={{0,4},{1,5},{2,6},{3,7},{4,0},{5,1},{6,2},{7,3},{8,12},{9,13},{10,... | collective-permute-start | bytes 1572872 | tf_op jit(solution)/shard_map/ppermute | solution.py:404
  137.6 16.6 %collective-permute-start.23 = (bf16[4,4,32,512]{3,2,1,0:T(8,128)(2,1)}, bf16[4,4,32,512]{3,2,1,0:T(8,128)(2,1)}, u32[]{:S(2)}, u32[]{:S(2)}) collective-permute-start(bf16[4,4,32,512]{3,2,1,0:T(8,128)(2,1)} %get-tuple-element.43.rest_8_), channel_id=1, source_target_pairs={{0,1},{1,0},{2,3},{3,2},{4,5},{5,4},{6,7},{7,6},{8,9},{9,8},{10,11... | collective-permute-start | bytes 1572872 | tf_op jit(solution)/shard_map/ppermute | solution.py:404
  149.0 21.1 %all-to-all-start.1 = ((bf16[16,64,512]{2,1,0:T(8,128)(2,1)}), bf16[16,64,512]{2,1,0:T(8,128)(2,1)S(1)}, u32[]{:S(2)}, u32[]{:S(2)}) async-start(bf16[16,64,512]{2,1,0:T(8,128)(2,1)} %bitcast.5), calls=%async_computation.1 | async-start | bytes 2097152 | tf_op jit(solution)/shard_map/all_to_all | solution.py:483
  154.2 27.9 %collective-permute-start.26 = (bf16[4,4,32,512]{3,2,1,0:T(8,128)(2,1)}, bf16[4,4,32,512]{3,2,1,0:T(8,128)(2,1)S(1)}, u32[]{:S(2)}, u32[]{:S(2)}) collective-permute-start(bf16[4,4,32,512]{3,2,1,0:T(8,128)(2,1)} %get-tuple-element.43.rest_8_), channel_id=1, source_target_pairs={{0,16},{16,0},{32,48},{48,32},{64,80},{80,64},{96,112},{112,96},{1... | collective-permute-start | bytes 1572872 | tf_op jit(solution)/shard_map/ppermute | solution.py:404
  154.5 27.6 %collective-permute-start.29 = (bf16[4,4,32,512]{3,2,1,0:T(8,128)(2,1)}, bf16[4,4,32,512]{3,2,1,0:T(8,128)(2,1)S(1)}, u32[]{:S(2)}, u32[]{:S(2)}) collective-permute-start(bf16[4,4,32,512]{3,2,1,0:T(8,128)(2,1)} %collective-permute-done.25.rest_11_), channel_id=1, source_target_pairs={{0,16},{16,0},{32,48},{48,32},{64,80},{80,64},{96,112},{112,96},{1... | collective-permute-start | bytes 1572872 | tf_op jit(solution)/shard_map/ppermute | solution.py:404
  154.7 27.4 %collective-permute-start.28 = (bf16[4,4,32,512]{3,2,1,0:T(8,128)(2,1)}, bf16[4,4,32,512]{3,2,1,0:T(8,128)(2,1)}, u32[]{:S(2)}, u32[]{:S(2)}) collective-permute-start(bf16[4,4,32,512]{3,2,1,0:T(8,128)(2,1)} %collective-permute-done.24.rest_10_), channel_id=1, source_target_pairs={{0,16},{16,0},{32,48},{48,32},{64,80},{80,64},{96,112},{112,96},{1... | collective-permute-start | bytes 1572872 | tf_op jit(solution)/shard_map/ppermute | solution.py:404
  155.0 27.1 %collective-permute-start.27 = (bf16[4,4,32,512]{3,2,1,0:T(8,128)(2,1)}, bf16[4,4,32,512]{3,2,1,0:T(8,128)(2,1)}, u32[]{:S(2)}, u32[]{:S(2)}) collective-permute-start(bf16[4,4,32,512]{3,2,1,0:T(8,128)(2,1)} %collective-permute-done.23.rest_9_), channel_id=1, source_target_pairs={{0,16},{16,0},{32,48},{48,32},{64,80},{80,64},{96,112},{112,96},{1... | collective-permute-start | bytes 1572872 | tf_op jit(solution)/shard_map/ppermute | solution.py:404
  156.8 25.3 %collective-permute-start.13 = (bf16[16,8,512]{2,1,0:T(8,128)(2,1)}, bf16[16,8,512]{2,1,0:T(8,128)(2,1)S(1)}, u32[]{:S(2)}, u32[]{:S(2)}) collective-permute-start(bf16[16,8,512]{2,1,0:T(8,128)(2,1)} %get-tuple-element.40), channel_id=1, source_target_pairs={{0,112},{16,96},{32,80},{48,64},{64,48},{80,32},{96,16},{112,0},{1... | collective-permute-start | bytes 393224 | tf_op jit(solution)/shard_map/ppermute | solution.py:410
  (48 other events, 626.9 us)

commit v7 on v6

--- a/solution.py
+++ b/solution.py
@@ -183,9 +183,8 @@
     lax.fori_loop(0, blocks // UNROLL, group, 0)
 
 
-def row_attend(pattern, count, x):
+def row_attend(pattern, chosen, count, x):
     cells = x.shape[0] * x.shape[1]
-    chosen = pattern.shape[-1]
     return pl.pallas_call(
         functools.partial(row_attend_kernel, chosen=chosen),
         grid_spec=pltpu.PrefetchScalarGridSpec(
@@ -197,7 +196,7 @@
         out_shape=jax.ShapeDtypeStruct((cells, HR * HD), x.dtype),
         compiler_params=grant(56),
         name="row_attend",
-    )(pattern.reshape(-1), count, in_place(x))
+    )(pattern, count, in_place(x))
 
 
 def col_attend_kernel(me_ref, pattern_ref, count_ref, *rest, chosen, lines):
@@ -259,11 +258,10 @@
                 outs[s][:, :, h * HD : (h + 1) * HD] = part.astype(jnp.bfloat16)
 
 
-def col_attend(me, pattern, count, pieces):
+def col_attend(me, pattern, chosen, count, pieces):
     peers = len(pieces)
     own, span, wide = pieces[0].shape
     width = HC * HD
-    chosen = pattern.shape[-1]
     lines = 2
     result = (span, own, width)
     return pl.pallas_call(
@@ -281,7 +279,7 @@
         out_shape=[jax.ShapeDtypeStruct(result, jnp.bfloat16)] * peers,
         compiler_params=grant(56),
         name="col_attend",
-    )(me, pattern.reshape(-1), count, pieces[0], *[in_place(p) for p in pieces[1:]])
+    )(me, pattern, count, pieces[0], *[in_place(p) for p in pieces[1:]])
 
 
 def fetch_weights(plane, weights, line, sem, step, slot, flipped):
@@ -325,7 +323,8 @@
 
 def project_rows_kernel(place, heads, *rest):
     weights, (out_ref, line, sem) = rest[:-3], rest[-3:]
-    out_ref[...] = project_step(place[1], weights, line, sem, False, heads)
+    added = project_step(place[1], weights, line, sem, False, heads)
+    out_ref[pl.program_id(0)] = added
 
 
 def project_cols_kernel(place, *rest, peers):
@@ -345,7 +344,7 @@
             heads[:, pl.ds(at, 2 * own), :] = both.astype(jnp.bfloat16)
 
     added = project_step(place[1], weights, line, sem, True, heads)
-    out_ref[...] = (partial_ref[...] + added).astype(jnp.bfloat16)
+    out_ref[...] = (partial_ref[pl.program_id(0)] + added).astype(jnp.bfloat16)
 
 
 def project_sizes(weights):
@@ -359,9 +358,9 @@
     return 2 * turns, tile, target, scratch
 
 
-def project_rows(place, row_out, weights, outs):
+def project_rows(place, row_out, weights):
     span, cells, _ = row_out.shape
-    steps, tile, target, scratch = project_sizes(weights)
+    steps, tile, _, scratch = project_sizes(weights)
     return pl.pallas_call(
         project_rows_kernel,
         grid_spec=pltpu.PrefetchScalarGridSpec(
@@ -369,34 +368,34 @@
             grid=(steps,),
             in_specs=[pl.BlockSpec(memory_space=pltpu.VMEM)]
             + [pl.BlockSpec(memory_space=pl.ANY)] * len(weights),
-            out_specs=pl.BlockSpec((span * cells, tile), target),
+            out_specs=pl.BlockSpec(memory_space=pltpu.VMEM),
             scratch_shapes=scratch,
         ),
-        out_shape=jax.ShapeDtypeStruct((span * cells, outs), jnp.float32),
-        compiler_params=grant(56),
+        out_shape=pltpu.VMEM((steps, span * cells, tile), jnp.float32),
+        compiler_params=grant(20),
         name="project_rows",
     )(place, in_place(row_out), *weights)
 
 
-def project_cols(place, pieces, weights, partial):
+def project_cols(place, pieces, weights, partial, outs):
     span, own, width = pieces[0].shape
     steps, tile, target, scratch = project_sizes(weights)
-    block = pl.BlockSpec((partial.shape[0], tile), target)
+    held = pl.BlockSpec(memory_space=pltpu.VMEM)
     return pl.pallas_call(
         functools.partial(project_cols_kernel, peers=len(pieces)),
         grid_spec=pltpu.PrefetchScalarGridSpec(
             num_scalar_prefetch=1,
             grid=(steps,),
-            in_specs=[pl.BlockSpec(memory_space=pltpu.VMEM)] * len(pieces)
+            in_specs=[held] * len(pieces)
             + [pl.BlockSpec(memory_space=pl.ANY)] * len(weights)
-            + [block],
-            out_specs=block,
+            + [held],
+            out_specs=pl.BlockSpec((partial.shape[1], tile), target),
             scratch_shapes=[pltpu.VMEM((span, own * len(pieces), width), jnp.bfloat16)] + scratch,
         ),
-        out_shape=jax.ShapeDtypeStruct(partial.shape, jnp.bfloat16),
-        compiler_params=grant(56),
+        out_shape=jax.ShapeDtypeStruct((partial.shape[1], outs), jnp.bfloat16),
+        compiler_params=grant(20),
         name="project_cols",
-    )(place, pieces[0], *[in_place(p) for p in pieces[1:]], *weights, partial)
+    )(place, pieces[0], *[in_place(p) for p in pieces[1:]], *weights, in_place(partial))
 
 
 def by_xor(x, axis, masks):
@@ -429,29 +428,34 @@
         out_shape=[whole, whole],
         compiler_params=grant(56),
         name="join_both",
-    )(*[in_place(p) for p in first], *[in_place(p) for p in second])
+    )(
+        first[0],
+        *[in_place(p) for p in first[1:]],
+        second[0],
+        *[in_place(p) for p in second[1:]],
+    )
 
 
 def halve_kernel(*refs):
-    parts, (upper, lower) = refs[:-2], refs[-2:]
+    parts, (upper, lower) = refs[:-4], refs[-2:]
     middle = upper.shape[2]
     for i, part in enumerate(parts):
         upper[i] = part[:, :middle]
         lower[i] = part[:, middle:]
 
 
-def halve(parts):
+def halve(parts, tables):
     span, channels = parts[0].shape
     half = jax.ShapeDtypeStruct((len(parts), span, channels // 2), parts[0].dtype)
     held = pl.BlockSpec(memory_space=pltpu.VMEM)
     return pl.pallas_call(
         halve_kernel,
-        in_specs=[held] * len(parts),
+        in_specs=[held] * len(parts) + [pl.BlockSpec(memory_space=pl.ANY)] * len(tables),
         out_specs=[held, held],
         out_shape=[half, half],
         compiler_params=grant(56),
         name="halve",
-    )(parts[0], *[in_place(p) for p in parts[1:]])
+    )(parts[0], *[in_place(p) for p in parts[1:]], *tables)
 
 
 def body(
@@ -462,7 +466,9 @@
     row_share = row_span // lax.axis_size("cols")
     me = lax.axis_index("rows").astype(jnp.int32).reshape(1)
     row_first = lax.axis_index("cols") * row_share
-    pattern = lax.dynamic_slice_in_dim(row_pattern, row_first, row_share, 0)
+    chosen = row_pattern.shape[-1]
+    pattern = lax.dynamic_slice_in_dim(row_pattern, row_first, row_share, 0).reshape(-1)
+    col_listed = col_pattern.reshape(-1)
     count = lax.dynamic_slice_in_dim(row_count, row_first, row_share, 0)
 
     place = jnp.stack([lax.axis_index("rows"), lax.axis_index("cols")]).astype(jnp.int32)
@@ -473,21 +479,21 @@
     along_y = [shard] + by_xor(shard, "rows", (2, 4, 6))
     sent = col_pack(me, query_cells, key_cells, value_cells, peers)
     pieces = swap_pieces(sent)
-    upper, lower = halve(along_y)
+    upper, lower = halve(along_y, (pattern, col_listed))
     along_z = [upper] + by_xor(upper, "cols", (1, 2, 3))
     along_x = [lower] + by_xor(lower, "cols", (4, 8, 12))
     upper, lower = join_both(along_z, along_x)
     uppers = [upper] + by_xor(upper, "cols", (4, 8, 12))
     lowers = [lower] + by_xor(lower, "cols", (1, 2, 3))
-    row_out = row_attend(pattern, count, lines)
+    row_out = row_attend(pattern, chosen, count, lines)
     row_out = lax.all_to_all(row_out.reshape(row_span, col_span, -1), "cols", 0, 0, tiled=True)
-    col_out = col_attend(me, col_pattern, col_count, pieces)
+    col_out = col_attend(me, col_listed, col_pattern.shape[-1], col_count, pieces)
     col_out = swap_pieces(col_out)
     uppers += [by_xor(w, "rows", (1,))[0] for w in uppers]
     lowers += [by_xor(w, "rows", (1,))[0] for w in lowers]
     outs = out_weight.shape[1] * peers * lax.axis_size("cols")
-    partial = project_rows(place, row_out, uppers, outs)
-    projected = project_cols(place, col_out, lowers, partial)
+    partial = project_rows(place, row_out, uppers)
+    projected = project_cols(place, col_out, lowers, partial, outs)
     return projected.reshape(row_span, col_span, projected.shape[-1])
 
 

time: 202 us -> 180 us (0.89)
  waiting for transfers between devices: 61.3 us -> 50.7 us
  local copies, waits for them, and re-layouts: 20.7 us -> 11.4 us
  Pallas kernels: 55.5 us -> 49.6 us
  starting transfers between devices: 60.3 us -> 64.1 us
    unnamed x67 -> x45, local copies, waits for them, and re-layouts: 17.7 us -> 9.24 us
    ppermute x23, waiting for transfers between devices: 19.7 us -> 12.2 us  [by_xor(): lax.ppermute(x, axis, [(d, d ^ s) for d in range(size)])]
    ppermute x23, starting transfers between devices: 24.2 us -> 30.6 us  [by_xor(): lax.ppermute(x, axis, [(d, d ^ s) for d in range(size)])]
    pallas_call x1, Pallas kernels: 15.6 us -> 11.9 us  [project_cols(): pl.pallas_call(functools.partial(project_cols_kernel, peers=len(pieces)),...]
    pallas_call x1, Pallas kernels: 12 us -> 9.27 us  [project_rows(): pl.pallas_call(project_rows_kernel, grid_spec=pltpu.PrefetchScalarGridSpe...]
    ppermute x14, starting transfers between devices: 22.9 us -> 20.8 us  [swap_pieces(): lax.ppermute(pieces[s], 'rows', [(d, d ^ s) for d in range(peers)])]
  transfers between devices with their start and end apart: 39 -> 39, of which waited for: 12 -> 12; matrix products, arithmetic and copies ran while one was open for 2% -> 1% of each run, Pallas kernels for 18% -> 19%
where the time goes in v7:
time: 180 us; the launch traced here: 176 us
  starting transfers between devices  64.1 us (36%)
  waiting for transfers between devices  50.7 us (28%)
  Pallas kernels  49.6 us (28%)
  local copies, waits for them, and re-layouts  11.4 us (6%)
    ppermute x23, starting transfers between devices, by_xor(): lax.ppermute(x, axis, [(d, d ^ s) for d in range(size)])  30.6 us
    ppermute x14, waiting for transfers between devices, swap_pieces(): lax.ppermute(pieces[s], 'rows', [(d, d ^ s) for d in range(peers)])  28.4 us
    ppermute x14, starting transfers between devices, swap_pieces(): lax.ppermute(pieces[s], 'rows', [(d, d ^ s) for d in range(peers)])  20.8 us
    ppermute x23, waiting for transfers between devices, by_xor(): lax.ppermute(x, axis, [(d, d ^ s) for d in range(size)])  12.2 us
    pallas_call x1, Pallas kernels, project_cols(): pl.pallas_call(functools.partial(project_cols_kernel, peers=len(pieces)),...  11.9 us
    all_to_all x1, waiting for transfers between devices, body(): lax.all_to_all(row_out.reshape(row_span, col_span, -1), 'cols', 0, 0, til...  10 us
    pallas_call x1, Pallas kernels, project_rows(): pl.pallas_call(project_rows_kernel, grid_spec=pltpu.PrefetchScalarGridSpe...  9.27 us
    unnamed x45, local copies, waits for them, and re-layouts  9.24 us
  transfers between devices with their start and end apart: 39, of which 12 were waited for; matrix products, arithmetic and copies ran while one was open for 1% of the time, Pallas kernels for 19%

profile of v7, /device:TPU:1, one launch (start us, length us, event | category | flops | bytes accessed | tf_op | source)
XLA Modules:
  0.0 176.3 jit_solution(15605546917563328563)
XLA Ops:
  0.0 4.2 %row_pack.1 = bf16[16,64,1536]{2,1,0:T(8,128)(2,1)} custom-call(bf16[16,64,1024]{2,1,0:T(8,128)(2,1)} %q_ref.3, bf16[16,64,1024]{2,1,0:T(8,128)(2,1)} %k_ref.3, bf16[16,64,1024]{2,1,0:T(8,128)(2,1)} %v_ref.3), custom_call_target="tpu_custom_call" | custom-call | tf_op jit(solution)/shard_map/row_pack/pallas_call | solution.py:41
  4.2 8.4 %all-to-all-start = ((bf16[16,64,1536]{2,1,0:T(8,128)(2,1)}), bf16[16,64,1536]{2,1,0:T(8,128)(2,1)S(1)}, u32[]{:S(2)}, u32[]{:S(2)}) async-start(bf16[16,64,1536]{2,1,0:T(8,128)(2,1)} %row_pack.1), calls=%async_computation | async-start | bytes 6291456 | tf_op jit(solution)/shard_map/all_to_all | solution.py:478
  12.6 6.9 %col_pack.1 = (bf16[8,16,1536]{2,1,0:T(8,128)(2,1)}, bf16[8,16,1536]{2,1,0:T(8,128)(2,1)}, bf16[8,16,1536]{2,1,0:T(8,128)(2,1)}, bf16[8,16,1536]{2,1,0:T(8,128)(...) custom-call(s32[1]{0:T(128)} %bitcast.me_ref, ...), custom_call_target="tpu_custom_call" | custom-call | tf_op jit(solution)/shard_map/col_pack/pallas_call | solution.py:92
  27.1 8.1 %collective-permute-done.15.refs_2_ = bf16[32,1024]{1,0:T(8,128)(2,1)S(1)} collective-permute-done((bf16[32,1024]{1,0:T(8,128)(2,1)S(1)}, bf16[32,1024]{1,0:T(8,128)(2,1)S(1)}, u32[]{:S(2)}, u32[]{:S(2)}) %collective-permute-start.15) | collective-permute-done | bytes 65568 | tf_op jit(solution)/shard_map/ppermute | solution.py:403
  35.5 4.3 %collective-permute-start.4 = (bf16[8,16,1536]{2,1,0:T(8,128)(2,1)}, bf16[8,16,1536]{2,1,0:T(8,128)(2,1)}, u32[]{:S(2)}, u32[]{:S(2)}) collective-permute-start(bf16[8,16,1536]{2,1,0:T(8,128)(2,1)} %get-tuple-element.30), channel_id=1, source_target_pairs={{0,80},{16,64},{32,112},{48,96},{64,16},{80,0},{96,48},{112,32},{1... | collective-permute-start | bytes 1179656 | tf_op jit(solution)/shard_map/ppermute | solution.py:409
  46.2 2.8 %collective-permute-start.19 = (bf16[4,32,512]{2,1,0:T(8,128)(2,1)}, bf16[4,32,512]{2,1,0:T(8,128)(2,1)S(1)}, u32[]{:S(2)}, u32[]{:S(2)}) collective-permute-start(bf16[4,32,512]{2,1,0:T(8,128)(2,1)} %get-tuple-element.41.refs_0_), channel_id=1, source_target_pairs={{0,3},{1,2},{2,1},{3,0},{4,7},{5,6},{6,5},{7,4},{8,11},{9,10},{10,... | collective-permute-start | bytes 393224 | tf_op jit(solution)/shard_map/ppermute | solution.py:403
  49.0 4.6 %collective-permute-done.3.rest_4_ = bf16[8,16,1536]{2,1,0:T(8,128)(2,1)} collective-permute-done((bf16[8,16,1536]{2,1,0:T(8,128)(2,1)}, bf16[8,16,1536]{2,1,0:T(8,128)(2,1)}, u32[]{:S(2)}, u32[]{:S(2)}) %collective-permute-start.3) | collective-permute-done | bytes 393248 | tf_op jit(solution)/shard_map/ppermute | solution.py:409
  53.6 3.1 %collective-permute-start.18 = (bf16[4,32,512]{2,1,0:T(8,128)(2,1)}, bf16[4,32,512]{2,1,0:T(8,128)(2,1)S(1)}, u32[]{:S(2)}, u32[]{:S(2)}) collective-permute-start(bf16[4,32,512]{2,1,0:T(8,128)(2,1)} %get-tuple-element.41.refs_0_), channel_id=1, source_target_pairs={{0,2},{1,3},{2,0},{3,1},{4,6},{5,7},{6,4},{7,5},{8,10},{9,11},{10,... | collective-permute-start | bytes 393224 | tf_op jit(solution)/shard_map/ppermute | solution.py:403
  56.7 5.6 %collective-permute-done.4.rest_5_ = bf16[8,16,1536]{2,1,0:T(8,128)(2,1)} collective-permute-done((bf16[8,16,1536]{2,1,0:T(8,128)(2,1)}, bf16[8,16,1536]{2,1,0:T(8,128)(2,1)}, u32[]{:S(2)}, u32[]{:S(2)}) %collective-permute-start.4) | collective-permute-done | bytes 393248 | tf_op jit(solution)/shard_map/ppermute | solution.py:409
  64.0 5.9 %collective-permute-done.5.rest_6_ = bf16[8,16,1536]{2,1,0:T(8,128)(2,1)} collective-permute-done((bf16[8,16,1536]{2,1,0:T(8,128)(2,1)}, bf16[8,16,1536]{2,1,0:T(8,128)(2,1)}, u32[]{:S(2)}, u32[]{:S(2)}) %collective-permute-start.5) | collective-permute-done | bytes 393248 | tf_op jit(solution)/shard_map/ppermute | solution.py:409
  69.8 2.9 %collective-permute-start.22 = (bf16[4,32,512]{2,1,0:T(8,128)(2,1)}, bf16[4,32,512]{2,1,0:T(8,128)(2,1)S(1)}, u32[]{:S(2)}, u32[]{:S(2)}) collective-permute-start(bf16[4,32,512]{2,1,0:T(8,128)(2,1)} %get-tuple-element.42.refs_4_), channel_id=1, source_target_pairs={{0,12},{1,13},{2,14},{3,15},{4,8},{5,9},{6,10},{7,11},{8,4},{9,5},... | collective-permute-start | bytes 393224 | tf_op jit(solution)/shard_map/ppermute | solution.py:403
  72.7 4.3 %collective-permute-done.6.rest_7_ = bf16[8,16,1536]{2,1,0:T(8,128)(2,1)} collective-permute-done((bf16[8,16,1536]{2,1,0:T(8,128)(2,1)}, bf16[8,16,1536]{2,1,0:T(8,128)(2,1)}, u32[]{:S(2)}, u32[]{:S(2)}) %collective-permute-start.6) | collective-permute-done | bytes 393248 | tf_op jit(solution)/shard_map/ppermute | solution.py:409
  76.9 3.1 %collective-permute-start.21 = (bf16[4,32,512]{2,1,0:T(8,128)(2,1)}, bf16[4,32,512]{2,1,0:T(8,128)(2,1)S(1)}, u32[]{:S(2)}, u32[]{:S(2)}) collective-permute-start(bf16[4,32,512]{2,1,0:T(8,128)(2,1)} %get-tuple-element.42.refs_4_), channel_id=1, source_target_pairs={{0,8},{1,9},{2,10},{3,11},{4,12},{5,13},{6,14},{7,15},{8,0},{9,1},... | collective-permute-start | bytes 393224 | tf_op jit(solution)/shard_map/ppermute | solution.py:403
  82.1 6.2 %col_attend.1 = (bf16[16,8,512]{2,1,0:T(8,128)(2,1)}, bf16[16,8,512]{2,1,0:T(8,128)(2,1)}, bf16[16,8,512]{2,1,0:T(8,128)(2,1)}, bf16[16,8,512]{2,1,0:T(8,128)(2,...) custom-call(s32[1]{0:T(128)} %bitcast.me_ref, ...), custom_call_target="tpu_custom_call" | custom-call | tf_op jit(solution)/shard_map/col_attend/pallas_call | solution.py:267
  94.3 2.4 %collective-permute-start.25 = (bf16[4,4,32,512]{3,2,1,0:T(8,128)(2,1)}, bf16[4,4,32,512]{3,2,1,0:T(8,128)(2,1)}, u32[]{:S(2)}, u32[]{:S(2)}) collective-permute-start(bf16[4,4,32,512]{3,2,1,0:T(8,128)(2,1)} %get-tuple-element.43.rest_8_), channel_id=1, source_target_pairs={{0,3},{1,2},{2,1},{3,0},{4,7},{5,6},{6,5},{7,4},{8,11},{9,10},{10,... | collective-permute-start | bytes 1572872 | tf_op jit(solution)/shard_map/ppermute | solution.py:403
  102.3 3.5 %collective-permute-start.11 = (bf16[16,8,512]{2,1,0:T(8,128)(2,1)}, bf16[16,8,512]{2,1,0:T(8,128)(2,1)S(1)}, u32[]{:S(2)}, u32[]{:S(2)}) collective-permute-start(bf16[16,8,512]{2,1,0:T(8,128)(2,1)} %get-tuple-element.38), channel_id=1, source_target_pairs={{0,80},{16,64},{32,112},{48,96},{64,16},{80,0},{96,48},{112,32},{1... | collective-permute-start | bytes 393224 | tf_op jit(solution)/shard_map/ppermute | solution.py:409
  105.8 3.6 %collective-permute-done.11.rest_5_ = bf16[16,8,512]{2,1,0:T(8,128)(2,1)S(1)} collective-permute-done((bf16[16,8,512]{2,1,0:T(8,128)(2,1)}, bf16[16,8,512]{2,1,0:T(8,128)(2,1)S(1)}, u32[]{:S(2)}, u32[]{:S(2)}) %collective-permute-start.11) | collective-permute-done | bytes 131104 | tf_op jit(solution)/shard_map/ppermute | solution.py:409
  112.3 3.3 %collective-permute-done.12.rest_6_ = bf16[16,8,512]{2,1,0:T(8,128)(2,1)S(1)} collective-permute-done((bf16[16,8,512]{2,1,0:T(8,128)(2,1)}, bf16[16,8,512]{2,1,0:T(8,128)(2,1)S(1)}, u32[]{:S(2)}, u32[]{:S(2)}) %collective-permute-start.12) | collective-permute-done | bytes 131104 | tf_op jit(solution)/shard_map/ppermute | solution.py:409
  121.7 2.7 %collective-permute-start.36 = (bf16[4,4,32,512]{3,2,1,0:T(8,128)(2,1)}, bf16[4,4,32,512]{3,2,1,0:T(8,128)(2,1)}, u32[]{:S(2)}, u32[]{:S(2)}) collective-permute-start(bf16[4,4,32,512]{3,2,1,0:T(8,128)(2,1)} %collective-permute-done.32.rest_3_), channel_id=1, source_target_pairs={{0,16},{16,0},{32,48},{48,32},{64,80},{80,64},{96,112},{112,96},{1... | collective-permute-start | bytes 1572872 | tf_op jit(solution)/shard_map/ppermute | solution.py:403
  125.1 7.8 %row_attend.1 = bf16[1024,512]{1,0:T(8,128)(2,1)} custom-call(s32[192]{0:T(256)} %reshape.14.refs_4_.pattern_ref, s32[1]{0:T(128)} %dynamic_slice.7.count_ref, bf16[16,64,1536]{2,1,0:T(8,128)(2,1)S(1)} %all-to-all-done.x_ref), custom_call_target="tpu_custom_call" | custom-call | tf_op jit(solution)/shard_map/row_attend/pallas_call | solution.py:188
  132.9 4.3 %all-to-all-start.1 = ((bf16[16,64,512]{2,1,0:T(8,128)(2,1)}), bf16[16,64,512]{2,1,0:T(8,128)(2,1)S(1)}, u32[]{:S(2)}, u32[]{:S(2)}) async-start(bf16[16,64,512]{2,1,0:T(8,128)(2,1)} %bitcast.5), calls=%async_computation.1 | async-start | bytes 2097152 | tf_op jit(solution)/shard_map/all_to_all | solution.py:489
  142.7 10.0 %all-to-all-done.1.heads = bf16[16,64,512]{2,1,0:T(8,128)(2,1)S(1)} async-done(((bf16[16,64,512]{2,1,0:T(8,128)(2,1)}), bf16[16,64,512]{2,1,0:T(8,128)(2,1)S(1)}, u32[]{:S(2)}, u32[]{:S(2)}) %all-to-all-start.1) | async-done | bytes 1048608 | tf_op jit(solution)/shard_map/all_to_all | solution.py:489
  154.9 9.3 %project_rows.1.rest_16_ = f32[8,1024,512]{2,1,0:T(8,128)S(1)} custom-call(s32[2]{0:T(128)S(1)} %pad_add_fusion.place, bf16[16,64,512]{2,1,0:T(8,128)(2,1)S(1)} %all-to-all-done.1.heads, bf16[4,4,32,512]{3,2,1,0:T(8,128)(2,1)S(1)} %copy-done.2, bf16[4,4,32,512]{3,2,1,0:T(8,128)(2,1)} %collective-permute-done.30.rest_1_, ...), custom_call_target="tpu_custom_call" | custom-call | tf_op jit(solution)/shard_map/project_rows/pallas_call | solution.py:364
  164.3 11.9 %project_cols.1 = bf16[1024,4096]{1,0:T(8,128)(2,1)} custom-call(s32[2]{0:T(128)S(1)} %pad_add_fusion.place, bf16[16,8,512]{2,1,0:T(8,128)(2,1)S(1)} %copy-done.9, bf16[16,8,512]{2,1,0:T(8,128)(2,1)S(1)} %collective-permute-done.7.rest_1_, bf16[16,8,512]{2,1,0:T(8,128)(2,1)S(1)} %collective-permute-done.8.rest_2_, bf16[16,8,512]{2,1,0:T(8,128)(2,1)S(1)} %copy-done.11, ...), custom_call_target="tpu_custom_call" | custom-call | tf_op jit(solution)/shard_map/project_cols/pallas_call | solution.py:384
  (113 shorter events, 46.9 us)
Async XLA Ops:
  4.2 120.9 %all-to-all-start = ((bf16[16,64,1536]{2,1,0:T(8,128)(2,1)}), bf16[16,64,1536]{2,1,0:T(8,128)(2,1)S(1)}, u32[]{:S(2)}, u32[]{:S(2)}) async-start(bf16[16,64,1536]{2,1,0:T(8,128)(2,1)} %row_pack.1), calls=%async_computation | async-start | bytes 6291456 | tf_op jit(solution)/shard_map/all_to_all | solution.py:478
  19.5 20.3 %collective-permute-start = (bf16[8,16,1536]{2,1,0:T(8,128)(2,1)}, bf16[8,16,1536]{2,1,0:T(8,128)(2,1)S(1)}, u32[]{:S(2)}, u32[]{:S(2)}) collective-permute-start(bf16[8,16,1536]{2,1,0:T(8,128)(2,1)} %get-tuple-element.26), channel_id=1, source_target_pairs={{0,16},{16,0},{32,48},{48,32},{64,80},{80,64},{96,112},{112,96},{1... | collective-permute-start | bytes 1179656 | tf_op jit(solution)/shard_map/ppermute | solution.py:409
  20.5 20.1 %collective-permute-start.1 = (bf16[8,16,1536]{2,1,0:T(8,128)(2,1)}, bf16[8,16,1536]{2,1,0:T(8,128)(2,1)S(1)}, u32[]{:S(2)}, u32[]{:S(2)}) collective-permute-start(bf16[8,16,1536]{2,1,0:T(8,128)(2,1)} %get-tuple-element.27), channel_id=1, source_target_pairs={{0,32},{16,48},{32,0},{48,16},{64,96},{80,112},{96,64},{112,80},{1... | collective-permute-start | bytes 1179656 | tf_op jit(solution)/shard_map/ppermute | solution.py:409
  26.5 19.7 %collective-permute-start.2 = (bf16[8,16,1536]{2,1,0:T(8,128)(2,1)}, bf16[8,16,1536]{2,1,0:T(8,128)(2,1)}, u32[]{:S(2)}, u32[]{:S(2)}) collective-permute-start(bf16[8,16,1536]{2,1,0:T(8,128)(2,1)} %get-tuple-element.28), channel_id=1, source_target_pairs={{0,48},{16,32},{32,16},{48,0},{64,112},{80,96},{96,80},{112,64},{1... | collective-permute-start | bytes 1179656 | tf_op jit(solution)/shard_map/ppermute | solution.py:409
  35.5 26.8 %collective-permute-start.4 = (bf16[8,16,1536]{2,1,0:T(8,128)(2,1)}, bf16[8,16,1536]{2,1,0:T(8,128)(2,1)}, u32[]{:S(2)}, u32[]{:S(2)}) collective-permute-start(bf16[8,16,1536]{2,1,0:T(8,128)(2,1)} %get-tuple-element.30), channel_id=1, source_target_pairs={{0,80},{16,64},{32,112},{48,96},{64,16},{80,0},{96,48},{112,32},{1... | collective-permute-start | bytes 1179656 | tf_op jit(solution)/shard_map/ppermute | solution.py:409
  40.6 29.2 %collective-permute-start.5 = (bf16[8,16,1536]{2,1,0:T(8,128)(2,1)}, bf16[8,16,1536]{2,1,0:T(8,128)(2,1)}, u32[]{:S(2)}, u32[]{:S(2)}) collective-permute-start(bf16[8,16,1536]{2,1,0:T(8,128)(2,1)} %get-tuple-element.31), channel_id=1, source_target_pairs={{0,96},{16,112},{32,64},{48,80},{64,32},{80,48},{96,0},{112,16},{1... | collective-permute-start | bytes 1179656 | tf_op jit(solution)/shard_map/ppermute | solution.py:409
  41.4 35.6 %collective-permute-start.6 = (bf16[8,16,1536]{2,1,0:T(8,128)(2,1)}, bf16[8,16,1536]{2,1,0:T(8,128)(2,1)}, u32[]{:S(2)}, u32[]{:S(2)}) collective-permute-start(bf16[8,16,1536]{2,1,0:T(8,128)(2,1)} %get-tuple-element.32), channel_id=1, source_target_pairs={{0,112},{16,96},{32,80},{48,64},{64,48},{80,32},{96,16},{112,0},{1... | collective-permute-start | bytes 1179656 | tf_op jit(solution)/shard_map/ppermute | solution.py:409
  46.2 42.1 %collective-permute-start.19 = (bf16[4,32,512]{2,1,0:T(8,128)(2,1)}, bf16[4,32,512]{2,1,0:T(8,128)(2,1)S(1)}, u32[]{:S(2)}, u32[]{:S(2)}) collective-permute-start(bf16[4,32,512]{2,1,0:T(8,128)(2,1)} %get-tuple-element.41.refs_0_), channel_id=1, source_target_pairs={{0,3},{1,2},{2,1},{3,0},{4,7},{5,6},{6,5},{7,4},{8,11},{9,10},{10,... | collective-permute-start | bytes 393224 | tf_op jit(solution)/shard_map/ppermute | solution.py:403
  53.6 35.0 %collective-permute-start.18 = (bf16[4,32,512]{2,1,0:T(8,128)(2,1)}, bf16[4,32,512]{2,1,0:T(8,128)(2,1)S(1)}, u32[]{:S(2)}, u32[]{:S(2)}) collective-permute-start(bf16[4,32,512]{2,1,0:T(8,128)(2,1)} %get-tuple-element.41.refs_0_), channel_id=1, source_target_pairs={{0,2},{1,3},{2,0},{3,1},{4,6},{5,7},{6,4},{7,5},{8,10},{9,11},{10,... | collective-permute-start | bytes 393224 | tf_op jit(solution)/shard_map/ppermute | solution.py:403
  62.3 28.1 %collective-permute-start.17 = (bf16[4,32,512]{2,1,0:T(8,128)(2,1)}, bf16[4,32,512]{2,1,0:T(8,128)(2,1)S(1)}, u32[]{:S(2)}, u32[]{:S(2)}) collective-permute-start(bf16[4,32,512]{2,1,0:T(8,128)(2,1)} %get-tuple-element.41.refs_0_), channel_id=1, source_target_pairs={{0,1},{1,0},{2,3},{3,2},{4,5},{5,4},{6,7},{7,6},{8,9},{9,8},{10,11... | collective-permute-start | bytes 393224 | tf_op jit(solution)/shard_map/ppermute | solution.py:403
  69.8 20.6 %collective-permute-start.22 = (bf16[4,32,512]{2,1,0:T(8,128)(2,1)}, bf16[4,32,512]{2,1,0:T(8,128)(2,1)S(1)}, u32[]{:S(2)}, u32[]{:S(2)}) collective-permute-start(bf16[4,32,512]{2,1,0:T(8,128)(2,1)} %get-tuple-element.42.refs_4_), channel_id=1, source_target_pairs={{0,12},{1,13},{2,14},{3,15},{4,8},{5,9},{6,10},{7,11},{8,4},{9,5},... | collective-permute-start | bytes 393224 | tf_op jit(solution)/shard_map/ppermute | solution.py:403
  94.3 25.0 %collective-permute-start.25 = (bf16[4,4,32,512]{3,2,1,0:T(8,128)(2,1)}, bf16[4,4,32,512]{3,2,1,0:T(8,128)(2,1)}, u32[]{:S(2)}, u32[]{:S(2)}) collective-permute-start(bf16[4,4,32,512]{3,2,1,0:T(8,128)(2,1)} %get-tuple-element.43.rest_8_), channel_id=1, source_target_pairs={{0,3},{1,2},{2,1},{3,0},{4,7},{5,6},{6,5},{7,4},{8,11},{9,10},{10,... | collective-permute-start | bytes 1572872 | tf_op jit(solution)/shard_map/ppermute | solution.py:403
  96.7 22.6 %collective-permute-start.24 = (bf16[4,4,32,512]{3,2,1,0:T(8,128)(2,1)}, bf16[4,4,32,512]{3,2,1,0:T(8,128)(2,1)}, u32[]{:S(2)}, u32[]{:S(2)}) collective-permute-start(bf16[4,4,32,512]{3,2,1,0:T(8,128)(2,1)} %get-tuple-element.43.rest_8_), channel_id=1, source_target_pairs={{0,2},{1,3},{2,0},{3,1},{4,6},{5,7},{6,4},{7,5},{8,10},{9,11},{10,... | collective-permute-start | bytes 1572872 | tf_op jit(solution)/shard_map/ppermute | solution.py:403
  97.3 24.4 %collective-permute-start.32 = (bf16[4,4,32,512]{3,2,1,0:T(8,128)(2,1)}, bf16[4,4,32,512]{3,2,1,0:T(8,128)(2,1)}, u32[]{:S(2)}, u32[]{:S(2)}) collective-permute-start(bf16[4,4,32,512]{3,2,1,0:T(8,128)(2,1)} %get-tuple-element.44.rest_0_), channel_id=1, source_target_pairs={{0,12},{1,13},{2,14},{3,15},{4,8},{5,9},{6,10},{7,11},{8,4},{9,5},... | collective-permute-start | bytes 1572872 | tf_op jit(solution)/shard_map/ppermute | solution.py:403
  99.8 24.6 %collective-permute-start.31 = (bf16[4,4,32,512]{3,2,1,0:T(8,128)(2,1)}, bf16[4,4,32,512]{3,2,1,0:T(8,128)(2,1)}, u32[]{:S(2)}, u32[]{:S(2)}) collective-permute-start(bf16[4,4,32,512]{3,2,1,0:T(8,128)(2,1)} %get-tuple-element.44.rest_0_), channel_id=1, source_target_pairs={{0,8},{1,9},{2,10},{3,11},{4,12},{5,13},{6,14},{7,15},{8,0},{9,1},... | collective-permute-start | bytes 1572872 | tf_op jit(solution)/shard_map/ppermute | solution.py:403
  116.3 20.8 %collective-permute-start.30 = (bf16[4,4,32,512]{3,2,1,0:T(8,128)(2,1)}, bf16[4,4,32,512]{3,2,1,0:T(8,128)(2,1)}, u32[]{:S(2)}, u32[]{:S(2)}) collective-permute-start(bf16[4,4,32,512]{3,2,1,0:T(8,128)(2,1)} %get-tuple-element.44.rest_0_), channel_id=1, source_target_pairs={{0,4},{1,5},{2,6},{3,7},{4,0},{5,1},{6,2},{7,3},{8,12},{9,13},{10,... | collective-permute-start | bytes 1572872 | tf_op jit(solution)/shard_map/ppermute | solution.py:403
  119.3 18.6 %collective-permute-start.23 = (bf16[4,4,32,512]{3,2,1,0:T(8,128)(2,1)}, bf16[4,4,32,512]{3,2,1,0:T(8,128)(2,1)}, u32[]{:S(2)}, u32[]{:S(2)}) collective-permute-start(bf16[4,4,32,512]{3,2,1,0:T(8,128)(2,1)} %get-tuple-element.43.rest_8_), channel_id=1, source_target_pairs={{0,1},{1,0},{2,3},{3,2},{4,5},{5,4},{6,7},{7,6},{8,9},{9,8},{10,11... | collective-permute-start | bytes 1572872 | tf_op jit(solution)/shard_map/ppermute | solution.py:403
  119.4 18.7 %collective-permute-start.33 = (bf16[4,4,32,512]{3,2,1,0:T(8,128)(2,1)}, bf16[4,4,32,512]{3,2,1,0:T(8,128)(2,1)}, u32[]{:S(2)}, u32[]{:S(2)}) collective-permute-start(bf16[4,4,32,512]{3,2,1,0:T(8,128)(2,1)} %get-tuple-element.44.rest_0_), channel_id=1, source_target_pairs={{0,16},{16,0},{32,48},{48,32},{64,80},{80,64},{96,112},{112,96},{1... | collective-permute-start | bytes 1572872 | tf_op jit(solution)/shard_map/ppermute | solution.py:403
  132.9 19.9 %all-to-all-start.1 = ((bf16[16,64,512]{2,1,0:T(8,128)(2,1)}), bf16[16,64,512]{2,1,0:T(8,128)(2,1)S(1)}, u32[]{:S(2)}, u32[]{:S(2)}) async-start(bf16[16,64,512]{2,1,0:T(8,128)(2,1)} %bitcast.5), calls=%async_computation.1 | async-start | bytes 2097152 | tf_op jit(solution)/shard_map/all_to_all | solution.py:489
  137.9 26.2 %collective-permute-start.26 = (bf16[4,4,32,512]{3,2,1,0:T(8,128)(2,1)}, bf16[4,4,32,512]{3,2,1,0:T(8,128)(2,1)}, u32[]{:S(2)}, u32[]{:S(2)}) collective-permute-start(bf16[4,4,32,512]{3,2,1,0:T(8,128)(2,1)} %get-tuple-element.43.rest_8_), channel_id=1, source_target_pairs={{0,16},{16,0},{32,48},{48,32},{64,80},{80,64},{96,112},{112,96},{1... | collective-permute-start | bytes 1572872 | tf_op jit(solution)/shard_map/ppermute | solution.py:403
  138.0 26.1 %collective-permute-start.29 = (bf16[4,4,32,512]{3,2,1,0:T(8,128)(2,1)}, bf16[4,4,32,512]{3,2,1,0:T(8,128)(2,1)}, u32[]{:S(2)}, u32[]{:S(2)}) collective-permute-start(bf16[4,4,32,512]{3,2,1,0:T(8,128)(2,1)} %collective-permute-done.25.rest_11_), channel_id=1, source_target_pairs={{0,16},{16,0},{32,48},{48,32},{64,80},{80,64},{96,112},{112,96},{1... | collective-permute-start | bytes 1572872 | tf_op jit(solution)/shard_map/ppermute | solution.py:403
  138.4 25.7 %collective-permute-start.28 = (bf16[4,4,32,512]{3,2,1,0:T(8,128)(2,1)}, bf16[4,4,32,512]{3,2,1,0:T(8,128)(2,1)}, u32[]{:S(2)}, u32[]{:S(2)}) collective-permute-start(bf16[4,4,32,512]{3,2,1,0:T(8,128)(2,1)} %collective-permute-done.24.rest_10_), channel_id=1, source_target_pairs={{0,16},{16,0},{32,48},{48,32},{64,80},{80,64},{96,112},{112,96},{1... | collective-permute-start | bytes 1572872 | tf_op jit(solution)/shard_map/ppermute | solution.py:403
  138.7 25.5 %collective-permute-start.27 = (bf16[4,4,32,512]{3,2,1,0:T(8,128)(2,1)}, bf16[4,4,32,512]{3,2,1,0:T(8,128)(2,1)}, u32[]{:S(2)}, u32[]{:S(2)}) collective-permute-start(bf16[4,4,32,512]{3,2,1,0:T(8,128)(2,1)} %collective-permute-done.23.rest_9_), channel_id=1, source_target_pairs={{0,16},{16,0},{32,48},{48,32},{64,80},{80,64},{96,112},{112,96},{1... | collective-permute-start | bytes 1572872 | tf_op jit(solution)/shard_map/ppermute | solution.py:403
  140.5 23.6 %collective-permute-start.13 = (bf16[16,8,512]{2,1,0:T(8,128)(2,1)}, bf16[16,8,512]{2,1,0:T(8,128)(2,1)}, u32[]{:S(2)}, u32[]{:S(2)}) collective-permute-start(bf16[16,8,512]{2,1,0:T(8,128)(2,1)} %get-tuple-element.40), channel_id=1, source_target_pairs={{0,112},{16,96},{32,80},{48,64},{64,48},{80,32},{96,16},{112,0},{1... | collective-permute-start | bytes 393224 | tf_op jit(solution)/shard_map/ppermute | solution.py:409
  (37 other events, 404.3 us)

commit v8 on v5

--- a/solution.py
+++ b/solution.py
@@ -183,9 +183,8 @@
     lax.fori_loop(0, blocks // UNROLL, group, 0)
 
 
-def row_attend(pattern, count, x):
+def row_attend(pattern, chosen, count, x):
     cells = x.shape[0] * x.shape[1]
-    chosen = pattern.shape[-1]
     return pl.pallas_call(
         functools.partial(row_attend_kernel, chosen=chosen),
         grid_spec=pltpu.PrefetchScalarGridSpec(
@@ -197,7 +196,7 @@
         out_shape=jax.ShapeDtypeStruct((cells, HR * HD), x.dtype),
         compiler_params=grant(56),
         name="row_attend",
-    )(pattern.reshape(-1), count, in_place(x))
+    )(pattern, count, in_place(x))
 
 
 def col_attend_kernel(me_ref, pattern_ref, count_ref, *rest, chosen, lines):
@@ -259,11 +258,10 @@
                 outs[s][:, :, h * HD : (h + 1) * HD] = part.astype(jnp.bfloat16)
 
 
-def col_attend(me, pattern, count, pieces):
+def col_attend(me, pattern, chosen, count, pieces):
     peers = len(pieces)
     own, span, wide = pieces[0].shape
     width = HC * HD
-    chosen = pattern.shape[-1]
     lines = 2
     result = (span, own, width)
     return pl.pallas_call(
@@ -281,7 +279,7 @@
         out_shape=[jax.ShapeDtypeStruct(result, jnp.bfloat16)] * peers,
         compiler_params=grant(56),
         name="col_attend",
-    )(me, pattern.reshape(-1), count, pieces[0], *[in_place(p) for p in pieces[1:]])
+    )(me, pattern, count, pieces[0], *[in_place(p) for p in pieces[1:]])
 
 
 def project_kernel(place, row_ref, *rest, peers, near):
@@ -382,26 +380,51 @@
     ]
 
 
+def join_kernel(*refs):
+    parts, outs = refs[:-2], refs[-2:]
+    each = len(parts) // 2
+    for i, part in enumerate(parts):
+        outs[i // each][i % each] = part[...]
+
+
+def join_both(first, second):
+    held = pl.BlockSpec(memory_space=pltpu.VMEM)
+    whole = jax.ShapeDtypeStruct((len(first),) + first[0].shape, first[0].dtype)
+    return pl.pallas_call(
+        join_kernel,
+        in_specs=[held] * (len(first) + len(second)),
+        out_specs=[held, held],
+        out_shape=[whole, whole],
+        compiler_params=grant(56),
+        name="join_both",
+    )(
+        first[0],
+        *[in_place(p) for p in first[1:]],
+        second[0],
+        *[in_place(p) for p in second[1:]],
+    )
+
+
 def halve_kernel(*refs):
-    parts, (upper, lower) = refs[:-2], refs[-2:]
+    parts, (upper, lower) = refs[:-6], refs[-2:]
     middle = upper.shape[2]
     for i, part in enumerate(parts):
         upper[i] = part[:, :middle]
         lower[i] = part[:, middle:]
 
 
-def halve(parts):
+def halve(parts, tables):
     span, channels = parts[0].shape
     half = jax.ShapeDtypeStruct((len(parts), span, channels // 2), parts[0].dtype)
     held = pl.BlockSpec(memory_space=pltpu.VMEM)
     return pl.pallas_call(
         halve_kernel,
-        in_specs=[held] * len(parts),
+        in_specs=[held] * len(parts) + [pl.BlockSpec(memory_space=pl.ANY)] * len(tables),
         out_specs=[held, held],
         out_shape=[half, half],
         compiler_params=grant(56),
         name="halve",
-    )(parts[0], *[in_place(p) for p in parts[1:]])
+    )(parts[0], *[in_place(p) for p in parts[1:]], *tables)
 
 
 def body(
@@ -412,7 +435,9 @@
     row_share = row_span // lax.axis_size("cols")
     me = lax.axis_index("rows").astype(jnp.int32).reshape(1)
     row_first = lax.axis_index("cols") * row_share
-    pattern = lax.dynamic_slice_in_dim(row_pattern, row_first, row_share, 0)
+    chosen = row_pattern.shape[-1]
+    pattern = lax.dynamic_slice_in_dim(row_pattern, row_first, row_share, 0).reshape(-1)
+    col_listed = col_pattern.reshape(-1)
     count = lax.dynamic_slice_in_dim(row_count, row_first, row_share, 0)
 
     place = jnp.stack([lax.axis_index("rows"), lax.axis_index("cols")]).astype(jnp.int32)
@@ -423,18 +448,21 @@
     along_y = [shard] + by_xor(shard, "rows", (2, 4, 6))
     sent = col_pack(me, query_cells, key_cells, value_cells, peers)
     pieces = swap_pieces(sent)
-    upper, lower = halve(along_y)
+    upper, lower = halve(along_y, (pattern, col_listed, count, place))
     along_z = [upper] + by_xor(upper, "cols", (1, 2, 3))
     along_x = [lower] + by_xor(lower, "cols", (4, 8, 12))
-    upper, lower = jnp.stack(along_z), jnp.stack(along_x)
-    weights = [upper] + by_xor(upper, "cols", (4, 8, 12))
-    weights += [lower] + by_xor(lower, "cols", (1, 2, 3))
-    row_out = row_attend(pattern, count, lines)
+    upper, lower = join_both(along_z, along_x)
+    uppers = [upper] + by_xor(upper, "cols", (4, 8, 12))
+    lowers = [lower] + by_xor(lower, "cols", (1, 2, 3))
+    row_out = row_attend(pattern, chosen, count, lines)
     row_out = lax.all_to_all(row_out.reshape(row_span, col_span, -1), "cols", 0, 0, tiled=True)
-    col_out = col_attend(me, col_pattern, col_count, pieces)
+    col_out = col_attend(me, col_listed, col_pattern.shape[-1], col_count, pieces)
     col_out = swap_pieces(col_out)
-    weights += [by_xor(w, "rows", (1,))[0] for w in weights]
+    uppers += [by_xor(w, "rows", (1,))[0] for w in uppers]
+    lowers += [by_xor(w, "rows", (1,))[0] for w in lowers]
     outs = out_weight.shape[1] * peers * lax.axis_size("cols")
+    near = len(along_z)
+    weights = uppers[:near] + lowers[:near] + uppers[near:] + lowers[near:]
     projected = project(place, row_out, col_out, weights, outs)
     return projected.reshape(row_span, col_span, projected.shape[-1])
 

time: 191 us -> 187 us (0.979)
  local copies, waits for them, and re-layouts: 21.6 us -> 15.7 us
  other arithmetic: 4.45 us -> 0.61 us
  Pallas kernels: 40.9 us -> 44.1 us
  waiting for transfers between devices: 56.5 us -> 58.5 us
    ppermute x23, waiting for transfers between devices: 18.7 us -> 25.9 us  [by_xor(): lax.ppermute(x, axis, [(d, d ^ s) for d in range(size)])]
    all_to_all x1, waiting for transfers between devices: 6.45 us -> 0.01 us  [body(): lax.all_to_all(row_out.reshape(row_span, col_span, -1), 'cols', 0, 0, til...]
    unnamed x67 -> x53, local copies, waits for them, and re-layouts: 19.4 us -> 13.6 us
    another operation x2 -> x0, other arithmetic: 3.86 us -> none  [body(): upper, lower = (jnp.stack(along_z), jnp.stack(along_x))]
    pallas_call x1 -> x2, Pallas kernels: 1.58 us -> 4.23 us  [the longest x1 2.19 us: halve(): pl.pallas_call(halve_kernel, in_specs=[held] * len(parts) + [pl.BlockSpec...]
    ppermute x23, starting transfers between devices: 29.8 us -> 32.1 us  [by_xor(): lax.ppermute(x, axis, [(d, d ^ s) for d in range(size)])]
  transfers between devices with their start and end apart: 39 -> 39, of which waited for: 17 -> 14; matrix products, arithmetic and copies ran while one was open for 4% -> 2% of each run, Pallas kernels for 12% -> 14%
where the time goes in v8:
time: 187 us; the launch traced here: 185 us
  starting transfers between devices  65.9 us (35%)
  waiting for transfers between devices  58.5 us (31%)
  Pallas kernels  44.1 us (24%)
  local copies, waits for them, and re-layouts  15.7 us (8%)
    ppermute x14, waiting for transfers between devices, swap_pieces(): lax.ppermute(pieces[s], 'rows', [(d, d ^ s) for d in range(peers)])  32.6 us
    ppermute x23, starting transfers between devices, by_xor(): lax.ppermute(x, axis, [(d, d ^ s) for d in range(size)])  32.1 us
    ppermute x23, waiting for transfers between devices, by_xor(): lax.ppermute(x, axis, [(d, d ^ s) for d in range(size)])  25.9 us
    ppermute x14, starting transfers between devices, swap_pieces(): lax.ppermute(pieces[s], 'rows', [(d, d ^ s) for d in range(peers)])  20.1 us
    pallas_call x1, Pallas kernels, project(): pl.pallas_call(functools.partial(project_kernel, peers=len(pieces), near=...  14.9 us
    unnamed x53, local copies, waits for them, and re-layouts  13.6 us
    all_to_all x1, starting transfers between devices, body(): lines = lax.all_to_all(packed, 'cols', 0, 0, tiled=True)  8.42 us
    pallas_call x1, Pallas kernels, row_attend(): pl.pallas_call(functools.partial(row_attend_kernel, chosen=chosen), grid_...  7.69 us
  transfers between devices with their start and end apart: 39, of which 14 were waited for; matrix products, arithmetic and copies ran while one was open for 2% of the time, Pallas kernels for 14%

profile of v8, /device:TPU:1, one launch (start us, length us, event | category | flops | bytes accessed | tf_op | source)
XLA Modules:
  0.0 185.2 jit_solution(6212130935232507253)
XLA Ops:
  0.0 4.2 %row_pack.1 = bf16[16,64,1536]{2,1,0:T(8,128)(2,1)} custom-call(bf16[16,64,1024]{2,1,0:T(8,128)(2,1)} %q_ref.3, bf16[16,64,1024]{2,1,0:T(8,128)(2,1)} %k_ref.3, bf16[16,64,1024]{2,1,0:T(8,128)(2,1)} %v_ref.3), custom_call_target="tpu_custom_call" | custom-call | tf_op jit(solution)/shard_map/row_pack/pallas_call | solution.py:41
  4.2 8.4 %all-to-all-start = ((bf16[16,64,1536]{2,1,0:T(8,128)(2,1)}), bf16[16,64,1536]{2,1,0:T(8,128)(2,1)S(1)}, u32[]{:S(2)}, u32[]{:S(2)}) async-start(bf16[16,64,1536]{2,1,0:T(8,128)(2,1)} %row_pack.1), calls=%async_computation | async-start | bytes 6291456 | tf_op jit(solution)/shard_map/all_to_all | solution.py:447
  12.6 6.9 %col_pack.1 = (bf16[8,16,1536]{2,1,0:T(8,128)(2,1)}, bf16[8,16,1536]{2,1,0:T(8,128)(2,1)}, bf16[8,16,1536]{2,1,0:T(8,128)(2,1)}, bf16[8,16,1536]{2,1,0:T(8,128)(...) custom-call(s32[1]{0:T(128)} %bitcast.me_ref, ...), custom_call_target="tpu_custom_call" | custom-call | tf_op jit(solution)/shard_map/col_pack/pallas_call | solution.py:92
  27.1 8.1 %collective-permute-done.15.refs_2_ = bf16[32,1024]{1,0:T(8,128)(2,1)S(1)} collective-permute-done((bf16[32,1024]{1,0:T(8,128)(2,1)S(1)}, bf16[32,1024]{1,0:T(8,128)(2,1)S(1)}, u32[]{:S(2)}, u32[]{:S(2)}) %collective-permute-start.15) | collective-permute-done | bytes 65568 | tf_op jit(solution)/shard_map/ppermute | solution.py:372
  35.5 4.3 %collective-permute-start.4 = (bf16[8,16,1536]{2,1,0:T(8,128)(2,1)}, bf16[8,16,1536]{2,1,0:T(8,128)(2,1)}, u32[]{:S(2)}, u32[]{:S(2)}) collective-permute-start(bf16[8,16,1536]{2,1,0:T(8,128)(2,1)} %get-tuple-element.30), channel_id=1, source_target_pairs={{0,80},{16,64},{32,112},{48,96},{64,16},{80,0},{96,48},{112,32},{1... | collective-permute-start | bytes 1179656 | tf_op jit(solution)/shard_map/ppermute | solution.py:378
  47.9 2.8 %collective-permute-start.19 = (bf16[4,32,512]{2,1,0:T(8,128)(2,1)}, bf16[4,32,512]{2,1,0:T(8,128)(2,1)S(1)}, u32[]{:S(2)}, u32[]{:S(2)}) collective-permute-start(bf16[4,32,512]{2,1,0:T(8,128)(2,1)} %get-tuple-element.41.refs_0_), channel_id=1, source_target_pairs={{0,3},{1,2},{2,1},{3,0},{4,7},{5,6},{6,5},{7,4},{8,11},{9,10},{10,... | collective-permute-start | bytes 393224 | tf_op jit(solution)/shard_map/ppermute | solution.py:372
  50.8 2.8 %collective-permute-done.3.rest_4_ = bf16[8,16,1536]{2,1,0:T(8,128)(2,1)} collective-permute-done((bf16[8,16,1536]{2,1,0:T(8,128)(2,1)}, bf16[8,16,1536]{2,1,0:T(8,128)(2,1)}, u32[]{:S(2)}, u32[]{:S(2)}) %collective-permute-start.3) | collective-permute-done | bytes 393248 | tf_op jit(solution)/shard_map/ppermute | solution.py:378
  53.6 3.1 %collective-permute-start.18 = (bf16[4,32,512]{2,1,0:T(8,128)(2,1)}, bf16[4,32,512]{2,1,0:T(8,128)(2,1)S(1)}, u32[]{:S(2)}, u32[]{:S(2)}) collective-permute-start(bf16[4,32,512]{2,1,0:T(8,128)(2,1)} %get-tuple-element.41.refs_0_), channel_id=1, source_target_pairs={{0,2},{1,3},{2,0},{3,1},{4,6},{5,7},{6,4},{7,5},{8,10},{9,11},{10,... | collective-permute-start | bytes 393224 | tf_op jit(solution)/shard_map/ppermute | solution.py:372
  56.7 5.6 %collective-permute-done.4.rest_5_ = bf16[8,16,1536]{2,1,0:T(8,128)(2,1)} collective-permute-done((bf16[8,16,1536]{2,1,0:T(8,128)(2,1)}, bf16[8,16,1536]{2,1,0:T(8,128)(2,1)}, u32[]{:S(2)}, u32[]{:S(2)}) %collective-permute-start.4) | collective-permute-done | bytes 393248 | tf_op jit(solution)/shard_map/ppermute | solution.py:378
  64.0 5.8 %collective-permute-done.5.rest_6_ = bf16[8,16,1536]{2,1,0:T(8,128)(2,1)} collective-permute-done((bf16[8,16,1536]{2,1,0:T(8,128)(2,1)}, bf16[8,16,1536]{2,1,0:T(8,128)(2,1)}, u32[]{:S(2)}, u32[]{:S(2)}) %collective-permute-start.5) | collective-permute-done | bytes 393248 | tf_op jit(solution)/shard_map/ppermute | solution.py:378
  69.8 2.9 %collective-permute-start.22 = (bf16[4,32,512]{2,1,0:T(8,128)(2,1)}, bf16[4,32,512]{2,1,0:T(8,128)(2,1)S(1)}, u32[]{:S(2)}, u32[]{:S(2)}) collective-permute-start(bf16[4,32,512]{2,1,0:T(8,128)(2,1)} %get-tuple-element.42.refs_4_), channel_id=1, source_target_pairs={{0,12},{1,13},{2,14},{3,15},{4,8},{5,9},{6,10},{7,11},{8,4},{9,5},... | collective-permute-start | bytes 393224 | tf_op jit(solution)/shard_map/ppermute | solution.py:372
  72.7 4.3 %collective-permute-done.6.rest_7_ = bf16[8,16,1536]{2,1,0:T(8,128)(2,1)} collective-permute-done((bf16[8,16,1536]{2,1,0:T(8,128)(2,1)}, bf16[8,16,1536]{2,1,0:T(8,128)(2,1)}, u32[]{:S(2)}, u32[]{:S(2)}) %collective-permute-start.6) | collective-permute-done | bytes 393248 | tf_op jit(solution)/shard_map/ppermute | solution.py:378
  76.9 3.1 %collective-permute-start.21 = (bf16[4,32,512]{2,1,0:T(8,128)(2,1)}, bf16[4,32,512]{2,1,0:T(8,128)(2,1)S(1)}, u32[]{:S(2)}, u32[]{:S(2)}) collective-permute-start(bf16[4,32,512]{2,1,0:T(8,128)(2,1)} %get-tuple-element.42.refs_4_), channel_id=1, source_target_pairs={{0,8},{1,9},{2,10},{3,11},{4,12},{5,13},{6,14},{7,15},{8,0},{9,1},... | collective-permute-start | bytes 393224 | tf_op jit(solution)/shard_map/ppermute | solution.py:372
  82.0 6.2 %col_attend.1 = (bf16[16,8,512]{2,1,0:T(8,128)(2,1)}, bf16[16,8,512]{2,1,0:T(8,128)(2,1)}, bf16[16,8,512]{2,1,0:T(8,128)(2,1)}, bf16[16,8,512]{2,1,0:T(8,128)(2,...) custom-call(s32[1]{0:T(128)} %bitcast.me_ref, ...), custom_call_target="tpu_custom_call" | custom-call | tf_op jit(solution)/shard_map/col_attend/pallas_call | solution.py:267
  94.4 2.5 %collective-permute-start.29 = (bf16[4,4,32,512]{3,2,1,0:T(8,128)(2,1)}, bf16[4,4,32,512]{3,2,1,0:T(8,128)(2,1)S(1)}, u32[]{:S(2)}, u32[]{:S(2)}) collective-permute-start(bf16[4,4,32,512]{3,2,1,0:T(8,128)(2,1)} %get-tuple-element.43.rest_8_), channel_id=1, source_target_pairs={{0,16},{16,0},{32,48},{48,32},{64,80},{80,64},{96,112},{112,96},{1... | collective-permute-start | bytes 1572872 | tf_op jit(solution)/shard_map/ppermute | solution.py:372
  104.2 5.6 %collective-permute-done.11.rest_5_ = bf16[16,8,512]{2,1,0:T(8,128)(2,1)S(1)} collective-permute-done((bf16[16,8,512]{2,1,0:T(8,128)(2,1)}, bf16[16,8,512]{2,1,0:T(8,128)(2,1)S(1)}, u32[]{:S(2)}, u32[]{:S(2)}) %collective-permute-start.11) | collective-permute-done | bytes 131104 | tf_op jit(solution)/shard_map/ppermute | solution.py:378
  112.5 3.9 %collective-permute-done.12.rest_6_ = bf16[16,8,512]{2,1,0:T(8,128)(2,1)S(1)} collective-permute-done((bf16[16,8,512]{2,1,0:T(8,128)(2,1)}, bf16[16,8,512]{2,1,0:T(8,128)(2,1)S(1)}, u32[]{:S(2)}, u32[]{:S(2)}) %collective-permute-start.12) | collective-permute-done | bytes 131104 | tf_op jit(solution)/shard_map/ppermute | solution.py:378
  117.0 3.3 %collective-permute-start.13 = (bf16[16,8,512]{2,1,0:T(8,128)(2,1)}, bf16[16,8,512]{2,1,0:T(8,128)(2,1)S(1)}, u32[]{:S(2)}, u32[]{:S(2)}) collective-permute-start(bf16[16,8,512]{2,1,0:T(8,128)(2,1)} %get-tuple-element.40), channel_id=1, source_target_pairs={{0,112},{16,96},{32,80},{48,64},{64,48},{80,32},{96,16},{112,0},{1... | collective-permute-start | bytes 393224 | tf_op jit(solution)/shard_map/ppermute | solution.py:378
  120.3 4.2 %collective-permute-done.13.rest_7_ = bf16[16,8,512]{2,1,0:T(8,128)(2,1)S(1)} collective-permute-done((bf16[16,8,512]{2,1,0:T(8,128)(2,1)}, bf16[16,8,512]{2,1,0:T(8,128)(2,1)S(1)}, u32[]{:S(2)}, u32[]{:S(2)}) %collective-permute-start.13) | collective-permute-done | bytes 131104 | tf_op jit(solution)/shard_map/ppermute | solution.py:378
  125.9 2.4 %collective-permute-start.28 = (bf16[4,4,32,512]{3,2,1,0:T(8,128)(2,1)}, bf16[4,4,32,512]{3,2,1,0:T(8,128)(2,1)}, u32[]{:S(2)}, u32[]{:S(2)}) collective-permute-start(bf16[4,4,32,512]{3,2,1,0:T(8,128)(2,1)} %get-tuple-element.44.rest_12_), channel_id=1, source_target_pairs={{0,3},{1,2},{2,1},{3,0},{4,7},{5,6},{6,5},{7,4},{8,11},{9,10},{10,... | collective-permute-start | bytes 1572872 | tf_op jit(solution)/shard_map/ppermute | solution.py:372
  131.2 7.7 %row_attend.1 = bf16[1024,512]{1,0:T(8,128)(2,1)} custom-call(s32[192]{0:T(256)} %reshape.13.pattern_ref.refs_4_, s32[1]{0:T(128)} %dynamic_slice.7.count_ref.refs_6_, bf16[16,64,1536]{2,1,0:T(8,128)(2,1)S(1)} %all-to-all-done.x_ref), custom_call_target="tpu_custom_call" | custom-call | tf_op jit(solution)/shard_map/row_attend/pallas_call | solution.py:188
  138.9 5.3 %all-to-all-start.1 = ((bf16[16,64,512]{2,1,0:T(8,128)(2,1)}), bf16[16,64,512]{2,1,0:T(8,128)(2,1)S(1)}, u32[]{:S(2)}, u32[]{:S(2)}) async-start(bf16[16,64,512]{2,1,0:T(8,128)(2,1)} %bitcast.5), calls=%async_computation.1 | async-start | bytes 2097152 | tf_op jit(solution)/shard_map/all_to_all | solution.py:458
  144.8 14.6 %collective-permute-done.28.rest_15_ = bf16[4,4,32,512]{3,2,1,0:T(8,128)(2,1)} collective-permute-done((bf16[4,4,32,512]{3,2,1,0:T(8,128)(2,1)}, bf16[4,4,32,512]{3,2,1,0:T(8,128)(2,1)}, u32[]{:S(2)}, u32[]{:S(2)}) %collective-permute-start.28) | collective-permute-done | bytes 524320 | tf_op jit(solution)/shard_map/ppermute | solution.py:372
  170.1 14.9 %project.1 = bf16[1024,4096]{1,0:T(8,128)(2,1)} custom-call(s32[2]{0:T(128)} %pad_add_fusion.refs_7_.place, bf16[16,64,512]{2,1,0:T(8,128)(2,1)S(1)} %all-to-all-done.1.row_ref, bf16[16,8,512]{2,1,0:T(8,128)(2,1)} %get-tuple-element.33.rest_0_, bf16[16,8,512]{2,1,0:T(8,128)(2,1)S(1)} %collective-permute-done.7.rest_1_, ...), custom_call_target="tpu_custom_call" | custom-call | tf_op jit(solution)/shard_map/project/pallas_call | solution.py:350
  (120 shorter events, 51.9 us)
Async XLA Ops:
  4.2 127.0 %all-to-all-start = ((bf16[16,64,1536]{2,1,0:T(8,128)(2,1)}), bf16[16,64,1536]{2,1,0:T(8,128)(2,1)S(1)}, u32[]{:S(2)}, u32[]{:S(2)}) async-start(bf16[16,64,1536]{2,1,0:T(8,128)(2,1)} %row_pack.1), calls=%async_computation | async-start | bytes 6291456 | tf_op jit(solution)/shard_map/all_to_all | solution.py:447
  19.5 20.3 %collective-permute-start = (bf16[8,16,1536]{2,1,0:T(8,128)(2,1)}, bf16[8,16,1536]{2,1,0:T(8,128)(2,1)S(1)}, u32[]{:S(2)}, u32[]{:S(2)}) collective-permute-start(bf16[8,16,1536]{2,1,0:T(8,128)(2,1)} %get-tuple-element.26), channel_id=1, source_target_pairs={{0,16},{16,0},{32,48},{48,32},{64,80},{80,64},{96,112},{112,96},{1... | collective-permute-start | bytes 1179656 | tf_op jit(solution)/shard_map/ppermute | solution.py:378
  20.5 20.1 %collective-permute-start.1 = (bf16[8,16,1536]{2,1,0:T(8,128)(2,1)}, bf16[8,16,1536]{2,1,0:T(8,128)(2,1)S(1)}, u32[]{:S(2)}, u32[]{:S(2)}) collective-permute-start(bf16[8,16,1536]{2,1,0:T(8,128)(2,1)} %get-tuple-element.27), channel_id=1, source_target_pairs={{0,32},{16,48},{32,0},{48,16},{64,96},{80,112},{96,64},{112,80},{1... | collective-permute-start | bytes 1179656 | tf_op jit(solution)/shard_map/ppermute | solution.py:378
  26.5 21.5 %collective-permute-start.2 = (bf16[8,16,1536]{2,1,0:T(8,128)(2,1)}, bf16[8,16,1536]{2,1,0:T(8,128)(2,1)}, u32[]{:S(2)}, u32[]{:S(2)}) collective-permute-start(bf16[8,16,1536]{2,1,0:T(8,128)(2,1)} %get-tuple-element.28), channel_id=1, source_target_pairs={{0,48},{16,32},{32,16},{48,0},{64,112},{80,96},{96,80},{112,64},{1... | collective-permute-start | bytes 1179656 | tf_op jit(solution)/shard_map/ppermute | solution.py:378
  35.2 18.4 %collective-permute-start.3 = (bf16[8,16,1536]{2,1,0:T(8,128)(2,1)}, bf16[8,16,1536]{2,1,0:T(8,128)(2,1)}, u32[]{:S(2)}, u32[]{:S(2)}) collective-permute-start(bf16[8,16,1536]{2,1,0:T(8,128)(2,1)} %get-tuple-element.29), channel_id=1, source_target_pairs={{0,64},{16,80},{32,96},{48,112},{64,0},{80,16},{96,32},{112,48},{1... | collective-permute-start | bytes 1179656 | tf_op jit(solution)/shard_map/ppermute | solution.py:378
  35.5 26.8 %collective-permute-start.4 = (bf16[8,16,1536]{2,1,0:T(8,128)(2,1)}, bf16[8,16,1536]{2,1,0:T(8,128)(2,1)}, u32[]{:S(2)}, u32[]{:S(2)}) collective-permute-start(bf16[8,16,1536]{2,1,0:T(8,128)(2,1)} %get-tuple-element.30), channel_id=1, source_target_pairs={{0,80},{16,64},{32,112},{48,96},{64,16},{80,0},{96,48},{112,32},{1... | collective-permute-start | bytes 1179656 | tf_op jit(solution)/shard_map/ppermute | solution.py:378
  40.6 29.2 %collective-permute-start.5 = (bf16[8,16,1536]{2,1,0:T(8,128)(2,1)}, bf16[8,16,1536]{2,1,0:T(8,128)(2,1)}, u32[]{:S(2)}, u32[]{:S(2)}) collective-permute-start(bf16[8,16,1536]{2,1,0:T(8,128)(2,1)} %get-tuple-element.31), channel_id=1, source_target_pairs={{0,96},{16,112},{32,64},{48,80},{64,32},{80,48},{96,0},{112,16},{1... | collective-permute-start | bytes 1179656 | tf_op jit(solution)/shard_map/ppermute | solution.py:378
  41.3 35.6 %collective-permute-start.6 = (bf16[8,16,1536]{2,1,0:T(8,128)(2,1)}, bf16[8,16,1536]{2,1,0:T(8,128)(2,1)}, u32[]{:S(2)}, u32[]{:S(2)}) collective-permute-start(bf16[8,16,1536]{2,1,0:T(8,128)(2,1)} %get-tuple-element.32), channel_id=1, source_target_pairs={{0,112},{16,96},{32,80},{48,64},{64,48},{80,32},{96,16},{112,0},{1... | collective-permute-start | bytes 1179656 | tf_op jit(solution)/shard_map/ppermute | solution.py:378
  47.9 40.3 %collective-permute-start.19 = (bf16[4,32,512]{2,1,0:T(8,128)(2,1)}, bf16[4,32,512]{2,1,0:T(8,128)(2,1)S(1)}, u32[]{:S(2)}, u32[]{:S(2)}) collective-permute-start(bf16[4,32,512]{2,1,0:T(8,128)(2,1)} %get-tuple-element.41.refs_0_), channel_id=1, source_target_pairs={{0,3},{1,2},{2,1},{3,0},{4,7},{5,6},{6,5},{7,4},{8,11},{9,10},{10,... | collective-permute-start | bytes 393224 | tf_op jit(solution)/shard_map/ppermute | solution.py:372
  53.6 35.0 %collective-permute-start.18 = (bf16[4,32,512]{2,1,0:T(8,128)(2,1)}, bf16[4,32,512]{2,1,0:T(8,128)(2,1)S(1)}, u32[]{:S(2)}, u32[]{:S(2)}) collective-permute-start(bf16[4,32,512]{2,1,0:T(8,128)(2,1)} %get-tuple-element.41.refs_0_), channel_id=1, source_target_pairs={{0,2},{1,3},{2,0},{3,1},{4,6},{5,7},{6,4},{7,5},{8,10},{9,11},{10,... | collective-permute-start | bytes 393224 | tf_op jit(solution)/shard_map/ppermute | solution.py:372
  62.3 28.1 %collective-permute-start.17 = (bf16[4,32,512]{2,1,0:T(8,128)(2,1)}, bf16[4,32,512]{2,1,0:T(8,128)(2,1)S(1)}, u32[]{:S(2)}, u32[]{:S(2)}) collective-permute-start(bf16[4,32,512]{2,1,0:T(8,128)(2,1)} %get-tuple-element.41.refs_0_), channel_id=1, source_target_pairs={{0,1},{1,0},{2,3},{3,2},{4,5},{5,4},{6,7},{7,6},{8,9},{9,8},{10,11... | collective-permute-start | bytes 393224 | tf_op jit(solution)/shard_map/ppermute | solution.py:372
  69.8 20.6 %collective-permute-start.22 = (bf16[4,32,512]{2,1,0:T(8,128)(2,1)}, bf16[4,32,512]{2,1,0:T(8,128)(2,1)S(1)}, u32[]{:S(2)}, u32[]{:S(2)}) collective-permute-start(bf16[4,32,512]{2,1,0:T(8,128)(2,1)} %get-tuple-element.42.refs_4_), channel_id=1, source_target_pairs={{0,12},{1,13},{2,14},{3,15},{4,8},{5,9},{6,10},{7,11},{8,4},{9,5},... | collective-permute-start | bytes 393224 | tf_op jit(solution)/shard_map/ppermute | solution.py:372
  76.9 15.2 %collective-permute-start.21 = (bf16[4,32,512]{2,1,0:T(8,128)(2,1)}, bf16[4,32,512]{2,1,0:T(8,128)(2,1)S(1)}, u32[]{:S(2)}, u32[]{:S(2)}) collective-permute-start(bf16[4,32,512]{2,1,0:T(8,128)(2,1)} %get-tuple-element.42.refs_4_), channel_id=1, source_target_pairs={{0,8},{1,9},{2,10},{3,11},{4,12},{5,13},{6,14},{7,15},{8,0},{9,1},... | collective-permute-start | bytes 393224 | tf_op jit(solution)/shard_map/ppermute | solution.py:372
  94.4 31.5 %collective-permute-start.29 = (bf16[4,4,32,512]{3,2,1,0:T(8,128)(2,1)}, bf16[4,4,32,512]{3,2,1,0:T(8,128)(2,1)S(1)}, u32[]{:S(2)}, u32[]{:S(2)}) collective-permute-start(bf16[4,4,32,512]{3,2,1,0:T(8,128)(2,1)} %get-tuple-element.43.rest_8_), channel_id=1, source_target_pairs={{0,16},{16,0},{32,48},{48,32},{64,80},{80,64},{96,112},{112,96},{1... | collective-permute-start | bytes 1572872 | tf_op jit(solution)/shard_map/ppermute | solution.py:372
  96.8 31.5 %collective-permute-start.25 = (bf16[4,4,32,512]{3,2,1,0:T(8,128)(2,1)}, bf16[4,4,32,512]{3,2,1,0:T(8,128)(2,1)}, u32[]{:S(2)}, u32[]{:S(2)}) collective-permute-start(bf16[4,4,32,512]{3,2,1,0:T(8,128)(2,1)} %get-tuple-element.43.rest_8_), channel_id=1, source_target_pairs={{0,12},{1,13},{2,14},{3,15},{4,8},{5,9},{6,10},{7,11},{8,4},{9,5},... | collective-permute-start | bytes 1572872 | tf_op jit(solution)/shard_map/ppermute | solution.py:372
  97.7 31.2 %collective-permute-start.24 = (bf16[4,4,32,512]{3,2,1,0:T(8,128)(2,1)}, bf16[4,4,32,512]{3,2,1,0:T(8,128)(2,1)S(1)}, u32[]{:S(2)}, u32[]{:S(2)}) collective-permute-start(bf16[4,4,32,512]{3,2,1,0:T(8,128)(2,1)} %get-tuple-element.43.rest_8_), channel_id=1, source_target_pairs={{0,8},{1,9},{2,10},{3,11},{4,12},{5,13},{6,14},{7,15},{8,0},{9,1},... | collective-permute-start | bytes 1572872 | tf_op jit(solution)/shard_map/ppermute | solution.py:372
  99.8 29.4 %collective-permute-start.23 = (bf16[4,4,32,512]{3,2,1,0:T(8,128)(2,1)}, bf16[4,4,32,512]{3,2,1,0:T(8,128)(2,1)S(1)}, u32[]{:S(2)}, u32[]{:S(2)}) collective-permute-start(bf16[4,4,32,512]{3,2,1,0:T(8,128)(2,1)} %get-tuple-element.43.rest_8_), channel_id=1, source_target_pairs={{0,4},{1,5},{2,6},{3,7},{4,0},{5,1},{6,2},{7,3},{8,12},{9,13},{10,... | collective-permute-start | bytes 1572872 | tf_op jit(solution)/shard_map/ppermute | solution.py:372
  125.2 19.0 %collective-permute-start.33 = (bf16[4,4,32,512]{3,2,1,0:T(8,128)(2,1)}, bf16[4,4,32,512]{3,2,1,0:T(8,128)(2,1)}, u32[]{:S(2)}, u32[]{:S(2)}) collective-permute-start(bf16[4,4,32,512]{3,2,1,0:T(8,128)(2,1)} %get-tuple-element.44.rest_12_), channel_id=1, source_target_pairs={{0,16},{16,0},{32,48},{48,32},{64,80},{80,64},{96,112},{112,96},{1... | collective-permute-start | bytes 1572872 | tf_op jit(solution)/shard_map/ppermute | solution.py:372
  125.9 33.4 %collective-permute-start.28 = (bf16[4,4,32,512]{3,2,1,0:T(8,128)(2,1)}, bf16[4,4,32,512]{3,2,1,0:T(8,128)(2,1)}, u32[]{:S(2)}, u32[]{:S(2)}) collective-permute-start(bf16[4,4,32,512]{3,2,1,0:T(8,128)(2,1)} %get-tuple-element.44.rest_12_), channel_id=1, source_target_pairs={{0,3},{1,2},{2,1},{3,0},{4,7},{5,6},{6,5},{7,4},{8,11},{9,10},{10,... | collective-permute-start | bytes 1572872 | tf_op jit(solution)/shard_map/ppermute | solution.py:372
  128.3 32.9 %collective-permute-start.27 = (bf16[4,4,32,512]{3,2,1,0:T(8,128)(2,1)}, bf16[4,4,32,512]{3,2,1,0:T(8,128)(2,1)}, u32[]{:S(2)}, u32[]{:S(2)}) collective-permute-start(bf16[4,4,32,512]{3,2,1,0:T(8,128)(2,1)} %get-tuple-element.44.rest_12_), channel_id=1, source_target_pairs={{0,2},{1,3},{2,0},{3,1},{4,6},{5,7},{6,4},{7,5},{8,10},{9,11},{10,... | collective-permute-start | bytes 1572872 | tf_op jit(solution)/shard_map/ppermute | solution.py:372
  128.9 32.3 %collective-permute-start.26 = (bf16[4,4,32,512]{3,2,1,0:T(8,128)(2,1)}, bf16[4,4,32,512]{3,2,1,0:T(8,128)(2,1)}, u32[]{:S(2)}, u32[]{:S(2)}) collective-permute-start(bf16[4,4,32,512]{3,2,1,0:T(8,128)(2,1)} %get-tuple-element.44.rest_12_), channel_id=1, source_target_pairs={{0,1},{1,0},{2,3},{3,2},{4,5},{5,4},{6,7},{7,6},{8,9},{9,8},{10,11... | collective-permute-start | bytes 1572872 | tf_op jit(solution)/shard_map/ppermute | solution.py:372
  130.5 32.4 %collective-permute-start.32 = (bf16[4,4,32,512]{3,2,1,0:T(8,128)(2,1)}, bf16[4,4,32,512]{3,2,1,0:T(8,128)(2,1)}, u32[]{:S(2)}, u32[]{:S(2)}) collective-permute-start(bf16[4,4,32,512]{3,2,1,0:T(8,128)(2,1)} %collective-permute-done.25.rest_11_), channel_id=1, source_target_pairs={{0,16},{16,0},{32,48},{48,32},{64,80},{80,64},{96,112},{112,96},{1... | collective-permute-start | bytes 1572872 | tf_op jit(solution)/shard_map/ppermute | solution.py:372
  138.9 26.7 %all-to-all-start.1 = ((bf16[16,64,512]{2,1,0:T(8,128)(2,1)}), bf16[16,64,512]{2,1,0:T(8,128)(2,1)S(1)}, u32[]{:S(2)}, u32[]{:S(2)}) async-start(bf16[16,64,512]{2,1,0:T(8,128)(2,1)} %bitcast.5), calls=%async_computation.1 | async-start | bytes 2097152 | tf_op jit(solution)/shard_map/all_to_all | solution.py:458
  144.2 18.7 %collective-permute-start.31 = (bf16[4,4,32,512]{3,2,1,0:T(8,128)(2,1)}, bf16[4,4,32,512]{3,2,1,0:T(8,128)(2,1)S(1)}, u32[]{:S(2)}, u32[]{:S(2)}) collective-permute-start(bf16[4,4,32,512]{3,2,1,0:T(8,128)(2,1)} %copy-done.16), channel_id=1, source_target_pairs={{0,16},{16,0},{32,48},{48,32},{64,80},{80,64},{96,112},{112,96},{1... | collective-permute-start | bytes 1572872 | tf_op jit(solution)/shard_map/ppermute | solution.py:372
  (41 other events, 243.1 us)
